TPU v7x, 256 devices: a whole 4x4x8 slice. The times are simulated.
256 devices in a mesh: dp: 16 (over z_lo, x, core), tensor: 16 (over y, z_hi).
Axes of the slice: x: 4, y: 4, z: 8 (z_hi: 4, z_lo: 2; z = z_hi * 2 + z_lo), core: 2. Of those that a mesh axis runs over, the one named last changes fastest.
Arguments:
- tokens: bfloat16 [16384, 4096], P(('dp', 'tensor')), parts along dimension 0, may hold values from -6 to 6
- gate_rows: int32 [224, 9], P('tensor'), may hold values from -1 to 31, as said below
- gate_blocks: bfloat16 [224, 9, 128, 128], P('tensor'), may hold values from -0.21875 to 0.21875
- up_rows: int32 [224, 9], P('tensor'), may hold values from -1 to 31, as said below
- up_blocks: bfloat16 [224, 9, 128, 128], P('tensor'), may hold values from -0.21875 to 0.21875
Outputs:
- hidden: bfloat16 [16384, 28672], P('dp', 'tensor'), parts along dimension 0
There are 16 independent parts, one for each index of `dp`. A program takes and returns all parts, laid end to end along the dimension named above; an argument that names none is the same for every part. Nothing has to cross between parts.
Inputs may be any that keep to these rules, and one draw needn't show every extreme that they name: `gate_rows`: row c lists, for block column c of 128 hidden units, the row blocks of its nonzero blocks, all different, followed by -1 in the unused slots; every tensor member's 14 block columns include one with exactly 9 entries. `up_rows`: as for gate_rows, drawn apart.
All inputs are finite; a program needn't handle non-finite values.
Results may differ from a plain program's by a relative error of at most 0.001.
Values may be sent and summed in bfloat16 or wider, within the bound.
No kernel may reach another device: no remote copies, remote signals or barrier semaphores. Data moves between devices by JAX's collectives and lax.ppermute only.
A program may use at most 192 MiB of HBM per device.

v0:
```python
import jax
import jax.numpy as jnp
from jax import lax
from jax.sharding import PartitionSpec as P


def passed_along(x, axis, by):
    length = lax.axis_size(axis)
    return lax.ppermute(x, axis, [(i, (i + by) % length) for i in range(length)])


def block_product(segment, row_list, block_values):
    row_count = segment.shape[0]
    col_blocks = row_list.shape[0]
    capacity = row_list.shape[1]
    block_size = block_values.shape[-1]
    token_blocks = segment.reshape(row_count, -1, block_size)
    flat_index = jnp.maximum(row_list, 0).reshape(-1)
    picked = jnp.take(token_blocks, flat_index, axis=1).reshape(
        row_count, col_blocks, capacity, block_size
    )
    picked = jnp.where((row_list >= 0)[None, :, :, None], picked, jnp.zeros((), picked.dtype))
    summed = jnp.einsum("rcjk,cjkn->rcn", picked, block_values, preferred_element_type=jnp.float32)
    return summed.reshape(row_count, col_blocks * block_size)


def shards(tokens, gate_rows, gate_blocks, up_rows, up_blocks):
    members = lax.axis_size("tensor")
    my_index = lax.axis_index("tensor")
    local_rows = tokens.shape[0]
    width = gate_rows.shape[0] * gate_blocks.shape[-1]

    def project(segment):
        gate_part = block_product(segment, gate_rows, gate_blocks)
        up_part = block_product(segment, up_rows, up_blocks)
        return (jax.nn.silu(gate_part) * up_part).astype(jnp.bfloat16)

    def advance(turn_index, carry):
        held_rows, result = carry
        source = (my_index - turn_index) % members
        result = lax.dynamic_update_slice_in_dim(result, project(held_rows), source * local_rows, 0)
        held_rows = passed_along(held_rows, "tensor", 1)
        return (held_rows, result)

    initial = jnp.zeros((members * local_rows, width), jnp.bfloat16)
    held_rows, result = lax.fori_loop(0, members - 1, advance, (tokens, initial))
    source = (my_index - (members - 1)) % members
    return lax.dynamic_update_slice_in_dim(result, project(held_rows), source * local_rows, 0)


def solution(mesh):
    in_specs = (
        P(("dp", "tensor"), None),
        P("tensor", None),
        P("tensor", None, None, None),
        P("tensor", None),
        P("tensor", None, None, None),
    )
    out_specs = P("dp", "tensor")
    return jax.shard_map(shards, mesh=mesh, in_specs=in_specs, out_specs=out_specs, check_vma=False)
```

profile of v0, /device:TPU:4, one launch (start us, length us, event | category | flops | bytes accessed | tf_op | source)
XLA Modules:
  0.0 423.4 jit_solution(2307995116643369271)
XLA Ops:
  4.0 409.0 %while.17 = (s32[]{:T(128)}, bf16[64,4096]{1,0:T(8,128)(2,1)}, bf16[1024,1792]{1,0:T(8,128)(2,1)}, s32[14,9]{1,0:T(8,128)S(1)}, bf16[14,9,128,128]{3,2,1,0:T(8,1...) while((s32[]{:T(128)}, bf16[64,4096]{1,0:T(8,128)(2,1)}, ...), condition=%wide.region_1.3_spmd, body=%wide.region_0.2_spmd.sunk | while | flops 533304032 | bytes 68209896 | solution.py:46
  5.0 3.3 collective-permute-start
  8.7 2.2 gather_fusion
  19.8 10.4 %collective-permute-done = bf16[64,4096]{1,0:T(8,128)(2,1)} collective-permute-done((bf16[64,4096]{1,0:T(8,128)(2,1)S(1)}, bf16[64,4096]{1,0:T(8,128)(2,1)}, u32[]{:S(2)}, u32[]{:S(2)}) %collective-permute-start) | collective-permute-done | bytes 524320 | tf_op jit(solution)/shard_map/while/body/eval_jaxpr/ppermute | solution.py:9
  31.2 4.9 %collective-permute-start = (bf16[64,4096]{1,0:T(8,128)(2,1)S(1)}, bf16[64,4096]{1,0:T(8,128)(2,1)}, u32[]{:S(2)}, u32[]{:S(2)}) collective-permute-start(bf16[64,4096]{1,0:T(8,128)(2,1)S(1)} %copy.57), channel_id=1, source_target_pairs={{0,1},{1,2},{2,3},{3,4},{4,5},{5,6},{6,7},{7,8},{8,9},{9,10},{10,1... | collective-permute-start | bytes 1572872 | tf_op jit(solution)/shard_map/while/body/eval_jaxpr/ppermute | solution.py:9
  47.6 10.7 %collective-permute-done = bf16[64,4096]{1,0:T(8,128)(2,1)} collective-permute-done((bf16[64,4096]{1,0:T(8,128)(2,1)S(1)}, bf16[64,4096]{1,0:T(8,128)(2,1)}, u32[]{:S(2)}, u32[]{:S(2)}) %collective-permute-start) | collective-permute-done | bytes 524320 | tf_op jit(solution)/shard_map/while/body/eval_jaxpr/ppermute | solution.py:9
  59.4 4.7 %collective-permute-start = (bf16[64,4096]{1,0:T(8,128)(2,1)S(1)}, bf16[64,4096]{1,0:T(8,128)(2,1)}, u32[]{:S(2)}, u32[]{:S(2)}) collective-permute-start(bf16[64,4096]{1,0:T(8,128)(2,1)S(1)} %copy.57), channel_id=1, source_target_pairs={{0,1},{1,2},{2,3},{3,4},{4,5},{5,6},{6,7},{7,8},{8,9},{9,10},{10,1... | collective-permute-start | bytes 1572872 | tf_op jit(solution)/shard_map/while/body/eval_jaxpr/ppermute | solution.py:9
  75.5 14.0 %collective-permute-done = bf16[64,4096]{1,0:T(8,128)(2,1)} collective-permute-done((bf16[64,4096]{1,0:T(8,128)(2,1)S(1)}, bf16[64,4096]{1,0:T(8,128)(2,1)}, u32[]{:S(2)}, u32[]{:S(2)}) %collective-permute-start) | collective-permute-done | bytes 524320 | tf_op jit(solution)/shard_map/while/body/eval_jaxpr/ppermute | solution.py:9
  102.1 11.4 %collective-permute-done = bf16[64,4096]{1,0:T(8,128)(2,1)} collective-permute-done((bf16[64,4096]{1,0:T(8,128)(2,1)S(1)}, bf16[64,4096]{1,0:T(8,128)(2,1)}, u32[]{:S(2)}, u32[]{:S(2)}) %collective-permute-start) | collective-permute-done | bytes 524320 | tf_op jit(solution)/shard_map/while/body/eval_jaxpr/ppermute | solution.py:9
  114.6 4.4 %collective-permute-start = (bf16[64,4096]{1,0:T(8,128)(2,1)S(1)}, bf16[64,4096]{1,0:T(8,128)(2,1)}, u32[]{:S(2)}, u32[]{:S(2)}) collective-permute-start(bf16[64,4096]{1,0:T(8,128)(2,1)S(1)} %copy.57), channel_id=1, source_target_pairs={{0,1},{1,2},{2,3},{3,4},{4,5},{5,6},{6,7},{7,8},{8,9},{9,10},{10,1... | collective-permute-start | bytes 1572872 | tf_op jit(solution)/shard_map/while/body/eval_jaxpr/ppermute | solution.py:9
  130.6 17.0 %collective-permute-done = bf16[64,4096]{1,0:T(8,128)(2,1)} collective-permute-done((bf16[64,4096]{1,0:T(8,128)(2,1)S(1)}, bf16[64,4096]{1,0:T(8,128)(2,1)}, u32[]{:S(2)}, u32[]{:S(2)}) %collective-permute-start) | collective-permute-done | bytes 524320 | tf_op jit(solution)/shard_map/while/body/eval_jaxpr/ppermute | solution.py:9
  149.1 2.2 gather_fusion
  160.2 7.6 %collective-permute-done = bf16[64,4096]{1,0:T(8,128)(2,1)} collective-permute-done((bf16[64,4096]{1,0:T(8,128)(2,1)S(1)}, bf16[64,4096]{1,0:T(8,128)(2,1)}, u32[]{:S(2)}, u32[]{:S(2)}) %collective-permute-start) | collective-permute-done | bytes 524320 | tf_op jit(solution)/shard_map/while/body/eval_jaxpr/ppermute | solution.py:9
  180.3 20.9 %collective-permute-done = bf16[64,4096]{1,0:T(8,128)(2,1)} collective-permute-done((bf16[64,4096]{1,0:T(8,128)(2,1)S(1)}, bf16[64,4096]{1,0:T(8,128)(2,1)}, u32[]{:S(2)}, u32[]{:S(2)}) %collective-permute-start) | collective-permute-done | bytes 524320 | tf_op jit(solution)/shard_map/while/body/eval_jaxpr/ppermute | solution.py:9
  213.8 16.4 %collective-permute-done = bf16[64,4096]{1,0:T(8,128)(2,1)} collective-permute-done((bf16[64,4096]{1,0:T(8,128)(2,1)S(1)}, bf16[64,4096]{1,0:T(8,128)(2,1)}, u32[]{:S(2)}, u32[]{:S(2)}) %collective-permute-start) | collective-permute-done | bytes 524320 | tf_op jit(solution)/shard_map/while/body/eval_jaxpr/ppermute | solution.py:9
  242.8 15.5 %collective-permute-done = bf16[64,4096]{1,0:T(8,128)(2,1)} collective-permute-done((bf16[64,4096]{1,0:T(8,128)(2,1)S(1)}, bf16[64,4096]{1,0:T(8,128)(2,1)}, u32[]{:S(2)}, u32[]{:S(2)}) %collective-permute-start) | collective-permute-done | bytes 524320 | tf_op jit(solution)/shard_map/while/body/eval_jaxpr/ppermute | solution.py:9
  270.8 19.5 %collective-permute-done = bf16[64,4096]{1,0:T(8,128)(2,1)} collective-permute-done((bf16[64,4096]{1,0:T(8,128)(2,1)S(1)}, bf16[64,4096]{1,0:T(8,128)(2,1)}, u32[]{:S(2)}, u32[]{:S(2)}) %collective-permute-start) | collective-permute-done | bytes 524320 | tf_op jit(solution)/shard_map/while/body/eval_jaxpr/ppermute | solution.py:9
  302.9 16.5 %collective-permute-done = bf16[64,4096]{1,0:T(8,128)(2,1)} collective-permute-done((bf16[64,4096]{1,0:T(8,128)(2,1)S(1)}, bf16[64,4096]{1,0:T(8,128)(2,1)}, u32[]{:S(2)}, u32[]{:S(2)}) %collective-permute-start) | collective-permute-done | bytes 524320 | tf_op jit(solution)/shard_map/while/body/eval_jaxpr/ppermute | solution.py:9
  320.4 3.5 collective-permute-start
  335.4 9.2 %collective-permute-done = bf16[64,4096]{1,0:T(8,128)(2,1)} collective-permute-done((bf16[64,4096]{1,0:T(8,128)(2,1)S(1)}, bf16[64,4096]{1,0:T(8,128)(2,1)}, u32[]{:S(2)}, u32[]{:S(2)}) %collective-permute-start) | collective-permute-done | bytes 524320 | tf_op jit(solution)/shard_map/while/body/eval_jaxpr/ppermute | solution.py:9
  345.7 2.6 collective-permute-start
  359.8 9.8 %collective-permute-done = bf16[64,4096]{1,0:T(8,128)(2,1)} collective-permute-done((bf16[64,4096]{1,0:T(8,128)(2,1)S(1)}, bf16[64,4096]{1,0:T(8,128)(2,1)}, u32[]{:S(2)}, u32[]{:S(2)}) %collective-permute-start) | collective-permute-done | bytes 524320 | tf_op jit(solution)/shard_map/while/body/eval_jaxpr/ppermute | solution.py:9
  370.7 3.5 collective-permute-start
  385.7 12.7 %collective-permute-done = bf16[64,4096]{1,0:T(8,128)(2,1)} collective-permute-done((bf16[64,4096]{1,0:T(8,128)(2,1)S(1)}, bf16[64,4096]{1,0:T(8,128)(2,1)}, u32[]{:S(2)}, u32[]{:S(2)}) %collective-permute-start) | collective-permute-done | bytes 524320 | tf_op jit(solution)/shard_map/while/body/eval_jaxpr/ppermute | solution.py:9
  (382 shorter events, 198.1 us)
Async XLA Ops:
  5.0 25.1 %collective-permute-start = (bf16[64,4096]{1,0:T(8,128)(2,1)S(1)}, bf16[64,4096]{1,0:T(8,128)(2,1)}, u32[]{:S(2)}, u32[]{:S(2)}) collective-permute-start(bf16[64,4096]{1,0:T(8,128)(2,1)S(1)} %copy.57), channel_id=1, source_target_pairs={{0,1},{1,2},{2,3},{3,4},{4,5},{5,6},{6,7},{7,8},{8,9},{9,10},{10,1... | collective-permute-start | bytes 1572872 | tf_op jit(solution)/shard_map/while/body/eval_jaxpr/ppermute | solution.py:9
  13.6 2.2 copy-start.2
  31.2 27.1 %collective-permute-start = (bf16[64,4096]{1,0:T(8,128)(2,1)S(1)}, bf16[64,4096]{1,0:T(8,128)(2,1)}, u32[]{:S(2)}, u32[]{:S(2)}) collective-permute-start(bf16[64,4096]{1,0:T(8,128)(2,1)S(1)} %copy.57), channel_id=1, source_target_pairs={{0,1},{1,2},{2,3},{3,4},{4,5},{5,6},{6,7},{7,8},{8,9},{9,10},{10,1... | collective-permute-start | bytes 1572872 | tf_op jit(solution)/shard_map/while/body/eval_jaxpr/ppermute | solution.py:9
  41.5 2.2 copy-start.2
  59.4 30.2 %collective-permute-start = (bf16[64,4096]{1,0:T(8,128)(2,1)S(1)}, bf16[64,4096]{1,0:T(8,128)(2,1)}, u32[]{:S(2)}, u32[]{:S(2)}) collective-permute-start(bf16[64,4096]{1,0:T(8,128)(2,1)S(1)} %copy.57), channel_id=1, source_target_pairs={{0,1},{1,2},{2,3},{3,4},{4,5},{5,6},{6,7},{7,8},{8,9},{9,10},{10,1... | collective-permute-start | bytes 1572872 | tf_op jit(solution)/shard_map/while/body/eval_jaxpr/ppermute | solution.py:9
  69.4 2.2 copy-start.2
  90.6 23.0 %collective-permute-start = (bf16[64,4096]{1,0:T(8,128)(2,1)S(1)}, bf16[64,4096]{1,0:T(8,128)(2,1)}, u32[]{:S(2)}, u32[]{:S(2)}) collective-permute-start(bf16[64,4096]{1,0:T(8,128)(2,1)S(1)} %copy.57), channel_id=1, source_target_pairs={{0,1},{1,2},{2,3},{3,4},{4,5},{5,6},{6,7},{7,8},{8,9},{9,10},{10,1... | collective-permute-start | bytes 1572872 | tf_op jit(solution)/shard_map/while/body/eval_jaxpr/ppermute | solution.py:9
  96.0 2.2 copy-start.2
  114.6 33.0 %collective-permute-start = (bf16[64,4096]{1,0:T(8,128)(2,1)S(1)}, bf16[64,4096]{1,0:T(8,128)(2,1)}, u32[]{:S(2)}, u32[]{:S(2)}) collective-permute-start(bf16[64,4096]{1,0:T(8,128)(2,1)S(1)} %copy.57), channel_id=1, source_target_pairs={{0,1},{1,2},{2,3},{3,4},{4,5},{5,6},{6,7},{7,8},{8,9},{9,10},{10,1... | collective-permute-start | bytes 1572872 | tf_op jit(solution)/shard_map/while/body/eval_jaxpr/ppermute | solution.py:9
  124.4 2.2 copy-start.2
  148.6 19.1 %collective-permute-start = (bf16[64,4096]{1,0:T(8,128)(2,1)S(1)}, bf16[64,4096]{1,0:T(8,128)(2,1)}, u32[]{:S(2)}, u32[]{:S(2)}) collective-permute-start(bf16[64,4096]{1,0:T(8,128)(2,1)S(1)} %copy.57), channel_id=1, source_target_pairs={{0,1},{1,2},{2,3},{3,4},{4,5},{5,6},{6,7},{7,8},{8,9},{9,10},{10,1... | collective-permute-start | bytes 1572872 | tf_op jit(solution)/shard_map/while/body/eval_jaxpr/ppermute | solution.py:9
  168.8 32.5 %collective-permute-start = (bf16[64,4096]{1,0:T(8,128)(2,1)S(1)}, bf16[64,4096]{1,0:T(8,128)(2,1)}, u32[]{:S(2)}, u32[]{:S(2)}) collective-permute-start(bf16[64,4096]{1,0:T(8,128)(2,1)S(1)} %copy.57), channel_id=1, source_target_pairs={{0,1},{1,2},{2,3},{3,4},{4,5},{5,6},{6,7},{7,8},{8,9},{9,10},{10,1... | collective-permute-start | bytes 1572872 | tf_op jit(solution)/shard_map/while/body/eval_jaxpr/ppermute | solution.py:9
  174.2 2.2 copy-start.2
  202.3 27.9 %collective-permute-start = (bf16[64,4096]{1,0:T(8,128)(2,1)S(1)}, bf16[64,4096]{1,0:T(8,128)(2,1)}, u32[]{:S(2)}, u32[]{:S(2)}) collective-permute-start(bf16[64,4096]{1,0:T(8,128)(2,1)S(1)} %copy.57), channel_id=1, source_target_pairs={{0,1},{1,2},{2,3},{3,4},{4,5},{5,6},{6,7},{7,8},{8,9},{9,10},{10,1... | collective-permute-start | bytes 1572872 | tf_op jit(solution)/shard_map/while/body/eval_jaxpr/ppermute | solution.py:9
  231.3 27.0 %collective-permute-start = (bf16[64,4096]{1,0:T(8,128)(2,1)S(1)}, bf16[64,4096]{1,0:T(8,128)(2,1)}, u32[]{:S(2)}, u32[]{:S(2)}) collective-permute-start(bf16[64,4096]{1,0:T(8,128)(2,1)S(1)} %copy.57), channel_id=1, source_target_pairs={{0,1},{1,2},{2,3},{3,4},{4,5},{5,6},{6,7},{7,8},{8,9},{9,10},{10,1... | collective-permute-start | bytes 1572872 | tf_op jit(solution)/shard_map/while/body/eval_jaxpr/ppermute | solution.py:9
  259.3 31.0 %collective-permute-start = (bf16[64,4096]{1,0:T(8,128)(2,1)S(1)}, bf16[64,4096]{1,0:T(8,128)(2,1)}, u32[]{:S(2)}, u32[]{:S(2)}) collective-permute-start(bf16[64,4096]{1,0:T(8,128)(2,1)S(1)} %copy.57), channel_id=1, source_target_pairs={{0,1},{1,2},{2,3},{3,4},{4,5},{5,6},{6,7},{7,8},{8,9},{9,10},{10,1... | collective-permute-start | bytes 1572872 | tf_op jit(solution)/shard_map/while/body/eval_jaxpr/ppermute | solution.py:9
  291.4 28.0 %collective-permute-start = (bf16[64,4096]{1,0:T(8,128)(2,1)S(1)}, bf16[64,4096]{1,0:T(8,128)(2,1)}, u32[]{:S(2)}, u32[]{:S(2)}) collective-permute-start(bf16[64,4096]{1,0:T(8,128)(2,1)S(1)} %copy.57), channel_id=1, source_target_pairs={{0,1},{1,2},{2,3},{3,4},{4,5},{5,6},{6,7},{7,8},{8,9},{9,10},{10,1... | collective-permute-start | bytes 1572872 | tf_op jit(solution)/shard_map/while/body/eval_jaxpr/ppermute | solution.py:9
  296.8 2.2 copy-start.2
  320.4 24.2 %collective-permute-start = (bf16[64,4096]{1,0:T(8,128)(2,1)S(1)}, bf16[64,4096]{1,0:T(8,128)(2,1)}, u32[]{:S(2)}, u32[]{:S(2)}) collective-permute-start(bf16[64,4096]{1,0:T(8,128)(2,1)S(1)} %copy.57), channel_id=1, source_target_pairs={{0,1},{1,2},{2,3},{3,4},{4,5},{5,6},{6,7},{7,8},{8,9},{9,10},{10,1... | collective-permute-start | bytes 1572872 | tf_op jit(solution)/shard_map/while/body/eval_jaxpr/ppermute | solution.py:9
  329.3 2.2 copy-start.2
  345.7 24.0 %collective-permute-start = (bf16[64,4096]{1,0:T(8,128)(2,1)S(1)}, bf16[64,4096]{1,0:T(8,128)(2,1)}, u32[]{:S(2)}, u32[]{:S(2)}) collective-permute-start(bf16[64,4096]{1,0:T(8,128)(2,1)S(1)} %copy.57), channel_id=1, source_target_pairs={{0,1},{1,2},{2,3},{3,4},{4,5},{5,6},{6,7},{7,8},{8,9},{9,10},{10,1... | collective-permute-start | bytes 1572872 | tf_op jit(solution)/shard_map/while/body/eval_jaxpr/ppermute | solution.py:9
  370.7 27.7 %collective-permute-start = (bf16[64,4096]{1,0:T(8,128)(2,1)S(1)}, bf16[64,4096]{1,0:T(8,128)(2,1)}, u32[]{:S(2)}, u32[]{:S(2)}) collective-permute-start(bf16[64,4096]{1,0:T(8,128)(2,1)S(1)} %copy.57), channel_id=1, source_target_pairs={{0,1},{1,2},{2,3},{3,4},{4,5},{5,6},{6,7},{7,8},{8,9},{9,10},{10,1... | collective-permute-start | bytes 1572872 | tf_op jit(solution)/shard_map/while/body/eval_jaxpr/ppermute | solution.py:9
  399.5 13.5 %collective-permute-start = (bf16[64,4096]{1,0:T(8,128)(2,1)S(1)}, bf16[64,4096]{1,0:T(8,128)(2,1)}, u32[]{:S(2)}, u32[]{:S(2)}) collective-permute-start(bf16[64,4096]{1,0:T(8,128)(2,1)S(1)} %copy.57), channel_id=1, source_target_pairs={{0,1},{1,2},{2,3},{3,4},{4,5},{5,6},{6,7},{7,8},{8,9},{9,10},{10,1... | collective-permute-start | bytes 1572872 | tf_op jit(solution)/shard_map/while/body/eval_jaxpr/ppermute | solution.py:9
  406.7 2.2 copy-start.2
  (25 other events, 54.1 us)
where the time goes:
time: 429 us; the launch traced here: 423 us
  waiting for transfers between devices  192 us (45%)
  local copies, waits for them, and re-layouts  124 us (29%)
  other arithmetic  46.1 us (11%)
  matrix products  30.1 us (7%)
  starting transfers between devices  28.9 us (7%)
    ppermute x15, waiting for transfers between devices, passed_along(): lax.ppermute(x, axis, [(i, (i + by) % length) for i in range(length)])  192 us
    gather x32, local copies, waits for them, and re-layouts, block_product(): jnp.take(token_blocks, flat_index, axis=1)  48.3 us
    while x60, local copies, waits for them, and re-layouts  46.6 us
    select_n x64, other arithmetic, block_product(): jnp.take(token_blocks, flat_index, axis=1)  32.3 us
    dot_general x32, matrix products, block_product(): jnp.einsum('rcjk,cjkn->rcn', picked, block_values, preferred_element_type...  30.1 us
    ppermute x15, starting transfers between devices, passed_along(): lax.ppermute(x, axis, [(i, (i + by) % length) for i in range(length)])  28.9 us
    another operation x15, local copies, waits for them, and re-layouts  15.6 us
    dynamic_update_slice x15, other arithmetic, advance(): lax.dynamic_update_slice_in_dim(result, project(held_rows), source * loca...  12.4 us
  transfers between devices with their start and end apart: 15, of which 15 were waited for; matrix products, arithmetic and copies ran while one was open for 29% of the time, Pallas kernels for 0%

commit v1 on v0

v1 whole, which is shorter than its diff:
```python
import functools

import jax
import jax.numpy as jnp
import numpy as np
from jax import lax
from jax.experimental import pallas as pl
from jax.experimental.pallas import tpu as pltpu
from jax.sharding import PartitionSpec as P

BLK = 128
SIDE = 4
AXES = ("dp", "tensor")
TURNED = 16
UNROLL = 7
COST = 22_000_000


def moved(member, core, dim, step):
    y, z = member // SIDE, member % SIDE
    v = y if dim == "y" else z
    v = v ^ 1 if (step + core) % 2 == 0 else SIDE - 1 - v
    return v * SIDE + z if dim == "y" else y * SIDE + v


class Piece:
    def __init__(self, rows, sources, size, offset):
        self.rows, self.sources, self.size, self.offset = rows, sources, size, offset

    def part(self, offset, size):
        count = self.rows.shape[0] // self.size
        rows = self.rows.reshape(count, self.size, -1)[:, offset : offset + size]
        return Piece(rows.reshape(count * size, -1), self.sources, size, self.offset + offset)


def joined(*pieces):
    rows = jnp.concatenate([p.rows for p in pieces], axis=0)
    return Piece(rows, lambda m, core: [s for p in pieces for s in p.sources(m, core)], pieces[0].size, pieces[0].offset)


def project_kernel(layout, first_block, n_prev, dst_ref, gate_rows_ref, up_rows_ref, *refs):
    n = len(layout)
    pieces, (gate_ref, up_ref) = refs[:n], refs[n : n + 2]
    out_ref, hidden, sems = refs[n + 2 + n_prev :]
    columns, cap = gate_rows_ref.shape

    def product(rows_ref, blocks_ref, c):
        def gathered(j):
            start = pl.multiple_of(jnp.maximum(rows_ref[c, j], 0) * BLK, BLK)
            return jnp.concatenate([p[:, pl.ds(start, BLK)] for p in pieces], axis=0)

        lhs = jnp.concatenate([gathered(j) for j in range(cap)], axis=1)
        rhs = jnp.concatenate(
            [jnp.where(rows_ref[c, j] >= 0, blocks_ref[c, j], jnp.zeros((), blocks_ref.dtype)) for j in range(cap)], axis=0
        )
        return jnp.dot(lhs, rhs, preferred_element_type=jnp.float32)

    @pl.loop(0, columns, step=UNROLL)
    def _(first):
        for k in range(UNROLL):
            c = first + k
            gate = product(gate_rows_ref, gate_ref, c)
            up = product(up_rows_ref, up_ref, c)
            value = gate * (1.0 / (1.0 + jnp.exp(-gate))) * up
            hidden[:, pl.ds(pl.multiple_of(c * BLK, BLK), BLK)] = value.astype(hidden.dtype)

    copies, base = [], 0
    for size, count in layout:
        for _ in range(count):
            i = len(copies)
            to = pl.multiple_of(dst_ref[first_block + i], 16)
            copies.append(pltpu.make_async_copy(hidden.at[pl.ds(base, size)], out_ref.at[pl.ds(to, size)], sems.at[i]))
            base += size
    for copy in copies:
        copy.start()
    for copy in copies:
        copy.wait()


def project(pieces, total_rows, dst, first_block, tables, blocks, result):
    rows = sum(p.rows.shape[0] for p in pieces)
    layout = [(p.size, p.rows.shape[0] // p.size) for p in pieces]
    width = blocks[0].shape[0] * BLK
    prev = [] if result is None else [result]
    vmem, smem, hbm = (pl.BlockSpec(memory_space=m) for m in (pltpu.VMEM, pltpu.SMEM, pl.ANY))
    cap = tables[0].shape[1]
    return pl.pallas_call(
        functools.partial(project_kernel, layout, first_block, len(prev)),
        out_shape=jax.ShapeDtypeStruct((total_rows, width), jnp.bfloat16),
        in_specs=[smem] * 3 + [vmem] * (len(pieces) + 2) + [hbm] * len(prev),
        out_specs=hbm,
        scratch_shapes=[
            pltpu.VMEM((rows, width), jnp.bfloat16),
            pltpu.SemaphoreType.DMA((sum(count for _, count in layout),)),
        ],
        input_output_aliases={5 + len(pieces): 0} if prev else {},
        cost_estimate=pl.CostEstimate(
            flops=COST * (rows + 110), bytes_accessed=2 * rows * width, transcendentals=rows * width
        ),
        compiler_params=pltpu.CompilerParams(vmem_limit_bytes=8 << 20),
    )(dst, *tables, *[p.rows for p in pieces], *blocks, *prev)


def solution(mesh):
    groups, members = mesh.shape["dp"], mesh.shape["tensor"]

    def swap(piece, dim, step):
        pairs = [
            (g * members + m, g * members + moved(m, g % 2, dim, step)) for g in range(groups) for m in range(members)
        ]
        rows = lax.ppermute(piece.rows, AXES, pairs)
        return Piece(
            rows, lambda m, core: piece.sources(moved(m, core, dim, step), core), piece.size, piece.offset
        )

    def shards(tokens, gate_rows, gate_blocks, up_rows, up_blocks):
        local = tokens.shape[0]
        blocks = (gate_blocks, up_blocks)
        tables = (gate_rows, up_rows)

        own = Piece(tokens, lambda m, core: [m], local, 0)
        mine = own.part(TURNED, local - TURNED)
        z1 = swap(mine, "z", 0)
        y1 = swap(own, "y", 0)
        z2 = swap(joined(mine, z1), "z", 1)
        y2 = swap(joined(own, y1), "y", 1)
        p1 = swap(z1, "y", 0)
        p2 = swap(joined(z1, p1), "y", 1)
        column = joined(own.part(0, TURNED), y1.part(0, TURNED), y2.part(0, TURNED))
        b1 = swap(column, "z", 0)
        q1 = swap(z2, "y", 0)
        b2 = swap(joined(column, b1), "z", 1)
        q2 = swap(joined(z2, q1), "y", 1)
        calls = ([own], [z1, y1], [y2, p1], [z2, p2], [q1, b1], [b2], [q2])
        places = np.array(
            [
                [
                    [s * local + p.offset for pieces in calls for p in pieces for s in p.sources(m, core)]
                    for m in range(members)
                ]
                for core in range(2)
            ],
            np.int32,
        )
        dst = jnp.asarray(places)[lax.axis_index("dp") % 2, lax.axis_index("tensor")]
        out, first = None, 0
        for pieces in calls:
            out = project(pieces, members * local, dst, first, tables, blocks, out)
            first += sum(p.rows.shape[0] // p.size for p in pieces)
        return out

    in_specs = (
        P(AXES, None),
        P("tensor", None),
        P("tensor", None, None, None),
        P("tensor", None),
        P("tensor", None, None, None),
    )
    return jax.shard_map(shards, mesh=mesh, in_specs=in_specs, out_specs=P("dp", "tensor"), check_vma=False)
```

time: 429 us -> 110 us (0.26); the launches traced: 423 us -> 109 us
  waiting for transfers between devices: 192 us -> 37.6 us
  local copies, waits for them, and re-layouts: 124 us -> 9.49 us
  other arithmetic: 46.1 us -> 0.43 us
  Pallas kernels: 0 us -> 36.4 us
  matrix products: 30.1 us -> 0 us
    ppermute x15 -> x10, waiting for transfers between devices: 192 us -> 37.6 us  [swap(): rows = lax.ppermute(piece.rows, AXES, pairs)]
    gather x32 -> x0, local copies, waits for them, and re-layouts: 48.3 us -> none  [block_product(): jnp.take(token_blocks, flat_index, axis=1)]
    while x60 -> x0, local copies, waits for them, and re-layouts: 46.6 us -> none
    pallas_call x0 -> x7, Pallas kernels: none -> 36.4 us  [project(): pl.pallas_call(functools.partial(project_kernel, layout, first_block, len...]
    select_n x64 -> x0, other arithmetic: 32.3 us -> none  [block_product(): jnp.take(token_blocks, flat_index, axis=1)]
    dot_general x32 -> x0, matrix products: 30.1 us -> none  [block_product(): jnp.einsum('rcjk,cjkn->rcn', picked, block_values, preferred_element_type...]
    another operation x15 -> x0, local copies, waits for them, and re-layouts: 15.6 us -> none
    dynamic_update_slice x16 -> x0, other arithmetic: 13.2 us -> none  [the longest x15 12.4 us: advance(): lax.dynamic_update_slice_in_dim(result, project(held_rows), source * loca...]
  transfers between devices with their start and end apart: 15 -> 10, of which waited for: 15 -> 4; matrix products, arithmetic and copies ran while one was open for 29% -> 3% of each run, Pallas kernels for 0% -> 28%
where the time goes in v1:
time: 110 us; the launch traced here: 109 us
  waiting for transfers between devices  37.6 us (34%)
  Pallas kernels  36.4 us (33%)
  starting transfers between devices  25 us (23%)
  local copies, waits for them, and re-layouts  9.49 us (9%)
    ppermute x10, waiting for transfers between devices, swap(): rows = lax.ppermute(piece.rows, AXES, pairs)  37.6 us
    pallas_call x7, Pallas kernels, project(): pl.pallas_call(functools.partial(project_kernel, layout, first_block, len...  36.4 us
    ppermute x10, starting transfers between devices, swap(): rows = lax.ppermute(piece.rows, AXES, pairs)  25 us
    unnamed x20, local copies, waits for them, and re-layouts  6.8 us
  transfers between devices with their start and end apart: 10, of which 4 were waited for; matrix products, arithmetic and copies ran while one was open for 3% of the time, Pallas kernels for 28%

profile of v1, /device:TPU:4, one launch (start us, length us, event | category | flops | bytes accessed | tf_op | source)
XLA Modules:
  0.0 109.3 jit_solution(11726194173995016206)
XLA Ops:
  0.0 1.6 %collective-permute-start.4 = (bf16[64,4096]{1,0:T(8,128)(2,1)}, bf16[64,4096]{1,0:T(8,128)(2,1)S(1)}, u32[]{:S(2)}, u32[]{:S(2)}) collective-permute-start(bf16[64,4096]{1,0:T(8,128)(2,1)} %refs_0_.1), channel_id=1, source_target_pairs={{0,4},{1,5},{2,6},{3,7},{4,0},{5,1},{6,2},{7,3},{8,12},{9,13},{10,... | collective-permute-start | bytes 1572872 | tf_op jit(solution)/shard_map/ppermute | solution.py:111
  1.6 1.1 slice_bitcast_fusion
  2.6 3.4 %collective-permute-start = (bf16[48,4096]{1,0:T(8,128)(2,1)S(1)}, bf16[48,4096]{1,0:T(8,128)(2,1)S(1)}, u32[]{:S(2)}, u32[]{:S(2)}) collective-permute-start(bf16[48,4096]{1,0:T(8,128)(2,1)S(1)} %slice_bitcast_fusion), channel_id=1, source_target_pairs={{0,1},{1,0},{2,3},{3,2},{4,5},{5,4},{6,7},{7,6},{8,9},{9,8},{10,11... | collective-permute-start | bytes 1179656 | tf_op jit(solution)/shard_map/ppermute | solution.py:111
  6.0 0.9 slice_bitcast_fusion.2
  6.9 0.7 dynamic-slice_bitcast_fusion.dst_ref
  7.6 1.0 copy-done
  8.7 2.2 %copy-done.2 = bf16[14,9,128,128]{3,2,1,0:T(8,128)(2,1)S(1)} copy-done((bf16[14,9,128,128]{3,2,1,0:T(8,128)(2,1)S(1)}, bf16[14,9,128,128]{3,2,1,0:T(8,128)(2,1)}, u32[]{:S(2)}) %copy-start.2) | copy-done | bytes 4128792
  10.8 2.2 %copy-done.4 = bf16[14,9,128,128]{3,2,1,0:T(8,128)(2,1)S(1)} copy-done((bf16[14,9,128,128]{3,2,1,0:T(8,128)(2,1)S(1)}, bf16[14,9,128,128]{3,2,1,0:T(8,128)(2,1)}, u32[]{:S(2)}) %copy-start.4) | copy-done | bytes 4128792
  14.4 3.7 %shard_map.64.refs_4_ = bf16[1024,1792]{1,0:T(8,128)(2,1)} custom-call(s32[28]{0:T(128)S(1)} %dynamic-slice_bitcast_fusion.dst_ref, s32[14,9]{1,0:T(8,128)S(1)} %copy-done.6, s32[14,9]{1,0:T(8,128)S(1)} %copy-done.8, bf16[64,4096]{1,0:T(8,128)(2,1)S(1)} %copy-done, bf16[14,9,128,128]{3,2,1,0:T(8,128)(2,1)S(1)} %copy-done.2, ...), custom_call_target="tpu_custom_call" | custom-call | flops 3828000000 | bytes 229376 | tf_op jit(solution)/shard_map/pallas_call | solution.py:87
  18.8 3.1 %collective-permute-start.5 = (bf16[128,4096]{1,0:T(8,128)(2,1)S(1)}, bf16[128,4096]{1,0:T(8,128)(2,1)S(1)}, u32[]{:S(2)}, u32[]{:S(2)}) collective-permute-start(bf16[128,4096]{1,0:T(8,128)(2,1)S(1)} %pad_maximum_fusion.1), channel_id=1, source_target_pairs={{0,12},{1,13},{2,14},{3,15},{4,8},{5,9},{6,10},{7,11},{8,4},{9,5},... | collective-permute-start | bytes 3145736 | tf_op jit(solution)/shard_map/ppermute | solution.py:111
  21.9 5.3 %collective-permute-done.8.refs_1_ = bf16[48,4096]{1,0:T(8,128)(2,1)S(1)} collective-permute-done((bf16[48,4096]{1,0:T(8,128)(2,1)S(1)}, bf16[48,4096]{1,0:T(8,128)(2,1)S(1)}, u32[]{:S(2)}, u32[]{:S(2)}) %collective-permute-start.8) | collective-permute-done | bytes 393248 | tf_op jit(solution)/shard_map/ppermute | solution.py:111
  27.3 7.5 %collective-permute-start.1 = (bf16[96,4096]{1,0:T(8,128)(2,1)S(1)}, bf16[96,4096]{1,0:T(8,128)(2,1)S(1)}, u32[]{:S(2)}, u32[]{:S(2)}) collective-permute-start(bf16[96,4096]{1,0:T(8,128)(2,1)S(1)} %get-tuple-element.6), channel_id=1, source_target_pairs={{0,3},{1,2},{2,1},{3,0},{4,7},{5,6},{6,5},{7,4},{8,11},{9,10},{10,... | collective-permute-start | bytes 2359304 | tf_op jit(solution)/shard_map/ppermute | solution.py:111
  34.9 4.4 %shard_map.65.refs_4_ = bf16[1024,1792]{1,0:T(8,128)(2,1)} custom-call(s32[28]{0:T(128)S(1)} %dynamic-slice_bitcast_fusion.dst_ref, s32[14,9]{1,0:T(8,128)S(1)} %copy-done.7, s32[14,9]{1,0:T(8,128)S(1)} %copy-done.9, bf16[48,4096]{1,0:T(8,128)(2,1)S(1)} %collective-permute-done.refs_0_, ...), custom_call_target="tpu_custom_call", output_to_operand_aliasing={{}: (7, {})} | custom-call | flops 4883999744 | bytes 401408 | tf_op jit(solution)/shard_map/pallas_call | solution.py:87
  39.3 2.1 %collective-permute-start.9 = (bf16[96,4096]{1,0:T(8,128)(2,1)S(1)}, bf16[96,4096]{1,0:T(8,128)(2,1)S(1)}, u32[]{:S(2)}, u32[]{:S(2)}) collective-permute-start(bf16[96,4096]{1,0:T(8,128)(2,1)S(1)} %get-tuple-element.5), channel_id=1, source_target_pairs={{0,12},{1,13},{2,14},{3,15},{4,8},{5,9},{6,10},{7,11},{8,4},{9,5},... | collective-permute-start | bytes 2359304 | tf_op jit(solution)/shard_map/ppermute | solution.py:111
  41.5 1.7 %collective-permute-start.6 = (bf16[64,4096]{1,0:T(8,128)(2,1)S(1)}, bf16[64,4096]{1,0:T(8,128)(2,1)S(1)}, u32[]{:S(2)}, u32[]{:S(2)}) collective-permute-start(bf16[64,4096]{1,0:T(8,128)(2,1)S(1)} %pad_maximum_fusion.5), channel_id=1, source_target_pairs={{0,1},{1,0},{2,3},{3,2},{4,5},{5,4},{6,7},{7,6},{8,9},{9,8},{10,11... | collective-permute-start | bytes 1572872 | tf_op jit(solution)/shard_map/ppermute | solution.py:111
  43.2 20.6 %collective-permute-done.1.refs_0_ = bf16[96,4096]{1,0:T(8,128)(2,1)S(1)} collective-permute-done((bf16[96,4096]{1,0:T(8,128)(2,1)S(1)}, bf16[96,4096]{1,0:T(8,128)(2,1)S(1)}, u32[]{:S(2)}, u32[]{:S(2)}) %collective-permute-start.1) | collective-permute-done | bytes 786464 | tf_op jit(solution)/shard_map/ppermute | solution.py:111
  63.8 5.8 %shard_map.66.refs_4_ = bf16[1024,1792]{1,0:T(8,128)(2,1)} custom-call(s32[28]{0:T(128)S(1)} %dynamic-slice_bitcast_fusion.dst_ref, s32[14,9]{1,0:T(8,128)S(1)} %copy-done.7, s32[14,9]{1,0:T(8,128)S(1)} %copy-done.9, bf16[128,4096]{1,0:T(8,128)(2,1)S(1)} %collective-permute-done.5.refs_0_, ...), custom_call_target="tpu_custom_call", output_to_operand_aliasing={{}: (7, {})} | custom-call | flops 6291999744 | bytes 630784 | tf_op jit(solution)/shard_map/pallas_call | solution.py:87
  69.7 4.7 %collective-permute-start.7 = (bf16[128,4096]{1,0:T(8,128)(2,1)S(1)}, bf16[128,4096]{1,0:T(8,128)(2,1)S(1)}, u32[]{:S(2)}, u32[]{:S(2)}) collective-permute-start(bf16[128,4096]{1,0:T(8,128)(2,1)S(1)} %pad_maximum_fusion.2), channel_id=1, source_target_pairs={{0,3},{1,2},{2,1},{3,0},{4,7},{5,6},{6,5},{7,4},{8,11},{9,10},{10,... | collective-permute-start | bytes 3145736 | tf_op jit(solution)/shard_map/ppermute | solution.py:111
  74.4 1.4 %collective-permute-done.2.refs_0_ = bf16[96,4096]{1,0:T(8,128)(2,1)S(1)} collective-permute-done((bf16[96,4096]{1,0:T(8,128)(2,1)S(1)}, bf16[96,4096]{1,0:T(8,128)(2,1)S(1)}, u32[]{:S(2)}, u32[]{:S(2)}) %collective-permute-start.2) | collective-permute-done | bytes 786464 | tf_op jit(solution)/shard_map/ppermute | solution.py:111
  76.2 6.3 %shard_map.67.refs_4_ = bf16[1024,1792]{1,0:T(8,128)(2,1)} custom-call(s32[28]{0:T(128)S(1)} %dynamic-slice_bitcast_fusion.dst_ref, s32[14,9]{1,0:T(8,128)S(1)} %copy-done.7, s32[14,9]{1,0:T(8,128)S(1)} %copy-done.9, bf16[96,4096]{1,0:T(8,128)(2,1)S(1)} %collective-permute-done.1.refs_0_, ...), custom_call_target="tpu_custom_call", output_to_operand_aliasing={{}: (7, {})} | custom-call | flops 6643999744 | bytes 688128 | tf_op jit(solution)/shard_map/pallas_call | solution.py:87
  82.5 5.5 %shard_map.68.refs_3_ = bf16[1024,1792]{1,0:T(8,128)(2,1)} custom-call(s32[28]{0:T(128)S(1)} %dynamic-slice_bitcast_fusion.dst_ref, s32[14,9]{1,0:T(8,128)S(1)} %copy-done.7, s32[14,9]{1,0:T(8,128)S(1)} %copy-done.9, bf16[96,4096]{1,0:T(8,128)(2,1)S(1)} %collective-permute-done.2.refs_0_, ...), custom_call_target="tpu_custom_call", output_to_operand_aliasing={{}: (7, {})} | custom-call | flops 5939999744 | bytes 573440 | tf_op jit(solution)/shard_map/pallas_call | solution.py:87
  88.1 10.3 %collective-permute-done.7.refs_0_ = bf16[128,4096]{1,0:T(8,128)(2,1)S(1)} collective-permute-done((bf16[128,4096]{1,0:T(8,128)(2,1)S(1)}, bf16[128,4096]{1,0:T(8,128)(2,1)S(1)}, u32[]{:S(2)}, u32[]{:S(2)}) %collective-permute-start.7) | collective-permute-done | bytes 1048608 | tf_op jit(solution)/shard_map/ppermute | solution.py:111
  98.4 4.6 %shard_map.69.refs_3_ = bf16[1024,1792]{1,0:T(8,128)(2,1)} custom-call(s32[28]{0:T(128)S(1)} %dynamic-slice_bitcast_fusion.dst_ref, s32[14,9]{1,0:T(8,128)S(1)} %copy-done.7, s32[14,9]{1,0:T(8,128)S(1)} %copy-done.9, bf16[128,4096]{1,0:T(8,128)(2,1)S(1)} %collective-permute-done.7.refs_0_, ...), custom_call_target="tpu_custom_call", output_to_operand_aliasing={{}: (6, {})} | custom-call | flops 5235999744 | bytes 458752 | tf_op jit(solution)/shard_map/pallas_call | solution.py:87
  103.0 6.1 %shard_map.70 = bf16[1024,1792]{1,0:T(8,128)(2,1)} custom-call(s32[28]{0:T(128)S(1)} %dynamic-slice_bitcast_fusion.dst_ref, s32[14,9]{1,0:T(8,128)S(1)} %copy-done.7, s32[14,9]{1,0:T(8,128)S(1)} %copy-done.9, bf16[192,4096]{1,0:T(8,128)(2,1)S(1)} %collective-permute-done.3.refs_0_, ...), custom_call_target="tpu_custom_call", output_to_operand_aliasing={{}: (6, {})} | custom-call | flops 6643999744 | bytes 688128 | tf_op jit(solution)/shard_map/pallas_call | solution.py:87
  (33 shorter events, 2.7 us)
Async XLA Ops:
  0.0 18.7 %collective-permute-start.4 = (bf16[64,4096]{1,0:T(8,128)(2,1)}, bf16[64,4096]{1,0:T(8,128)(2,1)S(1)}, u32[]{:S(2)}, u32[]{:S(2)}) collective-permute-start(bf16[64,4096]{1,0:T(8,128)(2,1)} %refs_0_.1), channel_id=1, source_target_pairs={{0,4},{1,5},{2,6},{3,7},{4,0},{5,1},{6,2},{7,3},{8,12},{9,13},{10,... | collective-permute-start | bytes 1572872 | tf_op jit(solution)/shard_map/ppermute | solution.py:111
  2.6 15.5 %collective-permute-start = (bf16[48,4096]{1,0:T(8,128)(2,1)S(1)}, bf16[48,4096]{1,0:T(8,128)(2,1)S(1)}, u32[]{:S(2)}, u32[]{:S(2)}) collective-permute-start(bf16[48,4096]{1,0:T(8,128)(2,1)S(1)} %slice_bitcast_fusion), channel_id=1, source_target_pairs={{0,1},{1,0},{2,3},{3,2},{4,5},{5,4},{6,7},{7,6},{8,9},{9,8},{10,11... | collective-permute-start | bytes 1179656 | tf_op jit(solution)/shard_map/ppermute | solution.py:111
  7.6 1.0 copy-start
  8.7 2.2 %copy-start.2 = (bf16[14,9,128,128]{3,2,1,0:T(8,128)(2,1)S(1)}, bf16[14,9,128,128]{3,2,1,0:T(8,128)(2,1)}, u32[]{:S(2)}) copy-start(bf16[14,9,128,128]{3,2,1,0:T(8,128)(2,1)} %refs_1_.5) | copy-start | bytes 12386308
  10.8 2.2 %copy-start.4 = (bf16[14,9,128,128]{3,2,1,0:T(8,128)(2,1)S(1)}, bf16[14,9,128,128]{3,2,1,0:T(8,128)(2,1)}, u32[]{:S(2)}) copy-start(bf16[14,9,128,128]{3,2,1,0:T(8,128)(2,1)} %refs_2_.13) | copy-start | bytes 12386308
  13.0 0.7 copy-start.6
  13.7 0.7 copy-start.8
  14.4 4.3 %copy-start.1 = (bf16[64,4096]{1,0:T(8,128)(2,1)S(1)}, bf16[64,4096]{1,0:T(8,128)(2,1)}, u32[]{:S(2)}) copy-start(bf16[64,4096]{1,0:T(8,128)(2,1)} %refs_0_.1) | copy-start | bytes 1572868
  14.4 20.5 %copy-start.5 = (bf16[14,9,128,128]{3,2,1,0:T(8,128)(2,1)S(1)}, bf16[14,9,128,128]{3,2,1,0:T(8,128)(2,1)}, u32[]{:S(2)}) copy-start(bf16[14,9,128,128]{3,2,1,0:T(8,128)(2,1)} %refs_2_.13) | copy-start | bytes 12386308
  18.1 16.8 %copy-start.3 = (bf16[14,9,128,128]{3,2,1,0:T(8,128)(2,1)S(1)}, bf16[14,9,128,128]{3,2,1,0:T(8,128)(2,1)}, u32[]{:S(2)}) copy-start(bf16[14,9,128,128]{3,2,1,0:T(8,128)(2,1)} %refs_1_.5) | copy-start | bytes 12386308
  18.1 16.8 %copy-start.7 = (s32[14,9]{1,0:T(8,128)S(1)}, s32[14,9]{1,0:T(8,128)}, u32[]{:S(2)}) copy-start(s32[14,9]{1,0:T(8,128)} %gate_rows_ref.13) | copy-start | bytes 1516
  18.1 16.8 %copy-start.9 = (s32[14,9]{1,0:T(8,128)S(1)}, s32[14,9]{1,0:T(8,128)}, u32[]{:S(2)}) copy-start(s32[14,9]{1,0:T(8,128)} %up_rows_ref.13) | copy-start | bytes 1516
  18.2 9.0 %collective-permute-start.8 = (bf16[48,4096]{1,0:T(8,128)(2,1)S(1)}, bf16[48,4096]{1,0:T(8,128)(2,1)S(1)}, u32[]{:S(2)}, u32[]{:S(2)}) collective-permute-start(bf16[48,4096]{1,0:T(8,128)(2,1)S(1)} %collective-permute-done.refs_0_), channel_id=1, source_target_pairs={{0,4},{1,5},{2,6},{3,7},{4,0},{5,1},{6,2},{7,3},{8,12},{9,13},{10,... | collective-permute-start | bytes 1179656 | tf_op jit(solution)/shard_map/ppermute | solution.py:111
  18.8 22.6 %collective-permute-start.5 = (bf16[128,4096]{1,0:T(8,128)(2,1)S(1)}, bf16[128,4096]{1,0:T(8,128)(2,1)S(1)}, u32[]{:S(2)}, u32[]{:S(2)}) collective-permute-start(bf16[128,4096]{1,0:T(8,128)(2,1)S(1)} %pad_maximum_fusion.1), channel_id=1, source_target_pairs={{0,12},{1,13},{2,14},{3,15},{4,8},{5,9},{6,10},{7,11},{8,4},{9,5},... | collective-permute-start | bytes 3145736 | tf_op jit(solution)/shard_map/ppermute | solution.py:111
  27.3 36.5 %collective-permute-start.1 = (bf16[96,4096]{1,0:T(8,128)(2,1)S(1)}, bf16[96,4096]{1,0:T(8,128)(2,1)S(1)}, u32[]{:S(2)}, u32[]{:S(2)}) collective-permute-start(bf16[96,4096]{1,0:T(8,128)(2,1)S(1)} %get-tuple-element.6), channel_id=1, source_target_pairs={{0,3},{1,2},{2,1},{3,0},{4,7},{5,6},{6,5},{7,4},{8,11},{9,10},{10,... | collective-permute-start | bytes 2359304 | tf_op jit(solution)/shard_map/ppermute | solution.py:111
  39.3 36.9 %collective-permute-start.9 = (bf16[96,4096]{1,0:T(8,128)(2,1)S(1)}, bf16[96,4096]{1,0:T(8,128)(2,1)S(1)}, u32[]{:S(2)}, u32[]{:S(2)}) collective-permute-start(bf16[96,4096]{1,0:T(8,128)(2,1)S(1)} %get-tuple-element.5), channel_id=1, source_target_pairs={{0,12},{1,13},{2,14},{3,15},{4,8},{5,9},{6,10},{7,11},{8,4},{9,5},... | collective-permute-start | bytes 2359304 | tf_op jit(solution)/shard_map/ppermute | solution.py:111
  41.5 28.2 %collective-permute-start.6 = (bf16[64,4096]{1,0:T(8,128)(2,1)S(1)}, bf16[64,4096]{1,0:T(8,128)(2,1)S(1)}, u32[]{:S(2)}, u32[]{:S(2)}) collective-permute-start(bf16[64,4096]{1,0:T(8,128)(2,1)S(1)} %pad_maximum_fusion.5), channel_id=1, source_target_pairs={{0,1},{1,0},{2,3},{3,2},{4,5},{5,4},{6,7},{7,6},{8,9},{9,8},{10,11... | collective-permute-start | bytes 1572872 | tf_op jit(solution)/shard_map/ppermute | solution.py:111
  63.8 12.0 %collective-permute-start.2 = (bf16[96,4096]{1,0:T(8,128)(2,1)S(1)}, bf16[96,4096]{1,0:T(8,128)(2,1)S(1)}, u32[]{:S(2)}, u32[]{:S(2)}) collective-permute-start(bf16[96,4096]{1,0:T(8,128)(2,1)S(1)} %collective-permute-done.1.refs_0_), channel_id=1, source_target_pairs={{0,4},{1,5},{2,6},{3,7},{4,0},{5,1},{6,2},{7,3},{8,12},{9,13},{10,... | collective-permute-start | bytes 2359304 | tf_op jit(solution)/shard_map/ppermute | solution.py:111
  69.7 28.7 %collective-permute-start.7 = (bf16[128,4096]{1,0:T(8,128)(2,1)S(1)}, bf16[128,4096]{1,0:T(8,128)(2,1)S(1)}, u32[]{:S(2)}, u32[]{:S(2)}) collective-permute-start(bf16[128,4096]{1,0:T(8,128)(2,1)S(1)} %pad_maximum_fusion.2), channel_id=1, source_target_pairs={{0,3},{1,2},{2,1},{3,0},{4,7},{5,6},{6,5},{7,4},{8,11},{9,10},{10,... | collective-permute-start | bytes 3145736 | tf_op jit(solution)/shard_map/ppermute | solution.py:111
  75.9 27.1 %collective-permute-start.3 = (bf16[192,4096]{1,0:T(8,128)(2,1)S(1)}, bf16[192,4096]{1,0:T(8,128)(2,1)S(1)}, u32[]{:S(2)}, u32[]{:S(2)}) collective-permute-start(bf16[192,4096]{1,0:T(8,128)(2,1)S(1)} %pad_maximum_fusion), channel_id=1, source_target_pairs={{0,12},{1,13},{2,14},{3,15},{4,8},{5,9},{6,10},{7,11},{8,4},{9,5},... | collective-permute-start | bytes 4718600 | tf_op jit(solution)/shard_map/ppermute | solution.py:111

commit v2 on v1

v2 whole, which is shorter than its diff:
```python
import functools

import jax
import jax.numpy as jnp
import numpy as np
from jax import lax
from jax.experimental import pallas as pl
from jax.experimental.pallas import tpu as pltpu
from jax.sharding import PartitionSpec as P

BLK = 128
SIDE = 4
AXES = ("dp", "tensor")
TURNED = 16
UNROLL = 7
COST = 22_000_000


STEPS = {("y", 0): 1, ("y", 1): 2, ("z", 0): 4, ("z", 1): 8}


def mask(core, code):
    found = 0
    for (dim, step), bit in STEPS.items():
        if code & bit:
            found ^= (1, 3)[(step + core) % 2] * (SIDE if dim == "y" else 1)
    return found


class Piece:
    def __init__(self, rows, codes, size, offset):
        self.rows, self.codes, self.size, self.offset = rows, codes, size, offset

    def part(self, offset, size):
        rows = self.rows.reshape(len(self.codes), self.size, -1)[:, offset : offset + size]
        return Piece(rows.reshape(len(self.codes) * size, -1), self.codes, size, self.offset + offset)


def joined(*pieces):
    rows = jnp.concatenate([p.rows for p in pieces], axis=0)
    return Piece(rows, sum([p.codes for p in pieces], []), pieces[0].size, pieces[0].offset)


def after(piece, *others):
    rows, *_ = lax.optimization_barrier((piece.rows, *[getattr(o, "rows", o) for o in others]))
    return Piece(rows, piece.codes, piece.size, piece.offset)


def project_kernel(layout, starts, n_prev, table_ref, *refs):
    n = len(layout)
    pieces, (gate_ref, up_ref) = refs[:n], refs[n : n + 2]
    out_ref, hidden, sems = refs[n + 2 + n_prev :]
    columns, cap = gate_ref.shape[:2]

    def product(start, blocks_ref, c):
        listed = [table_ref[start + c * cap + j] for j in range(cap)]

        def gathered(j):
            start = pl.multiple_of(jnp.maximum(listed[j], 0) * BLK, BLK)
            return jnp.concatenate([p[:, pl.ds(start, BLK)] for p in pieces], axis=0)

        lhs = jnp.concatenate([gathered(j) for j in range(cap)], axis=1)
        rhs = jnp.concatenate(
            [jnp.where(listed[j] >= 0, blocks_ref[c, j], jnp.zeros((), blocks_ref.dtype)) for j in range(cap)], axis=0
        )
        return jnp.dot(lhs, rhs, preferred_element_type=jnp.float32)

    @pl.loop(0, columns, step=UNROLL)
    def _(first):
        for k in range(UNROLL):
            c = first + k
            gate = product(starts[0], gate_ref, c)
            up = product(starts[1], up_ref, c)
            value = gate * (1.0 / (1.0 + jnp.exp(-gate))) * up
            hidden[:, pl.ds(pl.multiple_of(c * BLK, BLK), BLK)] = value.astype(hidden.dtype)

    copies, base = [], 0
    for codes, size, offset in layout:
        for code in codes:
            i = len(copies)
            to = pl.multiple_of(table_ref[code] + offset, 16)
            copies.append(pltpu.make_async_copy(hidden.at[pl.ds(base, size)], out_ref.at[pl.ds(to, size)], sems.at[i]))
            base += size
    for copy in copies:
        copy.start()
    for copy in copies:
        copy.wait()


def project(pieces, total_rows, table, starts, blocks, result):
    rows = sum(p.rows.shape[0] for p in pieces)
    layout = [(p.codes, p.size, p.offset) for p in pieces]
    width = blocks[0].shape[0] * BLK
    prev = [] if result is None else [result]
    vmem, smem, hbm = (pl.BlockSpec(memory_space=m) for m in (pltpu.VMEM, pltpu.SMEM, pl.ANY))
    return pl.pallas_call(
        functools.partial(project_kernel, layout, starts, len(prev)),
        out_shape=jax.ShapeDtypeStruct((total_rows, width), jnp.bfloat16),
        in_specs=[smem] + [vmem] * (len(pieces) + 2) + [hbm] * len(prev),
        out_specs=hbm,
        scratch_shapes=[
            pltpu.VMEM((rows, width), jnp.bfloat16),
            pltpu.SemaphoreType.DMA((sum(len(p.codes) for p in pieces),)),
        ],
        input_output_aliases={3 + len(pieces): 0} if prev else {},
        cost_estimate=pl.CostEstimate(
            flops=COST * (rows + 110), bytes_accessed=2 * rows * width, transcendentals=rows * width
        ),
        compiler_params=pltpu.CompilerParams(vmem_limit_bytes=8 << 20),
    )(table, *[p.rows for p in pieces], *blocks, *prev)


def solution(mesh):
    groups, members = mesh.shape["dp"], mesh.shape["tensor"]

    def swap(piece, dim, step):
        bit = STEPS[dim, step]
        pairs = [(g * members + m, g * members + (m ^ mask(g % 2, bit))) for g in range(groups) for m in range(members)]
        rows = lax.ppermute(piece.rows, AXES, pairs)
        return Piece(rows, [code ^ bit for code in piece.codes], piece.size, piece.offset)

    def shards(tokens, gate_rows, gate_blocks, up_rows, up_blocks):
        local = tokens.shape[0]
        masks = jnp.asarray(np.array([[mask(core, code) for code in range(members)] for core in range(2)], np.int32))
        core, me = lax.axis_index("dp") % 2, lax.axis_index("tensor")
        table = jnp.concatenate([(masks[core] ^ me) * local, gate_rows.reshape(-1), up_rows.reshape(-1)])
        starts = (members, members + gate_rows.size)
        run = lambda pieces, result: project(
            pieces, members * local, table, starts, (gate_blocks, up_blocks), result
        )

        own = Piece(tokens, [0], local, 0)
        mine = own.part(TURNED, local - TURNED)
        z1 = swap(mine, "z", 0)
        y1 = swap(own, "y", 0)
        y2 = swap(own, "y", 1)
        z2 = swap(mine, "z", 1)
        y3 = swap(y1, "y", 1)
        result = run([own, y1], None)
        z1, z2 = after(z1, result), after(z2, result)
        z3 = swap(after(z1, y3), "z", 1)
        pair = joined(z1, z2)
        p1 = swap(after(pair, y3), "y", 0)
        column = joined(*[p.part(0, TURNED) for p in (own, y1, y2, y3)])
        b1 = swap(column, "z", 0)
        b2 = swap(column, "z", 1)
        q1 = swap(after(z3, p1), "y", 0)
        p2 = swap(joined(pair, p1), "y", 1)
        b3 = swap(b1, "z", 1)
        q2 = swap(after(joined(z3, q1), b1), "y", 1)
        for pieces in ([y2, z1, z2], [y3, z3, p1], [q1, b1, b2], [p2], [b3], [q2]):
            result = run(pieces, result)
        return result

    in_specs = (
        P(AXES, None),
        P("tensor", None),
        P("tensor", None, None, None),
        P("tensor", None),
        P("tensor", None, None, None),
    )
    return jax.shard_map(shards, mesh=mesh, in_specs=in_specs, out_specs=P("dp", "tensor"), check_vma=False)
```

time: 110 us -> 104 us (0.945); the launches traced: 109 us -> 102 us
  waiting for transfers between devices: 37.6 us -> 31.9 us
  Pallas kernels: 36.4 us -> 34.4 us
    ppermute x10 -> x13, waiting for transfers between devices: 37.6 us -> 31.9 us  [swap(): rows = lax.ppermute(piece.rows, AXES, pairs)]
    pallas_call x7, Pallas kernels: 36.4 us -> 34.4 us  [project(): pl.pallas_call(functools.partial(project_kernel, layout, starts, len(prev...]
    reshape x3 -> x7, local copies, waits for them, and re-layouts: 1.98 us -> 3.56 us  [the longest x5 2 us: part(): rows.reshape(len(self.codes) * size, -1)]
    unnamed x20 -> x10, local copies, waits for them, and re-layouts: 6.8 us -> 5.39 us
    ppermute x10 -> x13, starting transfers between devices: 25 us -> 25.4 us  [swap(): rows = lax.ppermute(piece.rows, AXES, pairs)]
  transfers between devices with their start and end apart: 10 -> 13, of which waited for: 4 -> 4; matrix products, arithmetic and copies ran while one was open for 3% -> 5% of each run, Pallas kernels for 28% -> 30%
where the time goes in v2:
time: 104 us; the launch traced here: 102 us
  Pallas kernels  34.4 us (33%)
  waiting for transfers between devices  31.9 us (31%)
  starting transfers between devices  25.4 us (24%)
  local copies, waits for them, and re-layouts  8.94 us (9%)
  other arithmetic  1.05 us (1%)
    pallas_call x7, Pallas kernels, project(): pl.pallas_call(functools.partial(project_kernel, layout, starts, len(prev...  34.4 us
    ppermute x13, waiting for transfers between devices, swap(): rows = lax.ppermute(piece.rows, AXES, pairs)  31.9 us
    ppermute x13, starting transfers between devices, swap(): rows = lax.ppermute(piece.rows, AXES, pairs)  25.4 us
    unnamed x10, local copies, waits for them, and re-layouts  5.39 us
  transfers between devices with their start and end apart: 13, of which 4 were waited for; matrix products, arithmetic and copies ran while one was open for 5% of the time, Pallas kernels for 30%

profile of v2, /device:TPU:4, one launch (start us, length us, event | category | flops | bytes accessed | tf_op | source)
XLA Modules:
  0.0 102.0 jit_solution(1154228348679639700)
XLA Ops:
  0.0 1.6 %collective-permute-start.1 = (bf16[64,4096]{1,0:T(8,128)(2,1)}, bf16[64,4096]{1,0:T(8,128)(2,1)S(1)}, u32[]{:S(2)}, u32[]{:S(2)}) collective-permute-start(bf16[64,4096]{1,0:T(8,128)(2,1)} %refs_0_.1), channel_id=1, source_target_pairs={{0,4},{1,5},{2,6},{3,7},{4,0},{5,1},{6,2},{7,3},{8,12},{9,13},{10,... | collective-permute-start | bytes 1572872 | tf_op jit(solution)/shard_map/ppermute | solution.py:119
  1.6 1.1 %slice_bitcast_fusion = bf16[48,4096]{1,0:T(8,128)(2,1)S(1)} fusion(bf16[1,64,4096]{2,1,0:T(8,128)(2,1)} %bitcast.16), kind=kLoop, calls=%fused_computation.4 | loop fusion | bytes 786432 | tf_op jit(solution)/shard_map/reshape | solution.py:36
  2.6 3.4 %collective-permute-start = (bf16[48,4096]{1,0:T(8,128)(2,1)S(1)}, bf16[48,4096]{1,0:T(8,128)(2,1)S(1)}, u32[]{:S(2)}, u32[]{:S(2)}) collective-permute-start(bf16[48,4096]{1,0:T(8,128)(2,1)S(1)} %slice_bitcast_fusion), channel_id=1, source_target_pairs={{0,1},{1,0},{2,3},{3,2},{4,5},{5,4},{6,7},{7,6},{8,9},{9,8},{10,11... | collective-permute-start | bytes 1179656 | tf_op jit(solution)/shard_map/ppermute | solution.py:119
  6.0 4.5 %collective-permute-start.4 = (bf16[48,4096]{1,0:T(8,128)(2,1)S(1)}, bf16[48,4096]{1,0:T(8,128)(2,1)S(1)}, u32[]{:S(2)}, u32[]{:S(2)}) collective-permute-start(bf16[48,4096]{1,0:T(8,128)(2,1)S(1)} %slice_bitcast_fusion), channel_id=1, source_target_pairs={{0,3},{1,2},{2,1},{3,0},{4,7},{5,6},{6,5},{7,4},{8,11},{9,10},{10,... | collective-permute-start | bytes 1179656 | tf_op jit(solution)/shard_map/ppermute | solution.py:119
  10.5 2.2 %collective-permute-start.7 = (bf16[64,4096]{1,0:T(8,128)(2,1)}, bf16[64,4096]{1,0:T(8,128)(2,1)S(1)}, u32[]{:S(2)}, u32[]{:S(2)}) collective-permute-start(bf16[64,4096]{1,0:T(8,128)(2,1)} %refs_0_.1), channel_id=1, source_target_pairs={{0,12},{1,13},{2,14},{3,15},{4,8},{5,9},{6,10},{7,11},{8,4},{9,5},... | collective-permute-start | bytes 1572872 | tf_op jit(solution)/shard_map/ppermute | solution.py:119
  15.9 5.1 %collective-permute-done.7.refs_0_ = bf16[64,4096]{1,0:T(8,128)(2,1)S(1)} collective-permute-done((bf16[64,4096]{1,0:T(8,128)(2,1)}, bf16[64,4096]{1,0:T(8,128)(2,1)S(1)}, u32[]{:S(2)}, u32[]{:S(2)}) %collective-permute-start.7) | collective-permute-done | bytes 524320 | tf_op jit(solution)/shard_map/ppermute | solution.py:119
  21.1 2.3 %collective-permute-start.2 = (bf16[64,4096]{1,0:T(8,128)(2,1)S(1)}, bf16[64,4096]{1,0:T(8,128)(2,1)S(1)}, u32[]{:S(2)}, u32[]{:S(2)}) collective-permute-start(bf16[64,4096]{1,0:T(8,128)(2,1)S(1)} %collective-permute-done.1.refs_1_), channel_id=1, source_target_pairs={{0,12},{1,13},{2,14},{3,15},{4,8},{5,9},{6,10},{7,11},{8,4},{9,5},... | collective-permute-start | bytes 1572872 | tf_op jit(solution)/shard_map/ppermute | solution.py:119
  23.4 2.2 %copy-done = bf16[14,9,128,128]{3,2,1,0:T(8,128)(2,1)S(1)} copy-done((bf16[14,9,128,128]{3,2,1,0:T(8,128)(2,1)S(1)}, bf16[14,9,128,128]{3,2,1,0:T(8,128)(2,1)}, u32[]{:S(2)}) %copy-start) | copy-done | bytes 4128792
  25.5 2.2 %copy-done.2 = bf16[14,9,128,128]{3,2,1,0:T(8,128)(2,1)S(1)} copy-done((bf16[14,9,128,128]{3,2,1,0:T(8,128)(2,1)S(1)}, bf16[14,9,128,128]{3,2,1,0:T(8,128)(2,1)}, u32[]{:S(2)}) %copy-start.2) | copy-done | bytes 4128792
  28.7 4.3 %shard_map.64.refs_5_ = bf16[1024,1792]{1,0:T(8,128)(2,1)} custom-call(s32[268]{0:T(512)S(1)} %pad_add_fusion.table_ref, bf16[64,4096]{1,0:T(8,128)(2,1)S(1)} %copy-done.4, bf16[64,4096]{1,0:T(8,128)(2,1)S(1)} %collective-permute-done.1.refs_1_, bf16[14,9,128,128]{3,2,1,0:T(8,128)(2,1)S(1)} %copy-done, bf16[14,9,128,128]{3,2,1,0:T(8,128)(2,1)S(1)} %copy-done.2), custom_call_target="tpu_custom_call" | custom-call | flops 5235999744 | bytes 458752 | tf_op jit(solution)/shard_map/pallas_call | solution.py:96
  33.3 1.2 %collective-permute-start.3 = (bf16[48,4096]{1,0:T(8,128)(2,1)S(1)}, bf16[48,4096]{1,0:T(8,128)(2,1)S(1)}, u32[]{:S(2)}, u32[]{:S(2)}) collective-permute-start(bf16[48,4096]{1,0:T(8,128)(2,1)S(1)} %collective-permute-done.refs_1_), channel_id=1, source_target_pairs={{0,3},{1,2},{2,1},{3,0},{4,7},{5,6},{6,5},{7,4},{8,11},{9,10},{10,... | collective-permute-start | bytes 1179656 | tf_op jit(solution)/shard_map/ppermute | solution.py:119
  34.6 1.6 %collective-permute-start.8 = (bf16[64,4096]{1,0:T(8,128)(2,1)S(1)}, bf16[64,4096]{1,0:T(8,128)(2,1)S(1)}, u32[]{:S(2)}, u32[]{:S(2)}) collective-permute-start(bf16[64,4096]{1,0:T(8,128)(2,1)S(1)} %pad_maximum_fusion.3), channel_id=1, source_target_pairs={{0,1},{1,0},{2,3},{3,2},{4,5},{5,4},{6,7},{7,6},{8,9},{9,8},{10,11... | collective-permute-start | bytes 1572872 | tf_op jit(solution)/shard_map/ppermute | solution.py:119
  36.1 5.0 %shard_map.65.refs_5_ = bf16[1024,1792]{1,0:T(8,128)(2,1)} custom-call(s32[268]{0:T(512)S(1)} %pad_add_fusion.table_ref, bf16[64,4096]{1,0:T(8,128)(2,1)S(1)} %collective-permute-done.7.refs_0_, bf16[48,4096]{1,0:T(8,128)(2,1)S(1)} %collective-permute-done.refs_1_, ...), custom_call_target="tpu_custom_call", output_to_operand_aliasing={{}: (6, {})} | custom-call | flops 5939999744 | bytes 573440 | tf_op jit(solution)/shard_map/pallas_call | solution.py:96
  41.2 3.1 %collective-permute-start.12 = (bf16[64,4096]{1,0:T(8,128)(2,1)S(1)}, bf16[64,4096]{1,0:T(8,128)(2,1)S(1)}, u32[]{:S(2)}, u32[]{:S(2)}) collective-permute-start(bf16[64,4096]{1,0:T(8,128)(2,1)S(1)} %pad_maximum_fusion.3), channel_id=1, source_target_pairs={{0,3},{1,2},{2,1},{3,0},{4,7},{5,6},{6,5},{7,4},{8,11},{9,10},{10,... | collective-permute-start | bytes 1572872 | tf_op jit(solution)/shard_map/ppermute | solution.py:119
  44.3 17.7 %collective-permute-done.8.refs_1_ = bf16[64,4096]{1,0:T(8,128)(2,1)S(1)} collective-permute-done((bf16[64,4096]{1,0:T(8,128)(2,1)S(1)}, bf16[64,4096]{1,0:T(8,128)(2,1)S(1)}, u32[]{:S(2)}, u32[]{:S(2)}) %collective-permute-start.8) | collective-permute-done | bytes 524320 | tf_op jit(solution)/shard_map/ppermute | solution.py:119
  61.9 1.8 %collective-permute-start.10 = (bf16[64,4096]{1,0:T(8,128)(2,1)S(1)}, bf16[64,4096]{1,0:T(8,128)(2,1)S(1)}, u32[]{:S(2)}, u32[]{:S(2)}) collective-permute-start(bf16[64,4096]{1,0:T(8,128)(2,1)S(1)} %collective-permute-done.8.refs_1_), channel_id=1, source_target_pairs={{0,3},{1,2},{2,1},{3,0},{4,7},{5,6},{6,5},{7,4},{8,11},{9,10},{10,... | collective-permute-start | bytes 1572872 | tf_op jit(solution)/shard_map/ppermute | solution.py:119
  63.8 2.4 %collective-permute-start.6 = (bf16[48,4096]{1,0:T(8,128)(2,1)S(1)}, bf16[48,4096]{1,0:T(8,128)(2,1)S(1)}, u32[]{:S(2)}, u32[]{:S(2)}) collective-permute-start(bf16[48,4096]{1,0:T(8,128)(2,1)S(1)} %collective-permute-done.3.refs_1_), channel_id=1, source_target_pairs={{0,4},{1,5},{2,6},{3,7},{4,0},{5,1},{6,2},{7,3},{8,12},{9,13},{10,... | collective-permute-start | bytes 1179656 | tf_op jit(solution)/shard_map/ppermute | solution.py:119
  66.6 6.1 %shard_map.66.refs_5_ = bf16[1024,1792]{1,0:T(8,128)(2,1)} custom-call(s32[268]{0:T(512)S(1)} %pad_add_fusion.table_ref, bf16[64,4096]{1,0:T(8,128)(2,1)S(1)} %collective-permute-done.2.refs_0_, bf16[48,4096]{1,0:T(8,128)(2,1)S(1)} %collective-permute-done.3.refs_1_, ...), custom_call_target="tpu_custom_call", output_to_operand_aliasing={{}: (6, {})} | custom-call | flops 6995999744 | bytes 745472 | tf_op jit(solution)/shard_map/pallas_call | solution.py:96
  72.8 2.9 %collective-permute-done.6.refs_0_ = bf16[48,4096]{1,0:T(8,128)(2,1)S(1)} collective-permute-done((bf16[48,4096]{1,0:T(8,128)(2,1)S(1)}, bf16[48,4096]{1,0:T(8,128)(2,1)S(1)}, u32[]{:S(2)}, u32[]{:S(2)}) %collective-permute-start.6) | collective-permute-done | bytes 393248 | tf_op jit(solution)/shard_map/ppermute | solution.py:119
  76.8 5.6 %shard_map.67.refs_3_ = bf16[1024,1792]{1,0:T(8,128)(2,1)} custom-call(s32[268]{0:T(512)S(1)} %pad_add_fusion.table_ref, bf16[48,4096]{1,0:T(8,128)(2,1)S(1)} %collective-permute-done.6.refs_0_, bf16[64,4096]{1,0:T(8,128)(2,1)S(1)} %collective-permute-done.8.refs_1_, ...), custom_call_target="tpu_custom_call", output_to_operand_aliasing={{}: (6, {})} | custom-call | flops 6291999744 | bytes 630784 | tf_op jit(solution)/shard_map/pallas_call | solution.py:96
  82.4 6.2 %collective-permute-done.11.refs_0_ = bf16[192,4096]{1,0:T(8,128)(2,1)S(1)} collective-permute-done((bf16[192,4096]{1,0:T(8,128)(2,1)S(1)}, bf16[192,4096]{1,0:T(8,128)(2,1)S(1)}, u32[]{:S(2)}, u32[]{:S(2)}) %collective-permute-start.11) | collective-permute-done | bytes 1572896 | tf_op jit(solution)/shard_map/ppermute | solution.py:119
  88.5 5.9 %shard_map.68.refs_3_ = bf16[1024,1792]{1,0:T(8,128)(2,1)} custom-call(s32[268]{0:T(512)S(1)} %pad_add_fusion.table_ref, bf16[192,4096]{1,0:T(8,128)(2,1)S(1)} %collective-permute-done.11.refs_0_, bf16[14,9,128,128]{3,2,1,0:T(8,128)(2,1)S(1)} %copy-done.1, bf16[14,9,128,128]{3,2,1,0:T(8,128)(2,1)S(1)} %copy-done.3, ...), custom_call_target="tpu_custom_call", output_to_operand_aliasing={{}: (4, {})} | custom-call | flops 6643999744 | bytes 688128 | tf_op jit(solution)/shard_map/pallas_call | solution.py:96
  94.5 3.5 %shard_map.69.refs_3_ = bf16[1024,1792]{1,0:T(8,128)(2,1)} custom-call(s32[268]{0:T(512)S(1)} %pad_add_fusion.table_ref, bf16[64,4096]{1,0:T(8,128)(2,1)S(1)} %collective-permute-done.10.refs_0_, bf16[14,9,128,128]{3,2,1,0:T(8,128)(2,1)S(1)} %copy-done.1, bf16[14,9,128,128]{3,2,1,0:T(8,128)(2,1)S(1)} %copy-done.3, ...), custom_call_target="tpu_custom_call", output_to_operand_aliasing={{}: (4, {})} | custom-call | flops 3828000000 | bytes 229376 | tf_op jit(solution)/shard_map/pallas_call | solution.py:96
  98.0 3.9 %shard_map.70 = bf16[1024,1792]{1,0:T(8,128)(2,1)} custom-call(s32[268]{0:T(512)S(1)} %pad_add_fusion.table_ref, bf16[96,4096]{1,0:T(8,128)(2,1)S(1)} %collective-permute-done.9.refs_0_, bf16[14,9,128,128]{3,2,1,0:T(8,128)(2,1)S(1)} %copy-done.1, bf16[14,9,128,128]{3,2,1,0:T(8,128)(2,1)S(1)} %copy-done.3, ...), custom_call_target="tpu_custom_call", output_to_operand_aliasing={{}: (4, {})} | custom-call | flops 4531999744 | bytes 344064 | tf_op jit(solution)/shard_map/pallas_call | solution.py:96
  (32 shorter events, 6.0 us)
Async XLA Ops:
  0.0 15.9 %collective-permute-start.1 = (bf16[64,4096]{1,0:T(8,128)(2,1)}, bf16[64,4096]{1,0:T(8,128)(2,1)S(1)}, u32[]{:S(2)}, u32[]{:S(2)}) collective-permute-start(bf16[64,4096]{1,0:T(8,128)(2,1)} %refs_0_.1), channel_id=1, source_target_pairs={{0,4},{1,5},{2,6},{3,7},{4,0},{5,1},{6,2},{7,3},{8,12},{9,13},{10,... | collective-permute-start | bytes 1572872 | tf_op jit(solution)/shard_map/ppermute | solution.py:119
  2.6 30.5 %collective-permute-start = (bf16[48,4096]{1,0:T(8,128)(2,1)S(1)}, bf16[48,4096]{1,0:T(8,128)(2,1)S(1)}, u32[]{:S(2)}, u32[]{:S(2)}) collective-permute-start(bf16[48,4096]{1,0:T(8,128)(2,1)S(1)} %slice_bitcast_fusion), channel_id=1, source_target_pairs={{0,1},{1,0},{2,3},{3,2},{4,5},{5,4},{6,7},{7,6},{8,9},{9,8},{10,11... | collective-permute-start | bytes 1179656 | tf_op jit(solution)/shard_map/ppermute | solution.py:119
  6.0 27.1 %collective-permute-start.4 = (bf16[48,4096]{1,0:T(8,128)(2,1)S(1)}, bf16[48,4096]{1,0:T(8,128)(2,1)S(1)}, u32[]{:S(2)}, u32[]{:S(2)}) collective-permute-start(bf16[48,4096]{1,0:T(8,128)(2,1)S(1)} %slice_bitcast_fusion), channel_id=1, source_target_pairs={{0,3},{1,2},{2,1},{3,0},{4,7},{5,6},{6,5},{7,4},{8,11},{9,10},{10,... | collective-permute-start | bytes 1179656 | tf_op jit(solution)/shard_map/ppermute | solution.py:119
  10.5 10.6 %collective-permute-start.7 = (bf16[64,4096]{1,0:T(8,128)(2,1)}, bf16[64,4096]{1,0:T(8,128)(2,1)S(1)}, u32[]{:S(2)}, u32[]{:S(2)}) collective-permute-start(bf16[64,4096]{1,0:T(8,128)(2,1)} %refs_0_.1), channel_id=1, source_target_pairs={{0,12},{1,13},{2,14},{3,15},{4,8},{5,9},{6,10},{7,11},{8,4},{9,5},... | collective-permute-start | bytes 1572872 | tf_op jit(solution)/shard_map/ppermute | solution.py:119
  21.1 12.1 %collective-permute-start.2 = (bf16[64,4096]{1,0:T(8,128)(2,1)S(1)}, bf16[64,4096]{1,0:T(8,128)(2,1)S(1)}, u32[]{:S(2)}, u32[]{:S(2)}) collective-permute-start(bf16[64,4096]{1,0:T(8,128)(2,1)S(1)} %collective-permute-done.1.refs_1_), channel_id=1, source_target_pairs={{0,12},{1,13},{2,14},{3,15},{4,8},{5,9},{6,10},{7,11},{8,4},{9,5},... | collective-permute-start | bytes 1572872 | tf_op jit(solution)/shard_map/ppermute | solution.py:119
  23.4 2.2 %copy-start = (bf16[14,9,128,128]{3,2,1,0:T(8,128)(2,1)S(1)}, bf16[14,9,128,128]{3,2,1,0:T(8,128)(2,1)}, u32[]{:S(2)}) copy-start(bf16[14,9,128,128]{3,2,1,0:T(8,128)(2,1)} %refs_1_.5) | copy-start | bytes 12386308
  25.5 2.2 %copy-start.2 = (bf16[14,9,128,128]{3,2,1,0:T(8,128)(2,1)S(1)}, bf16[14,9,128,128]{3,2,1,0:T(8,128)(2,1)}, u32[]{:S(2)}) copy-start(bf16[14,9,128,128]{3,2,1,0:T(8,128)(2,1)} %refs_2_.7) | copy-start | bytes 12386308
  27.7 1.0 %copy-start.4 = (bf16[64,4096]{1,0:T(8,128)(2,1)S(1)}, bf16[64,4096]{1,0:T(8,128)(2,1)}, u32[]{:S(2)}) copy-start(bf16[64,4096]{1,0:T(8,128)(2,1)} %refs_0_.1) | copy-start | bytes 1572868
  28.7 7.4 %copy-start.1 = (bf16[14,9,128,128]{3,2,1,0:T(8,128)(2,1)S(1)}, bf16[14,9,128,128]{3,2,1,0:T(8,128)(2,1)}, u32[]{:S(2)}) copy-start(bf16[14,9,128,128]{3,2,1,0:T(8,128)(2,1)} %refs_1_.5) | copy-start | bytes 12386308
  28.7 7.4 %copy-start.3 = (bf16[14,9,128,128]{3,2,1,0:T(8,128)(2,1)S(1)}, bf16[14,9,128,128]{3,2,1,0:T(8,128)(2,1)}, u32[]{:S(2)}) copy-start(bf16[14,9,128,128]{3,2,1,0:T(8,128)(2,1)} %refs_2_.7) | copy-start | bytes 12386308
  33.2 30.6 %collective-permute-start.5 = (bf16[96,4096]{1,0:T(8,128)(2,1)S(1)}, bf16[96,4096]{1,0:T(8,128)(2,1)S(1)}, u32[]{:S(2)}, u32[]{:S(2)}) collective-permute-start(bf16[96,4096]{1,0:T(8,128)(2,1)S(1)} %pad_maximum_fusion.1), channel_id=1, source_target_pairs={{0,4},{1,5},{2,6},{3,7},{4,0},{5,1},{6,2},{7,3},{8,12},{9,13},{10,... | collective-permute-start | bytes 2359304 | tf_op jit(solution)/shard_map/ppermute | solution.py:119
  33.3 30.5 %collective-permute-start.3 = (bf16[48,4096]{1,0:T(8,128)(2,1)S(1)}, bf16[48,4096]{1,0:T(8,128)(2,1)S(1)}, u32[]{:S(2)}, u32[]{:S(2)}) collective-permute-start(bf16[48,4096]{1,0:T(8,128)(2,1)S(1)} %collective-permute-done.refs_1_), channel_id=1, source_target_pairs={{0,3},{1,2},{2,1},{3,0},{4,7},{5,6},{6,5},{7,4},{8,11},{9,10},{10,... | collective-permute-start | bytes 1179656 | tf_op jit(solution)/shard_map/ppermute | solution.py:119
  34.6 27.4 %collective-permute-start.8 = (bf16[64,4096]{1,0:T(8,128)(2,1)S(1)}, bf16[64,4096]{1,0:T(8,128)(2,1)S(1)}, u32[]{:S(2)}, u32[]{:S(2)}) collective-permute-start(bf16[64,4096]{1,0:T(8,128)(2,1)S(1)} %pad_maximum_fusion.3), channel_id=1, source_target_pairs={{0,1},{1,0},{2,3},{3,2},{4,5},{5,4},{6,7},{7,6},{8,9},{9,8},{10,11... | collective-permute-start | bytes 1572872 | tf_op jit(solution)/shard_map/ppermute | solution.py:119
  41.2 35.6 %collective-permute-start.12 = (bf16[64,4096]{1,0:T(8,128)(2,1)S(1)}, bf16[64,4096]{1,0:T(8,128)(2,1)S(1)}, u32[]{:S(2)}, u32[]{:S(2)}) collective-permute-start(bf16[64,4096]{1,0:T(8,128)(2,1)S(1)} %pad_maximum_fusion.3), channel_id=1, source_target_pairs={{0,3},{1,2},{2,1},{3,0},{4,7},{5,6},{6,5},{7,4},{8,11},{9,10},{10,... | collective-permute-start | bytes 1572872 | tf_op jit(solution)/shard_map/ppermute | solution.py:119
  61.9 32.5 %collective-permute-start.10 = (bf16[64,4096]{1,0:T(8,128)(2,1)S(1)}, bf16[64,4096]{1,0:T(8,128)(2,1)S(1)}, u32[]{:S(2)}, u32[]{:S(2)}) collective-permute-start(bf16[64,4096]{1,0:T(8,128)(2,1)S(1)} %collective-permute-done.8.refs_1_), channel_id=1, source_target_pairs={{0,3},{1,2},{2,1},{3,0},{4,7},{5,6},{6,5},{7,4},{8,11},{9,10},{10,... | collective-permute-start | bytes 1572872 | tf_op jit(solution)/shard_map/ppermute | solution.py:119
  63.8 11.9 %collective-permute-start.6 = (bf16[48,4096]{1,0:T(8,128)(2,1)S(1)}, bf16[48,4096]{1,0:T(8,128)(2,1)S(1)}, u32[]{:S(2)}, u32[]{:S(2)}) collective-permute-start(bf16[48,4096]{1,0:T(8,128)(2,1)S(1)} %collective-permute-done.3.refs_1_), channel_id=1, source_target_pairs={{0,4},{1,5},{2,6},{3,7},{4,0},{5,1},{6,2},{7,3},{8,12},{9,13},{10,... | collective-permute-start | bytes 1179656 | tf_op jit(solution)/shard_map/ppermute | solution.py:119
  66.4 22.2 %collective-permute-start.11 = (bf16[192,4096]{1,0:T(8,128)(2,1)S(1)}, bf16[192,4096]{1,0:T(8,128)(2,1)S(1)}, u32[]{:S(2)}, u32[]{:S(2)}) collective-permute-start(bf16[192,4096]{1,0:T(8,128)(2,1)S(1)} %pad_maximum_fusion), channel_id=1, source_target_pairs={{0,12},{1,13},{2,14},{3,15},{4,8},{5,9},{6,10},{7,11},{8,4},{9,5},... | collective-permute-start | bytes 4718600 | tf_op jit(solution)/shard_map/ppermute | solution.py:119
  75.8 22.3 %collective-permute-start.9 = (bf16[96,4096]{1,0:T(8,128)(2,1)S(1)}, bf16[96,4096]{1,0:T(8,128)(2,1)S(1)}, u32[]{:S(2)}, u32[]{:S(2)}) collective-permute-start(bf16[96,4096]{1,0:T(8,128)(2,1)S(1)} %pad_maximum_fusion.2), channel_id=1, source_target_pairs={{0,12},{1,13},{2,14},{3,15},{4,8},{5,9},{6,10},{7,11},{8,4},{9,5},... | collective-permute-start | bytes 2359304 | tf_op jit(solution)/shard_map/ppermute | solution.py:119

commit v3 on v2

--- a/solution.py
+++ b/solution.py
@@ -131,24 +131,24 @@
 
         own = Piece(tokens, [0], local, 0)
         mine = own.part(TURNED, local - TURNED)
-        z1 = swap(mine, "z", 0)
         y1 = swap(own, "y", 0)
         y2 = swap(own, "y", 1)
+        z1 = swap(mine, "z", 0)
         z2 = swap(mine, "z", 1)
         y3 = swap(y1, "y", 1)
-        result = run([own, y1], None)
-        z1, z2 = after(z1, result), after(z2, result)
+        z1, z2 = after(z1, y1, y2), after(z2, y1, y2)
         z3 = swap(after(z1, y3), "z", 1)
         pair = joined(z1, z2)
         p1 = swap(after(pair, y3), "y", 0)
         column = joined(*[p.part(0, TURNED) for p in (own, y1, y2, y3)])
         b1 = swap(column, "z", 0)
-        b2 = swap(column, "z", 1)
+        p2 = swap(joined(pair, p1), "y", 1)
         q1 = swap(after(z3, p1), "y", 0)
-        p2 = swap(joined(pair, p1), "y", 1)
-        b3 = swap(b1, "z", 1)
+        b2 = swap(after(column, z3), "z", 1)
+        b3 = swap(after(b1, q1), "z", 1)
         q2 = swap(after(joined(z3, q1), b1), "y", 1)
-        for pieces in ([y2, z1, z2], [y3, z3, p1], [q1, b1, b2], [p2], [b3], [q2]):
+        result = None
+        for pieces in ([own, y1, after(y2, y3)], [y3, z1, z2], [z3, p1, b1], [q1, p2], [b2, b3], [q2]):
             result = run(pieces, result)
         return result
 

time: 104 us -> 91.5 us (0.88); the launches traced: 102 us -> 91.2 us
  waiting for transfers between devices: 31.9 us -> 21.2 us
  starting transfers between devices: 25.4 us -> 28.5 us
  Pallas kernels: 34.4 us -> 32.3 us
    ppermute x13, waiting for transfers between devices: 31.9 us -> 21.2 us  [swap(): rows = lax.ppermute(piece.rows, AXES, pairs)]
    ppermute x13, starting transfers between devices: 25.4 us -> 28.5 us  [swap(): rows = lax.ppermute(piece.rows, AXES, pairs)]
    pallas_call x7 -> x6, Pallas kernels: 34.4 us -> 32.3 us  [project(): pl.pallas_call(functools.partial(project_kernel, layout, starts, len(prev...]
  transfers between devices with their start and end apart: 13 -> 13, of which waited for: 4 -> 6; matrix products, arithmetic and copies ran while one was open for 5% -> 5% of each run, Pallas kernels for 30% -> 31%
where the time goes in v3:
time: 91.5 us; the launch traced here: 91.2 us
  Pallas kernels  32.3 us (35%)
  starting transfers between devices  28.5 us (31%)
  waiting for transfers between devices  21.2 us (23%)
  local copies, waits for them, and re-layouts  7.91 us (9%)
  other arithmetic  1.05 us (1%)
    pallas_call x6, Pallas kernels, project(): pl.pallas_call(functools.partial(project_kernel, layout, starts, len(prev...  32.3 us
    ppermute x13, starting transfers between devices, swap(): rows = lax.ppermute(piece.rows, AXES, pairs)  28.5 us
    ppermute x13, waiting for transfers between devices, swap(): rows = lax.ppermute(piece.rows, AXES, pairs)  21.2 us
    unnamed x10, local copies, waits for them, and re-layouts  4.35 us
    reshape x5, local copies, waits for them, and re-layouts, part(): rows.reshape(len(self.codes) * size, -1)  2 us
  transfers between devices with their start and end apart: 13, of which 6 were waited for; matrix products, arithmetic and copies ran while one was open for 5% of the time, Pallas kernels for 31%

profile of v3, /device:TPU:4, one launch (start us, length us, event | category | flops | bytes accessed | tf_op | source)
XLA Modules:
  0.0 91.2 jit_solution(14295487321505453420)
XLA Ops:
  0.0 1.6 %collective-permute-start.1 = (bf16[64,4096]{1,0:T(8,128)(2,1)}, bf16[64,4096]{1,0:T(8,128)(2,1)S(1)}, u32[]{:S(2)}, u32[]{:S(2)}) collective-permute-start(bf16[64,4096]{1,0:T(8,128)(2,1)} %refs_0_.1), channel_id=1, source_target_pairs={{0,4},{1,5},{2,6},{3,7},{4,0},{5,1},{6,2},{7,3},{8,12},{9,13},{10,... | collective-permute-start | bytes 1572872 | tf_op jit(solution)/shard_map/ppermute | solution.py:119
  1.6 2.2 %collective-permute-start.2 = (bf16[64,4096]{1,0:T(8,128)(2,1)}, bf16[64,4096]{1,0:T(8,128)(2,1)S(1)}, u32[]{:S(2)}, u32[]{:S(2)}) collective-permute-start(bf16[64,4096]{1,0:T(8,128)(2,1)} %refs_0_.1), channel_id=1, source_target_pairs={{0,12},{1,13},{2,14},{3,15},{4,8},{5,9},{6,10},{7,11},{8,4},{9,5},... | collective-permute-start | bytes 1572872 | tf_op jit(solution)/shard_map/ppermute | solution.py:119
  4.8 3.4 %collective-permute-start = (bf16[48,4096]{1,0:T(8,128)(2,1)S(1)}, bf16[48,4096]{1,0:T(8,128)(2,1)S(1)}, u32[]{:S(2)}, u32[]{:S(2)}) collective-permute-start(bf16[48,4096]{1,0:T(8,128)(2,1)S(1)} %slice_bitcast_fusion), channel_id=1, source_target_pairs={{0,1},{1,0},{2,3},{3,2},{4,5},{5,4},{6,7},{7,6},{8,9},{9,8},{10,11... | collective-permute-start | bytes 1179656 | tf_op jit(solution)/shard_map/ppermute | solution.py:119
  8.2 4.5 %collective-permute-start.5 = (bf16[48,4096]{1,0:T(8,128)(2,1)S(1)}, bf16[48,4096]{1,0:T(8,128)(2,1)S(1)}, u32[]{:S(2)}, u32[]{:S(2)}) collective-permute-start(bf16[48,4096]{1,0:T(8,128)(2,1)S(1)} %slice_bitcast_fusion), channel_id=1, source_target_pairs={{0,3},{1,2},{2,1},{3,0},{4,7},{5,6},{6,5},{7,4},{8,11},{9,10},{10,... | collective-permute-start | bytes 1179656 | tf_op jit(solution)/shard_map/ppermute | solution.py:119
  15.9 1.1 %collective-permute-start.3 = (bf16[64,4096]{1,0:T(8,128)(2,1)S(1)}, bf16[64,4096]{1,0:T(8,128)(2,1)S(1)}, u32[]{:S(2)}, u32[]{:S(2)}) collective-permute-start(bf16[64,4096]{1,0:T(8,128)(2,1)S(1)} %collective-permute-done.1.refs_1_), channel_id=1, source_target_pairs={{0,12},{1,13},{2,14},{3,15},{4,8},{5,9},{6,10},{7,11},{8,4},{9,5},... | collective-permute-start | bytes 1572872 | tf_op jit(solution)/shard_map/ppermute | solution.py:119
  17.1 5.4 %collective-permute-done.refs_1_ = bf16[48,4096]{1,0:T(8,128)(2,1)S(1)} collective-permute-done((bf16[48,4096]{1,0:T(8,128)(2,1)S(1)}, bf16[48,4096]{1,0:T(8,128)(2,1)S(1)}, u32[]{:S(2)}, u32[]{:S(2)}) %collective-permute-start) | collective-permute-done | bytes 393248 | tf_op jit(solution)/shard_map/ppermute | solution.py:119
  22.5 4.5 %collective-permute-done.5.refs_2_ = bf16[48,4096]{1,0:T(8,128)(2,1)S(1)} collective-permute-done((bf16[48,4096]{1,0:T(8,128)(2,1)S(1)}, bf16[48,4096]{1,0:T(8,128)(2,1)S(1)}, u32[]{:S(2)}, u32[]{:S(2)}) %collective-permute-start.5) | collective-permute-done | bytes 393248 | tf_op jit(solution)/shard_map/ppermute | solution.py:119
  27.1 1.8 %collective-permute-start.6 = (bf16[96,4096]{1,0:T(8,128)(2,1)S(1)}, bf16[96,4096]{1,0:T(8,128)(2,1)S(1)}, u32[]{:S(2)}, u32[]{:S(2)}) collective-permute-start(bf16[96,4096]{1,0:T(8,128)(2,1)S(1)} %pad_maximum_fusion.1), channel_id=1, source_target_pairs={{0,4},{1,5},{2,6},{3,7},{4,0},{5,1},{6,2},{7,3},{8,12},{9,13},{10,... | collective-permute-start | bytes 2359304 | tf_op jit(solution)/shard_map/ppermute | solution.py:119
  28.9 4.6 %collective-permute-start.4 = (bf16[48,4096]{1,0:T(8,128)(2,1)S(1)}, bf16[48,4096]{1,0:T(8,128)(2,1)S(1)}, u32[]{:S(2)}, u32[]{:S(2)}) collective-permute-start(bf16[48,4096]{1,0:T(8,128)(2,1)S(1)} %collective-permute-done.refs_1_), channel_id=1, source_target_pairs={{0,3},{1,2},{2,1},{3,0},{4,7},{5,6},{6,5},{7,4},{8,11},{9,10},{10,... | collective-permute-start | bytes 1179656 | tf_op jit(solution)/shard_map/ppermute | solution.py:119
  33.5 1.5 %collective-permute-start.8 = (bf16[64,4096]{1,0:T(8,128)(2,1)S(1)}, bf16[64,4096]{1,0:T(8,128)(2,1)S(1)}, u32[]{:S(2)}, u32[]{:S(2)}) collective-permute-start(bf16[64,4096]{1,0:T(8,128)(2,1)S(1)} %pad_maximum_fusion.3), channel_id=1, source_target_pairs={{0,1},{1,0},{2,3},{3,2},{4,5},{5,4},{6,7},{7,6},{8,9},{9,8},{10,11... | collective-permute-start | bytes 1572872 | tf_op jit(solution)/shard_map/ppermute | solution.py:119
  35.0 2.2 %copy-done.1 = bf16[14,9,128,128]{3,2,1,0:T(8,128)(2,1)S(1)} copy-done((bf16[14,9,128,128]{3,2,1,0:T(8,128)(2,1)S(1)}, bf16[14,9,128,128]{3,2,1,0:T(8,128)(2,1)}, u32[]{:S(2)}) %copy-start.1) | copy-done | bytes 4128792
  37.2 2.2 %copy-done.3 = bf16[14,9,128,128]{3,2,1,0:T(8,128)(2,1)S(1)} copy-done((bf16[14,9,128,128]{3,2,1,0:T(8,128)(2,1)S(1)}, bf16[14,9,128,128]{3,2,1,0:T(8,128)(2,1)}, u32[]{:S(2)}) %copy-start.3) | copy-done | bytes 4128792
  39.4 5.9 %shard_map.64.refs_5_ = bf16[1024,1792]{1,0:T(8,128)(2,1)} custom-call(s32[268]{0:T(512)S(1)} %pad_add_fusion.table_ref, bf16[64,4096]{1,0:T(8,128)(2,1)S(1)} %copy-done, bf16[64,4096]{1,0:T(8,128)(2,1)S(1)} %collective-permute-done.1.refs_1_, bf16[64,4096]{1,0:T(8,128)(2,1)S(1)} %collective-permute-done.2.refs_2_, bf16[14,9,128,128]{3,2,1,0:T(8,128)(2,1)S(1)} %copy-done.1, ...), custom_call_target="tpu_custom_call" | custom-call | flops 6643999744 | bytes 688128 | tf_op jit(solution)/shard_map/pallas_call | solution.py:96
  45.9 5.1 %shard_map.65.refs_5_ = bf16[1024,1792]{1,0:T(8,128)(2,1)} custom-call(s32[268]{0:T(512)S(1)} %pad_add_fusion.table_ref, bf16[64,4096]{1,0:T(8,128)(2,1)S(1)} %collective-permute-done.3.refs_0_, bf16[48,4096]{1,0:T(8,128)(2,1)S(1)} %collective-permute-done.refs_1_, ...), custom_call_target="tpu_custom_call", output_to_operand_aliasing={{}: (6, {})} | custom-call | flops 5939999744 | bytes 573440 | tf_op jit(solution)/shard_map/pallas_call | solution.py:96
  51.0 2.0 %collective-permute-done.4.refs_0_ = bf16[48,4096]{1,0:T(8,128)(2,1)S(1)} collective-permute-done((bf16[48,4096]{1,0:T(8,128)(2,1)S(1)}, bf16[48,4096]{1,0:T(8,128)(2,1)S(1)}, u32[]{:S(2)}, u32[]{:S(2)}) %collective-permute-start.4) | collective-permute-done | bytes 393248 | tf_op jit(solution)/shard_map/ppermute | solution.py:119
  52.9 3.4 %collective-permute-start.10 = (bf16[64,4096]{1,0:T(8,128)(2,1)S(1)}, bf16[64,4096]{1,0:T(8,128)(2,1)S(1)}, u32[]{:S(2)}, u32[]{:S(2)}) collective-permute-start(bf16[64,4096]{1,0:T(8,128)(2,1)S(1)} %pad_maximum_fusion.3), channel_id=1, source_target_pairs={{0,3},{1,2},{2,1},{3,0},{4,7},{5,6},{6,5},{7,4},{8,11},{9,10},{10,... | collective-permute-start | bytes 1572872 | tf_op jit(solution)/shard_map/ppermute | solution.py:119
  57.3 6.1 %shard_map.66.refs_4_ = bf16[1024,1792]{1,0:T(8,128)(2,1)} custom-call(s32[268]{0:T(512)S(1)} %pad_add_fusion.table_ref, bf16[48,4096]{1,0:T(8,128)(2,1)S(1)} %collective-permute-done.4.refs_0_, bf16[96,4096]{1,0:T(8,128)(2,1)S(1)} %collective-permute-done.6.refs_1_, ...), custom_call_target="tpu_custom_call", output_to_operand_aliasing={{}: (6, {})} | custom-call | flops 6995999744 | bytes 745472 | tf_op jit(solution)/shard_map/pallas_call | solution.py:96
  63.5 2.3 %collective-permute-done.7.refs_0_ = bf16[48,4096]{1,0:T(8,128)(2,1)S(1)} collective-permute-done((bf16[48,4096]{1,0:T(8,128)(2,1)S(1)}, bf16[48,4096]{1,0:T(8,128)(2,1)S(1)}, u32[]{:S(2)}, u32[]{:S(2)}) %collective-permute-start.7) | collective-permute-done | bytes 393248 | tf_op jit(solution)/shard_map/ppermute | solution.py:119
  66.6 2.3 %collective-permute-start.9 = (bf16[96,4096]{1,0:T(8,128)(2,1)S(1)}, bf16[96,4096]{1,0:T(8,128)(2,1)S(1)}, u32[]{:S(2)}, u32[]{:S(2)}) collective-permute-start(bf16[96,4096]{1,0:T(8,128)(2,1)S(1)} %pad_maximum_fusion.2), channel_id=1, source_target_pairs={{0,12},{1,13},{2,14},{3,15},{4,8},{5,9},{6,10},{7,11},{8,4},{9,5},... | collective-permute-start | bytes 2359304 | tf_op jit(solution)/shard_map/ppermute | solution.py:119
  68.9 2.4 %collective-permute-done.12.refs_1_ = bf16[192,4096]{1,0:T(8,128)(2,1)S(1)} collective-permute-done((bf16[192,4096]{1,0:T(8,128)(2,1)S(1)}, bf16[192,4096]{1,0:T(8,128)(2,1)S(1)}, u32[]{:S(2)}, u32[]{:S(2)}) %collective-permute-start.12) | collective-permute-done | bytes 1572896 | tf_op jit(solution)/shard_map/ppermute | solution.py:119
  71.4 6.8 %shard_map.67.refs_4_ = bf16[1024,1792]{1,0:T(8,128)(2,1)} custom-call(s32[268]{0:T(512)S(1)} %pad_add_fusion.table_ref, bf16[48,4096]{1,0:T(8,128)(2,1)S(1)} %collective-permute-done.7.refs_0_, bf16[192,4096]{1,0:T(8,128)(2,1)S(1)} %collective-permute-done.12.refs_1_, bf16[14,9,128,128]{3,2,1,0:T(8,128)(2,1)S(1)} %copy-done.2, ...), custom_call_target="tpu_custom_call", output_to_operand_aliasing={{}: (5, {})} | custom-call | flops 7699999744 | bytes 860160 | tf_op jit(solution)/shard_map/pallas_call | solution.py:96
  78.2 4.5 %collective-permute-done.11.refs_1_ = bf16[64,4096]{1,0:T(8,128)(2,1)S(1)} collective-permute-done((bf16[64,4096]{1,0:T(8,128)(2,1)S(1)}, bf16[64,4096]{1,0:T(8,128)(2,1)S(1)}, u32[]{:S(2)}, u32[]{:S(2)}) %collective-permute-start.11) | collective-permute-done | bytes 524320 | tf_op jit(solution)/shard_map/ppermute | solution.py:119
  82.7 4.4 %shard_map.68.refs_3_ = bf16[1024,1792]{1,0:T(8,128)(2,1)} custom-call(s32[268]{0:T(512)S(1)} %pad_add_fusion.table_ref, bf16[64,4096]{1,0:T(8,128)(2,1)S(1)} %collective-permute-done.10.refs_0_, bf16[64,4096]{1,0:T(8,128)(2,1)S(1)} %collective-permute-done.11.refs_1_, bf16[14,9,128,128]{3,2,1,0:T(8,128)(2,1)S(1)} %copy-done.2, ...), custom_call_target="tpu_custom_call", output_to_operand_aliasing={{}: (5, {})} | custom-call | flops 5235999744 | bytes 458752 | tf_op jit(solution)/shard_map/pallas_call | solution.py:96
  87.1 3.9 %shard_map.69 = bf16[1024,1792]{1,0:T(8,128)(2,1)} custom-call(s32[268]{0:T(512)S(1)} %pad_add_fusion.table_ref, bf16[96,4096]{1,0:T(8,128)(2,1)S(1)} %collective-permute-done.9.refs_0_, bf16[14,9,128,128]{3,2,1,0:T(8,128)(2,1)S(1)} %copy-done.2, bf16[14,9,128,128]{3,2,1,0:T(8,128)(2,1)S(1)} %copy-done.4, ...), custom_call_target="tpu_custom_call", output_to_operand_aliasing={{}: (4, {})} | custom-call | flops 4531999744 | bytes 344064 | tf_op jit(solution)/shard_map/pallas_call | solution.py:96
  (31 shorter events, 6.9 us)
Async XLA Ops:
  0.0 35.0 %copy-start = (bf16[64,4096]{1,0:T(8,128)(2,1)S(1)}, bf16[64,4096]{1,0:T(8,128)(2,1)}, u32[]{:S(2)}) copy-start(bf16[64,4096]{1,0:T(8,128)(2,1)} %refs_0_.1) | copy-start | bytes 1572868
  0.0 15.9 %collective-permute-start.1 = (bf16[64,4096]{1,0:T(8,128)(2,1)}, bf16[64,4096]{1,0:T(8,128)(2,1)S(1)}, u32[]{:S(2)}, u32[]{:S(2)}) collective-permute-start(bf16[64,4096]{1,0:T(8,128)(2,1)} %refs_0_.1), channel_id=1, source_target_pairs={{0,4},{1,5},{2,6},{3,7},{4,0},{5,1},{6,2},{7,3},{8,12},{9,13},{10,... | collective-permute-start | bytes 1572872 | tf_op jit(solution)/shard_map/ppermute | solution.py:119
  1.6 15.5 %collective-permute-start.2 = (bf16[64,4096]{1,0:T(8,128)(2,1)}, bf16[64,4096]{1,0:T(8,128)(2,1)S(1)}, u32[]{:S(2)}, u32[]{:S(2)}) collective-permute-start(bf16[64,4096]{1,0:T(8,128)(2,1)} %refs_0_.1), channel_id=1, source_target_pairs={{0,12},{1,13},{2,14},{3,15},{4,8},{5,9},{6,10},{7,11},{8,4},{9,5},... | collective-permute-start | bytes 1572872 | tf_op jit(solution)/shard_map/ppermute | solution.py:119
  4.8 17.7 %collective-permute-start = (bf16[48,4096]{1,0:T(8,128)(2,1)S(1)}, bf16[48,4096]{1,0:T(8,128)(2,1)S(1)}, u32[]{:S(2)}, u32[]{:S(2)}) collective-permute-start(bf16[48,4096]{1,0:T(8,128)(2,1)S(1)} %slice_bitcast_fusion), channel_id=1, source_target_pairs={{0,1},{1,0},{2,3},{3,2},{4,5},{5,4},{6,7},{7,6},{8,9},{9,8},{10,11... | collective-permute-start | bytes 1179656 | tf_op jit(solution)/shard_map/ppermute | solution.py:119
  8.2 18.9 %collective-permute-start.5 = (bf16[48,4096]{1,0:T(8,128)(2,1)S(1)}, bf16[48,4096]{1,0:T(8,128)(2,1)S(1)}, u32[]{:S(2)}, u32[]{:S(2)}) collective-permute-start(bf16[48,4096]{1,0:T(8,128)(2,1)S(1)} %slice_bitcast_fusion), channel_id=1, source_target_pairs={{0,3},{1,2},{2,1},{3,0},{4,7},{5,6},{6,5},{7,4},{8,11},{9,10},{10,... | collective-permute-start | bytes 1179656 | tf_op jit(solution)/shard_map/ppermute | solution.py:119
  15.9 11.2 %collective-permute-start.3 = (bf16[64,4096]{1,0:T(8,128)(2,1)S(1)}, bf16[64,4096]{1,0:T(8,128)(2,1)S(1)}, u32[]{:S(2)}, u32[]{:S(2)}) collective-permute-start(bf16[64,4096]{1,0:T(8,128)(2,1)S(1)} %collective-permute-done.1.refs_1_), channel_id=1, source_target_pairs={{0,12},{1,13},{2,14},{3,15},{4,8},{5,9},{6,10},{7,11},{8,4},{9,5},... | collective-permute-start | bytes 1572872 | tf_op jit(solution)/shard_map/ppermute | solution.py:119
  27.1 18.1 %collective-permute-start.6 = (bf16[96,4096]{1,0:T(8,128)(2,1)S(1)}, bf16[96,4096]{1,0:T(8,128)(2,1)S(1)}, u32[]{:S(2)}, u32[]{:S(2)}) collective-permute-start(bf16[96,4096]{1,0:T(8,128)(2,1)S(1)} %pad_maximum_fusion.1), channel_id=1, source_target_pairs={{0,4},{1,5},{2,6},{3,7},{4,0},{5,1},{6,2},{7,3},{8,12},{9,13},{10,... | collective-permute-start | bytes 2359304 | tf_op jit(solution)/shard_map/ppermute | solution.py:119
  28.9 24.0 %collective-permute-start.4 = (bf16[48,4096]{1,0:T(8,128)(2,1)S(1)}, bf16[48,4096]{1,0:T(8,128)(2,1)S(1)}, u32[]{:S(2)}, u32[]{:S(2)}) collective-permute-start(bf16[48,4096]{1,0:T(8,128)(2,1)S(1)} %collective-permute-done.refs_1_), channel_id=1, source_target_pairs={{0,3},{1,2},{2,1},{3,0},{4,7},{5,6},{6,5},{7,4},{8,11},{9,10},{10,... | collective-permute-start | bytes 1179656 | tf_op jit(solution)/shard_map/ppermute | solution.py:119
  33.5 23.8 %collective-permute-start.8 = (bf16[64,4096]{1,0:T(8,128)(2,1)S(1)}, bf16[64,4096]{1,0:T(8,128)(2,1)S(1)}, u32[]{:S(2)}, u32[]{:S(2)}) collective-permute-start(bf16[64,4096]{1,0:T(8,128)(2,1)S(1)} %pad_maximum_fusion.3), channel_id=1, source_target_pairs={{0,1},{1,0},{2,3},{3,2},{4,5},{5,4},{6,7},{7,6},{8,9},{9,8},{10,11... | collective-permute-start | bytes 1572872 | tf_op jit(solution)/shard_map/ppermute | solution.py:119
  35.0 2.2 %copy-start.1 = (bf16[14,9,128,128]{3,2,1,0:T(8,128)(2,1)S(1)}, bf16[14,9,128,128]{3,2,1,0:T(8,128)(2,1)}, u32[]{:S(2)}) copy-start(bf16[14,9,128,128]{3,2,1,0:T(8,128)(2,1)} %refs_1_.1) | copy-start | bytes 12386308
  37.2 2.2 %copy-start.3 = (bf16[14,9,128,128]{3,2,1,0:T(8,128)(2,1)S(1)}, bf16[14,9,128,128]{3,2,1,0:T(8,128)(2,1)}, u32[]{:S(2)}) copy-start(bf16[14,9,128,128]{3,2,1,0:T(8,128)(2,1)} %refs_2_.5) | copy-start | bytes 12386308
  39.4 6.5 %copy-start.2 = (bf16[14,9,128,128]{3,2,1,0:T(8,128)(2,1)S(1)}, bf16[14,9,128,128]{3,2,1,0:T(8,128)(2,1)}, u32[]{:S(2)}) copy-start(bf16[14,9,128,128]{3,2,1,0:T(8,128)(2,1)} %refs_1_.1) | copy-start | bytes 12386308
  39.4 6.5 %copy-start.4 = (bf16[14,9,128,128]{3,2,1,0:T(8,128)(2,1)S(1)}, bf16[14,9,128,128]{3,2,1,0:T(8,128)(2,1)}, u32[]{:S(2)}) copy-start(bf16[14,9,128,128]{3,2,1,0:T(8,128)(2,1)} %refs_2_.5) | copy-start | bytes 12386308
  45.4 25.9 %collective-permute-start.12 = (bf16[192,4096]{1,0:T(8,128)(2,1)S(1)}, bf16[192,4096]{1,0:T(8,128)(2,1)S(1)}, u32[]{:S(2)}, u32[]{:S(2)}) collective-permute-start(bf16[192,4096]{1,0:T(8,128)(2,1)S(1)} %pad_maximum_fusion), channel_id=1, source_target_pairs={{0,12},{1,13},{2,14},{3,15},{4,8},{5,9},{6,10},{7,11},{8,4},{9,5},... | collective-permute-start | bytes 4718600 | tf_op jit(solution)/shard_map/ppermute | solution.py:119
  52.9 25.3 %collective-permute-start.10 = (bf16[64,4096]{1,0:T(8,128)(2,1)S(1)}, bf16[64,4096]{1,0:T(8,128)(2,1)S(1)}, u32[]{:S(2)}, u32[]{:S(2)}) collective-permute-start(bf16[64,4096]{1,0:T(8,128)(2,1)S(1)} %pad_maximum_fusion.3), channel_id=1, source_target_pairs={{0,3},{1,2},{2,1},{3,0},{4,7},{5,6},{6,5},{7,4},{8,11},{9,10},{10,... | collective-permute-start | bytes 1572872 | tf_op jit(solution)/shard_map/ppermute | solution.py:119
  56.3 9.5 %collective-permute-start.7 = (bf16[48,4096]{1,0:T(8,128)(2,1)S(1)}, bf16[48,4096]{1,0:T(8,128)(2,1)S(1)}, u32[]{:S(2)}, u32[]{:S(2)}) collective-permute-start(bf16[48,4096]{1,0:T(8,128)(2,1)S(1)} %collective-permute-done.4.refs_0_), channel_id=1, source_target_pairs={{0,4},{1,5},{2,6},{3,7},{4,0},{5,1},{6,2},{7,3},{8,12},{9,13},{10,... | collective-permute-start | bytes 1179656 | tf_op jit(solution)/shard_map/ppermute | solution.py:119
  65.8 16.9 %collective-permute-start.11 = (bf16[64,4096]{1,0:T(8,128)(2,1)S(1)}, bf16[64,4096]{1,0:T(8,128)(2,1)S(1)}, u32[]{:S(2)}, u32[]{:S(2)}) collective-permute-start(bf16[64,4096]{1,0:T(8,128)(2,1)S(1)} %collective-permute-done.8.refs_2_), channel_id=1, source_target_pairs={{0,3},{1,2},{2,1},{3,0},{4,7},{5,6},{6,5},{7,4},{8,11},{9,10},{10,... | collective-permute-start | bytes 1572872 | tf_op jit(solution)/shard_map/ppermute | solution.py:119
  66.6 20.5 %collective-permute-start.9 = (bf16[96,4096]{1,0:T(8,128)(2,1)S(1)}, bf16[96,4096]{1,0:T(8,128)(2,1)S(1)}, u32[]{:S(2)}, u32[]{:S(2)}) collective-permute-start(bf16[96,4096]{1,0:T(8,128)(2,1)S(1)} %pad_maximum_fusion.2), channel_id=1, source_target_pairs={{0,12},{1,13},{2,14},{3,15},{4,8},{5,9},{6,10},{7,11},{8,4},{9,5},... | collective-permute-start | bytes 2359304 | tf_op jit(solution)/shard_map/ppermute | solution.py:119

commit v4 on v3

--- a/solution.py
+++ b/solution.py
@@ -13,7 +13,7 @@
 AXES = ("dp", "tensor")
 TURNED = 16
 UNROLL = 7
-COST = 22_000_000
+COST = 30_000_000
 
 
 STEPS = {("y", 0): 1, ("y", 1): 2, ("z", 0): 4, ("z", 1): 8}
@@ -44,6 +44,21 @@
 def after(piece, *others):
     rows, *_ = lax.optimization_barrier((piece.rows, *[getattr(o, "rows", o) for o in others]))
     return Piece(rows, piece.codes, piece.size, piece.offset)
+
+
+def met_kernel(table_ref, *refs):
+    refs[-1][...] = table_ref[...]
+
+
+def met(table, *arrays):
+    vmem = pl.BlockSpec(memory_space=pltpu.VMEM)
+    return pl.pallas_call(
+        met_kernel,
+        out_shape=jax.ShapeDtypeStruct(table.shape, table.dtype),
+        in_specs=[vmem] * (1 + len(arrays)),
+        out_specs=vmem,
+        compiler_params=pltpu.CompilerParams(vmem_limit_bytes=1 << 20),
+    )(table, *arrays)
 
 
 def project_kernel(layout, starts, n_prev, table_ref, *refs):
@@ -124,31 +139,34 @@
         masks = jnp.asarray(np.array([[mask(core, code) for code in range(members)] for core in range(2)], np.int32))
         core, me = lax.axis_index("dp") % 2, lax.axis_index("tensor")
         table = jnp.concatenate([(masks[core] ^ me) * local, gate_rows.reshape(-1), up_rows.reshape(-1)])
+        table = met(table, gate_blocks, up_blocks)
         starts = (members, members + gate_rows.size)
         run = lambda pieces, result: project(
-            pieces, members * local, table, starts, (gate_blocks, up_blocks), result
+            pieces, members * local, table, starts, blocks, result
         )
 
         own = Piece(tokens, [0], local, 0)
         mine = own.part(TURNED, local - TURNED)
+        blocks = (gate_blocks, up_blocks)
         y1 = swap(own, "y", 0)
-        y2 = swap(own, "y", 1)
         z1 = swap(mine, "z", 0)
         z2 = swap(mine, "z", 1)
-        y3 = swap(y1, "y", 1)
-        z1, z2 = after(z1, y1, y2), after(z2, y1, y2)
-        z3 = swap(after(z1, y3), "z", 1)
+        y2 = swap(after(own, mine), "y", 1)
+        y3 = swap(after(y1, table), "y", 1)
+        z1, z2 = after(z1, y1), after(z2, y1)
+        z3 = swap(z1, "z", 1)
         pair = joined(z1, z2)
         p1 = swap(after(pair, y3), "y", 0)
         column = joined(*[p.part(0, TURNED) for p in (own, y1, y2, y3)])
         b1 = swap(column, "z", 0)
+        result = run([own, y1], None)
+        result = run([after(y2, p1), y3, z1, z2], result)
         p2 = swap(joined(pair, p1), "y", 1)
-        q1 = swap(after(z3, p1), "y", 0)
-        b2 = swap(after(column, z3), "z", 1)
+        q1 = swap(after(z3, p1, result), "y", 0)
+        b2 = swap(after(column, z3, result), "z", 1)
         b3 = swap(after(b1, q1), "z", 1)
         q2 = swap(after(joined(z3, q1), b1), "y", 1)
-        result = None
-        for pieces in ([own, y1, after(y2, y3)], [y3, z1, z2], [z3, p1, b1], [q1, p2], [b2, b3], [q2]):
+        for pieces in ([z3, p1, b1], [q1, p2], [b2, q2], [b3]):
             result = run(pieces, result)
         return result
 

time: 91.5 us -> 90.6 us (level)
  starting transfers between devices: 28.5 us -> 26.9 us
    ppermute x13, starting transfers between devices: 28.5 us -> 26.9 us  [swap(): rows = lax.ppermute(piece.rows, AXES, pairs)]
  transfers between devices with their start and end apart: 13 -> 13, of which waited for: 6 -> 5; matrix products, arithmetic and copies ran while one was open for 5% -> 5% of each run, Pallas kernels for 31% -> 32%
where the time goes in v4:
time: 90.6 us; the launch traced here: 90.3 us
  Pallas kernels  32.4 us (36%)
  starting transfers between devices  26.9 us (30%)
  waiting for transfers between devices  21.7 us (24%)
  local copies, waits for them, and re-layouts  7.94 us (9%)
  other arithmetic  1.07 us (1%)
    pallas_call x6, Pallas kernels, project(): pl.pallas_call(functools.partial(project_kernel, layout, starts, len(prev...  32.4 us
    ppermute x13, starting transfers between devices, swap(): rows = lax.ppermute(piece.rows, AXES, pairs)  26.9 us
    ppermute x13, waiting for transfers between devices, swap(): rows = lax.ppermute(piece.rows, AXES, pairs)  21.7 us
    unnamed x10, local copies, waits for them, and re-layouts  4.35 us
    reshape x5, local copies, waits for them, and re-layouts, part(): rows.reshape(len(self.codes) * size, -1)  2.03 us
  transfers between devices with their start and end apart: 13, of which 5 were waited for; matrix products, arithmetic and copies ran while one was open for 5% of the time, Pallas kernels for 32%

profile of v4, /device:TPU:4, one launch (start us, length us, event | category | flops | bytes accessed | tf_op | source)
XLA Modules:
  0.0 90.3 jit_solution(1980700860798188973)
XLA Ops:
  0.0 1.6 %collective-permute-start = (bf16[64,4096]{1,0:T(8,128)(2,1)}, bf16[64,4096]{1,0:T(8,128)(2,1)S(1)}, u32[]{:S(2)}, u32[]{:S(2)}) collective-permute-start(bf16[64,4096]{1,0:T(8,128)(2,1)} %refs_0_.3), channel_id=1, source_target_pairs={{0,4},{1,5},{2,6},{3,7},{4,0},{5,1},{6,2},{7,3},{8,12},{9,13},{10,... | collective-permute-start | bytes 1572872 | tf_op jit(solution)/shard_map/ppermute | solution.py:134
  1.6 1.1 %slice_bitcast_fusion = bf16[48,4096]{1,0:T(8,128)(2,1)S(1)} fusion(bf16[1,64,4096]{2,1,0:T(8,128)(2,1)} %bitcast.16), kind=kLoop, calls=%fused_computation.4 | loop fusion | bytes 786432 | tf_op jit(solution)/shard_map/reshape | solution.py:36
  2.6 3.4 %collective-permute-start.4 = (bf16[48,4096]{1,0:T(8,128)(2,1)S(1)}, bf16[48,4096]{1,0:T(8,128)(2,1)S(1)}, u32[]{:S(2)}, u32[]{:S(2)}) collective-permute-start(bf16[48,4096]{1,0:T(8,128)(2,1)S(1)} %slice_bitcast_fusion), channel_id=1, source_target_pairs={{0,1},{1,0},{2,3},{3,2},{4,5},{5,4},{6,7},{7,6},{8,9},{9,8},{10,11... | collective-permute-start | bytes 1179656 | tf_op jit(solution)/shard_map/ppermute | solution.py:134
  6.0 4.5 %collective-permute-start.6 = (bf16[48,4096]{1,0:T(8,128)(2,1)S(1)}, bf16[48,4096]{1,0:T(8,128)(2,1)S(1)}, u32[]{:S(2)}, u32[]{:S(2)}) collective-permute-start(bf16[48,4096]{1,0:T(8,128)(2,1)S(1)} %slice_bitcast_fusion), channel_id=1, source_target_pairs={{0,3},{1,2},{2,1},{3,0},{4,7},{5,6},{6,5},{7,4},{8,11},{9,10},{10,... | collective-permute-start | bytes 1179656 | tf_op jit(solution)/shard_map/ppermute | solution.py:134
  10.5 2.2 %collective-permute-start.1 = (bf16[64,4096]{1,0:T(8,128)(2,1)}, bf16[64,4096]{1,0:T(8,128)(2,1)S(1)}, u32[]{:S(2)}, u32[]{:S(2)}) collective-permute-start(bf16[64,4096]{1,0:T(8,128)(2,1)} %refs_0_.3), channel_id=1, source_target_pairs={{0,12},{1,13},{2,14},{3,15},{4,8},{5,9},{6,10},{7,11},{8,4},{9,5},... | collective-permute-start | bytes 1572872 | tf_op jit(solution)/shard_map/ppermute | solution.py:134
  12.7 0.9 %slice_bitcast_fusion.4 = bf16[16,4096]{1,0:T(8,128)(2,1)S(1)} fusion(bf16[1,64,4096]{2,1,0:T(8,128)(2,1)} %bitcast.17), kind=kLoop, calls=%fused_computation.8 | loop fusion | bytes 262144 | tf_op jit(solution)/shard_map/reshape | solution.py:36
  13.6 0.8 reshape.38
  14.4 0.8 reshape.39
  16.0 2.2 %copy-done = bf16[14,9,128,128]{3,2,1,0:T(8,128)(2,1)S(1)} copy-done((bf16[14,9,128,128]{3,2,1,0:T(8,128)(2,1)S(1)}, bf16[14,9,128,128]{3,2,1,0:T(8,128)(2,1)}, u32[]{:S(2)}) %copy-start) | copy-done | bytes 4128792
  18.1 2.2 %copy-done.2 = bf16[14,9,128,128]{3,2,1,0:T(8,128)(2,1)S(1)} copy-done((bf16[14,9,128,128]{3,2,1,0:T(8,128)(2,1)S(1)}, bf16[14,9,128,128]{3,2,1,0:T(8,128)(2,1)}, u32[]{:S(2)}) %copy-start.2) | copy-done | bytes 4128792
  20.3 1.1 %collective-permute-start.2 = (bf16[64,4096]{1,0:T(8,128)(2,1)S(1)}, bf16[64,4096]{1,0:T(8,128)(2,1)S(1)}, u32[]{:S(2)}, u32[]{:S(2)}) collective-permute-start(bf16[64,4096]{1,0:T(8,128)(2,1)S(1)} %collective-permute-done.refs_1_), channel_id=1, source_target_pairs={{0,12},{1,13},{2,14},{3,15},{4,8},{5,9},{6,10},{7,11},{8,4},{9,5},... | collective-permute-start | bytes 1572872 | tf_op jit(solution)/shard_map/ppermute | solution.py:134
  22.1 8.2 %collective-permute-start.5 = (bf16[48,4096]{1,0:T(8,128)(2,1)S(1)}, bf16[48,4096]{1,0:T(8,128)(2,1)S(1)}, u32[]{:S(2)}, u32[]{:S(2)}) collective-permute-start(bf16[48,4096]{1,0:T(8,128)(2,1)S(1)} %collective-permute-done.4.refs_2_), channel_id=1, source_target_pairs={{0,3},{1,2},{2,1},{3,0},{4,7},{5,6},{6,5},{7,4},{8,11},{9,10},{10,... | collective-permute-start | bytes 1179656 | tf_op jit(solution)/shard_map/ppermute | solution.py:134
  30.4 4.4 %shard_map.65.refs_6_ = bf16[1024,1792]{1,0:T(8,128)(2,1)} custom-call(s32[268]{0:T(512)S(1)} %shard_map.64.table_ref, bf16[64,4096]{1,0:T(8,128)(2,1)S(1)} %copy-done.4, bf16[64,4096]{1,0:T(8,128)(2,1)S(1)} %collective-permute-done.refs_1_, bf16[14,9,128,128]{3,2,1,0:T(8,128)(2,1)S(1)} %copy-done.1, bf16[14,9,128,128]{3,2,1,0:T(8,128)(2,1)S(1)} %copy-done.3), custom_call_target="tpu_custom_call" | custom-call | flops 7139999744 | bytes 458752 | tf_op jit(solution)/shard_map/pallas_call | solution.py:111
  35.4 1.5 %collective-permute-start.3 = (bf16[64,4096]{1,0:T(8,128)(2,1)S(1)}, bf16[64,4096]{1,0:T(8,128)(2,1)S(1)}, u32[]{:S(2)}, u32[]{:S(2)}) collective-permute-start(bf16[64,4096]{1,0:T(8,128)(2,1)S(1)} %pad_maximum_fusion.3), channel_id=1, source_target_pairs={{0,1},{1,0},{2,3},{3,2},{4,5},{5,4},{6,7},{7,6},{8,9},{9,8},{10,11... | collective-permute-start | bytes 1572872 | tf_op jit(solution)/shard_map/ppermute | solution.py:134
  36.9 10.1 %collective-permute-done.7.refs_1_ = bf16[96,4096]{1,0:T(8,128)(2,1)S(1)} collective-permute-done((bf16[96,4096]{1,0:T(8,128)(2,1)S(1)}, bf16[96,4096]{1,0:T(8,128)(2,1)S(1)}, u32[]{:S(2)}, u32[]{:S(2)}) %collective-permute-start.7) | collective-permute-done | bytes 786464 | tf_op jit(solution)/shard_map/ppermute | solution.py:134
  47.2 6.3 %shard_map.66.refs_5_ = bf16[1024,1792]{1,0:T(8,128)(2,1)} custom-call(s32[268]{0:T(512)S(1)} %shard_map.64.table_ref, bf16[64,4096]{1,0:T(8,128)(2,1)S(1)} %collective-permute-done.1.refs_0_, bf16[64,4096]{1,0:T(8,128)(2,1)S(1)} %collective-permute-done.2.refs_1_, ...), custom_call_target="tpu_custom_call", output_to_operand_aliasing={{}: (7, {})} | custom-call | flops 10019999744 | bytes 802816 | tf_op jit(solution)/shard_map/pallas_call | solution.py:111
  54.1 6.1 %shard_map.67.refs_4_ = bf16[1024,1792]{1,0:T(8,128)(2,1)} custom-call(s32[268]{0:T(512)S(1)} %shard_map.64.table_ref, bf16[48,4096]{1,0:T(8,128)(2,1)S(1)} %collective-permute-done.5.refs_0_, bf16[96,4096]{1,0:T(8,128)(2,1)S(1)} %collective-permute-done.7.refs_1_, ...), custom_call_target="tpu_custom_call", output_to_operand_aliasing={{}: (6, {})} | custom-call | flops 9539999744 | bytes 745472 | tf_op jit(solution)/shard_map/pallas_call | solution.py:111
  60.2 5.5 %collective-permute-done.8.refs_0_ = bf16[48,4096]{1,0:T(8,128)(2,1)S(1)} collective-permute-done((bf16[48,4096]{1,0:T(8,128)(2,1)S(1)}, bf16[48,4096]{1,0:T(8,128)(2,1)S(1)}, u32[]{:S(2)}, u32[]{:S(2)}) %collective-permute-start.8) | collective-permute-done | bytes 393248 | tf_op jit(solution)/shard_map/ppermute | solution.py:134
  65.8 3.4 %collective-permute-start.11 = (bf16[96,4096]{1,0:T(8,128)(2,1)S(1)}, bf16[96,4096]{1,0:T(8,128)(2,1)S(1)}, u32[]{:S(2)}, u32[]{:S(2)}) collective-permute-start(bf16[96,4096]{1,0:T(8,128)(2,1)S(1)} %pad_maximum_fusion.2), channel_id=1, source_target_pairs={{0,12},{1,13},{2,14},{3,15},{4,8},{5,9},{6,10},{7,11},{8,4},{9,5},... | collective-permute-start | bytes 2359304 | tf_op jit(solution)/shard_map/ppermute | solution.py:134
  69.1 3.9 %collective-permute-done.12.refs_1_ = bf16[192,4096]{1,0:T(8,128)(2,1)S(1)} collective-permute-done((bf16[192,4096]{1,0:T(8,128)(2,1)S(1)}, bf16[192,4096]{1,0:T(8,128)(2,1)S(1)}, u32[]{:S(2)}, u32[]{:S(2)}) %collective-permute-start.12) | collective-permute-done | bytes 1572896 | tf_op jit(solution)/shard_map/ppermute | solution.py:134
  73.0 6.9 %shard_map.68.refs_4_ = bf16[1024,1792]{1,0:T(8,128)(2,1)} custom-call(s32[268]{0:T(512)S(1)} %shard_map.64.table_ref, bf16[48,4096]{1,0:T(8,128)(2,1)S(1)} %collective-permute-done.8.refs_0_, bf16[192,4096]{1,0:T(8,128)(2,1)S(1)} %collective-permute-done.12.refs_1_, bf16[14,9,128,128]{3,2,1,0:T(8,128)(2,1)S(1)} %copy-done.1, ...), custom_call_target="tpu_custom_call", output_to_operand_aliasing={{}: (5, {})} | custom-call | flops 10499999744 | bytes 860160 | tf_op jit(solution)/shard_map/pallas_call | solution.py:111
  79.9 1.5 %collective-permute-done.11.refs_1_ = bf16[96,4096]{1,0:T(8,128)(2,1)S(1)} collective-permute-done((bf16[96,4096]{1,0:T(8,128)(2,1)S(1)}, bf16[96,4096]{1,0:T(8,128)(2,1)S(1)}, u32[]{:S(2)}, u32[]{:S(2)}) %collective-permute-start.11) | collective-permute-done | bytes 786464 | tf_op jit(solution)/shard_map/ppermute | solution.py:134
  81.5 5.2 %shard_map.69.refs_3_ = bf16[1024,1792]{1,0:T(8,128)(2,1)} custom-call(s32[268]{0:T(512)S(1)} %shard_map.64.table_ref, bf16[64,4096]{1,0:T(8,128)(2,1)S(1)} %collective-permute-done.10.refs_0_, bf16[96,4096]{1,0:T(8,128)(2,1)S(1)} %collective-permute-done.11.refs_1_, bf16[14,9,128,128]{3,2,1,0:T(8,128)(2,1)S(1)} %copy-done.1, ...), custom_call_target="tpu_custom_call", output_to_operand_aliasing={{}: (5, {})} | custom-call | flops 8099999744 | bytes 573440 | tf_op jit(solution)/shard_map/pallas_call | solution.py:111
  86.7 3.5 %shard_map.70 = bf16[1024,1792]{1,0:T(8,128)(2,1)} custom-call(s32[268]{0:T(512)S(1)} %shard_map.64.table_ref, bf16[64,4096]{1,0:T(8,128)(2,1)S(1)} %collective-permute-done.9.refs_0_, bf16[14,9,128,128]{3,2,1,0:T(8,128)(2,1)S(1)} %copy-done.1, bf16[14,9,128,128]{3,2,1,0:T(8,128)(2,1)S(1)} %copy-done.3, ...), custom_call_target="tpu_custom_call", output_to_operand_aliasing={{}: (4, {})} | custom-call | flops 5219999744 | bytes 229376 | tf_op jit(solution)/shard_map/pallas_call | solution.py:111
  (32 shorter events, 2.8 us)
Async XLA Ops:
  0.0 20.3 %collective-permute-start = (bf16[64,4096]{1,0:T(8,128)(2,1)}, bf16[64,4096]{1,0:T(8,128)(2,1)S(1)}, u32[]{:S(2)}, u32[]{:S(2)}) collective-permute-start(bf16[64,4096]{1,0:T(8,128)(2,1)} %refs_0_.3), channel_id=1, source_target_pairs={{0,4},{1,5},{2,6},{3,7},{4,0},{5,1},{6,2},{7,3},{8,12},{9,13},{10,... | collective-permute-start | bytes 1572872 | tf_op jit(solution)/shard_map/ppermute | solution.py:134
  2.6 19.5 %collective-permute-start.4 = (bf16[48,4096]{1,0:T(8,128)(2,1)S(1)}, bf16[48,4096]{1,0:T(8,128)(2,1)S(1)}, u32[]{:S(2)}, u32[]{:S(2)}) collective-permute-start(bf16[48,4096]{1,0:T(8,128)(2,1)S(1)} %slice_bitcast_fusion), channel_id=1, source_target_pairs={{0,1},{1,0},{2,3},{3,2},{4,5},{5,4},{6,7},{7,6},{8,9},{9,8},{10,11... | collective-permute-start | bytes 1179656 | tf_op jit(solution)/shard_map/ppermute | solution.py:134
  6.0 28.8 %collective-permute-start.6 = (bf16[48,4096]{1,0:T(8,128)(2,1)S(1)}, bf16[48,4096]{1,0:T(8,128)(2,1)S(1)}, u32[]{:S(2)}, u32[]{:S(2)}) collective-permute-start(bf16[48,4096]{1,0:T(8,128)(2,1)S(1)} %slice_bitcast_fusion), channel_id=1, source_target_pairs={{0,3},{1,2},{2,1},{3,0},{4,7},{5,6},{6,5},{7,4},{8,11},{9,10},{10,... | collective-permute-start | bytes 1179656 | tf_op jit(solution)/shard_map/ppermute | solution.py:134
  10.5 11.6 %collective-permute-start.1 = (bf16[64,4096]{1,0:T(8,128)(2,1)}, bf16[64,4096]{1,0:T(8,128)(2,1)S(1)}, u32[]{:S(2)}, u32[]{:S(2)}) collective-permute-start(bf16[64,4096]{1,0:T(8,128)(2,1)} %refs_0_.3), channel_id=1, source_target_pairs={{0,12},{1,13},{2,14},{3,15},{4,8},{5,9},{6,10},{7,11},{8,4},{9,5},... | collective-permute-start | bytes 1572872 | tf_op jit(solution)/shard_map/ppermute | solution.py:134
  16.0 2.2 %copy-start = (bf16[14,9,128,128]{3,2,1,0:T(8,128)(2,1)S(1)}, bf16[14,9,128,128]{3,2,1,0:T(8,128)(2,1)}, u32[]{:S(2)}) copy-start(bf16[14,9,128,128]{3,2,1,0:T(8,128)(2,1)} %refs_1_.3) | copy-start | bytes 12386308
  18.1 2.2 %copy-start.2 = (bf16[14,9,128,128]{3,2,1,0:T(8,128)(2,1)S(1)}, bf16[14,9,128,128]{3,2,1,0:T(8,128)(2,1)}, u32[]{:S(2)}) copy-start(bf16[14,9,128,128]{3,2,1,0:T(8,128)(2,1)} %refs_2_.7) | copy-start | bytes 12386308
  20.3 10.1 %copy-start.1 = (bf16[14,9,128,128]{3,2,1,0:T(8,128)(2,1)S(1)}, bf16[14,9,128,128]{3,2,1,0:T(8,128)(2,1)}, u32[]{:S(2)}) copy-start(bf16[14,9,128,128]{3,2,1,0:T(8,128)(2,1)} %refs_1_.3) | copy-start | bytes 12386308
  20.3 10.1 %copy-start.3 = (bf16[14,9,128,128]{3,2,1,0:T(8,128)(2,1)S(1)}, bf16[14,9,128,128]{3,2,1,0:T(8,128)(2,1)}, u32[]{:S(2)}) copy-start(bf16[14,9,128,128]{3,2,1,0:T(8,128)(2,1)} %refs_2_.7) | copy-start | bytes 12386308
  20.3 10.1 %copy-start.4 = (bf16[64,4096]{1,0:T(8,128)(2,1)S(1)}, bf16[64,4096]{1,0:T(8,128)(2,1)}, u32[]{:S(2)}) copy-start(bf16[64,4096]{1,0:T(8,128)(2,1)} %refs_0_.3) | copy-start | bytes 1572868
  20.3 14.6 %collective-permute-start.2 = (bf16[64,4096]{1,0:T(8,128)(2,1)S(1)}, bf16[64,4096]{1,0:T(8,128)(2,1)S(1)}, u32[]{:S(2)}, u32[]{:S(2)}) collective-permute-start(bf16[64,4096]{1,0:T(8,128)(2,1)S(1)} %collective-permute-done.refs_1_), channel_id=1, source_target_pairs={{0,12},{1,13},{2,14},{3,15},{4,8},{5,9},{6,10},{7,11},{8,4},{9,5},... | collective-permute-start | bytes 1572872 | tf_op jit(solution)/shard_map/ppermute | solution.py:134
  22.1 31.4 %collective-permute-start.5 = (bf16[48,4096]{1,0:T(8,128)(2,1)S(1)}, bf16[48,4096]{1,0:T(8,128)(2,1)S(1)}, u32[]{:S(2)}, u32[]{:S(2)}) collective-permute-start(bf16[48,4096]{1,0:T(8,128)(2,1)S(1)} %collective-permute-done.4.refs_2_), channel_id=1, source_target_pairs={{0,3},{1,2},{2,1},{3,0},{4,7},{5,6},{6,5},{7,4},{8,11},{9,10},{10,... | collective-permute-start | bytes 1179656 | tf_op jit(solution)/shard_map/ppermute | solution.py:134
  34.9 12.1 %collective-permute-start.7 = (bf16[96,4096]{1,0:T(8,128)(2,1)S(1)}, bf16[96,4096]{1,0:T(8,128)(2,1)S(1)}, u32[]{:S(2)}, u32[]{:S(2)}) collective-permute-start(bf16[96,4096]{1,0:T(8,128)(2,1)S(1)} %pad_maximum_fusion.1), channel_id=1, source_target_pairs={{0,4},{1,5},{2,6},{3,7},{4,0},{5,1},{6,2},{7,3},{8,12},{9,13},{10,... | collective-permute-start | bytes 2359304 | tf_op jit(solution)/shard_map/ppermute | solution.py:134
  35.4 18.7 %collective-permute-start.3 = (bf16[64,4096]{1,0:T(8,128)(2,1)S(1)}, bf16[64,4096]{1,0:T(8,128)(2,1)S(1)}, u32[]{:S(2)}, u32[]{:S(2)}) collective-permute-start(bf16[64,4096]{1,0:T(8,128)(2,1)S(1)} %pad_maximum_fusion.3), channel_id=1, source_target_pairs={{0,1},{1,0},{2,3},{3,2},{4,5},{5,4},{6,7},{7,6},{8,9},{9,8},{10,11... | collective-permute-start | bytes 1572872 | tf_op jit(solution)/shard_map/ppermute | solution.py:134
  47.1 25.9 %collective-permute-start.12 = (bf16[192,4096]{1,0:T(8,128)(2,1)S(1)}, bf16[192,4096]{1,0:T(8,128)(2,1)S(1)}, u32[]{:S(2)}, u32[]{:S(2)}) collective-permute-start(bf16[192,4096]{1,0:T(8,128)(2,1)S(1)} %pad_maximum_fusion), channel_id=1, source_target_pairs={{0,12},{1,13},{2,14},{3,15},{4,8},{5,9},{6,10},{7,11},{8,4},{9,5},... | collective-permute-start | bytes 4718600 | tf_op jit(solution)/shard_map/ppermute | solution.py:134
  53.6 12.1 %collective-permute-start.8 = (bf16[48,4096]{1,0:T(8,128)(2,1)S(1)}, bf16[48,4096]{1,0:T(8,128)(2,1)S(1)}, u32[]{:S(2)}, u32[]{:S(2)}) collective-permute-start(bf16[48,4096]{1,0:T(8,128)(2,1)S(1)} %collective-permute-done.5.refs_0_), channel_id=1, source_target_pairs={{0,4},{1,5},{2,6},{3,7},{4,0},{5,1},{6,2},{7,3},{8,12},{9,13},{10,... | collective-permute-start | bytes 1179656 | tf_op jit(solution)/shard_map/ppermute | solution.py:134
  54.0 25.9 %collective-permute-start.10 = (bf16[64,4096]{1,0:T(8,128)(2,1)S(1)}, bf16[64,4096]{1,0:T(8,128)(2,1)S(1)}, u32[]{:S(2)}, u32[]{:S(2)}) collective-permute-start(bf16[64,4096]{1,0:T(8,128)(2,1)S(1)} %pad_maximum_fusion.3), channel_id=1, source_target_pairs={{0,3},{1,2},{2,1},{3,0},{4,7},{5,6},{6,5},{7,4},{8,11},{9,10},{10,... | collective-permute-start | bytes 1572872 | tf_op jit(solution)/shard_map/ppermute | solution.py:134
  65.8 15.7 %collective-permute-start.11 = (bf16[96,4096]{1,0:T(8,128)(2,1)S(1)}, bf16[96,4096]{1,0:T(8,128)(2,1)S(1)}, u32[]{:S(2)}, u32[]{:S(2)}) collective-permute-start(bf16[96,4096]{1,0:T(8,128)(2,1)S(1)} %pad_maximum_fusion.2), channel_id=1, source_target_pairs={{0,12},{1,13},{2,14},{3,15},{4,8},{5,9},{6,10},{7,11},{8,4},{9,5},... | collective-permute-start | bytes 2359304 | tf_op jit(solution)/shard_map/ppermute | solution.py:134
  69.1 17.5 %collective-permute-start.9 = (bf16[64,4096]{1,0:T(8,128)(2,1)S(1)}, bf16[64,4096]{1,0:T(8,128)(2,1)S(1)}, u32[]{:S(2)}, u32[]{:S(2)}) collective-permute-start(bf16[64,4096]{1,0:T(8,128)(2,1)S(1)} %collective-permute-done.3.refs_2_), channel_id=1, source_target_pairs={{0,3},{1,2},{2,1},{3,0},{4,7},{5,6},{6,5},{7,4},{8,11},{9,10},{10,... | collective-permute-start | bytes 1572872 | tf_op jit(solution)/shard_map/ppermute | solution.py:134

commit v5 on v4

--- a/solution.py
+++ b/solution.py
@@ -153,20 +153,20 @@
         z2 = swap(mine, "z", 1)
         y2 = swap(after(own, mine), "y", 1)
         y3 = swap(after(y1, table), "y", 1)
-        z1, z2 = after(z1, y1), after(z2, y1)
+        result = run([after(own, y1)], None)
+        z1, z2 = after(z1, y1, result), after(z2, y1, result)
         z3 = swap(z1, "z", 1)
         pair = joined(z1, z2)
         p1 = swap(after(pair, y3), "y", 0)
         column = joined(*[p.part(0, TURNED) for p in (own, y1, y2, y3)])
         b1 = swap(column, "z", 0)
-        result = run([own, y1], None)
-        result = run([after(y2, p1), y3, z1, z2], result)
-        p2 = swap(joined(pair, p1), "y", 1)
+        result = run([y1, after(y2, column), y3, z1, z2], result)
+        p2 = swap(after(joined(pair, p1), result), "y", 1)
         q1 = swap(after(z3, p1, result), "y", 0)
         b2 = swap(after(column, z3, result), "z", 1)
         b3 = swap(after(b1, q1), "z", 1)
         q2 = swap(after(joined(z3, q1), b1), "y", 1)
-        for pieces in ([z3, p1, b1], [q1, p2], [b2, q2], [b3]):
+        for pieces in ([z3, p1, b1], [q1, p2, b2], [q2, b3]):
             result = run(pieces, result)
         return result
 

time: 90.6 us -> 86.1 us (0.950)
  waiting for transfers between devices: 21.7 us -> 17.7 us
  Pallas kernels: 32.4 us -> 30.3 us
    ppermute x13, waiting for transfers between devices: 21.7 us -> 17.7 us  [swap(): rows = lax.ppermute(piece.rows, AXES, pairs)]
    pallas_call x6 -> x5, Pallas kernels: 32.4 us -> 30.2 us  [project(): pl.pallas_call(functools.partial(project_kernel, layout, starts, len(prev...]
    unnamed x10, local copies, waits for them, and re-layouts: 4.35 us -> 6.02 us
    ppermute x13, starting transfers between devices: 26.9 us -> 27.8 us  [swap(): rows = lax.ppermute(piece.rows, AXES, pairs)]
  transfers between devices with their start and end apart: 13 -> 13, of which waited for: 5 -> 6; matrix products, arithmetic and copies ran while one was open for 5% -> 4% of each run, Pallas kernels for 32% -> 29%
where the time goes in v5:
time: 86.1 us; the launch traced here: 85.9 us
  Pallas kernels  30.3 us (35%)
  starting transfers between devices  27.8 us (32%)
  waiting for transfers between devices  17.7 us (21%)
  local copies, waits for them, and re-layouts  8.75 us (10%)
  other arithmetic  1.06 us (1%)
    pallas_call x5, Pallas kernels, project(): pl.pallas_call(functools.partial(project_kernel, layout, starts, len(prev...  30.2 us
    ppermute x13, starting transfers between devices, swap(): rows = lax.ppermute(piece.rows, AXES, pairs)  27.8 us
    ppermute x13, waiting for transfers between devices, swap(): rows = lax.ppermute(piece.rows, AXES, pairs)  17.7 us
    unnamed x10, local copies, waits for them, and re-layouts  6.02 us
  transfers between devices with their start and end apart: 13, of which 6 were waited for; matrix products, arithmetic and copies ran while one was open for 4% of the time, Pallas kernels for 29%

profile of v5, /device:TPU:4, one launch (start us, length us, event | category | flops | bytes accessed | tf_op | source)
XLA Modules:
  0.0 85.9 jit_solution(630786437251130363)
XLA Ops:
  0.0 1.6 %collective-permute-start.1 = (bf16[64,4096]{1,0:T(8,128)(2,1)}, bf16[64,4096]{1,0:T(8,128)(2,1)S(1)}, u32[]{:S(2)}, u32[]{:S(2)}) collective-permute-start(bf16[64,4096]{1,0:T(8,128)(2,1)} %refs_0_.2), channel_id=1, source_target_pairs={{0,4},{1,5},{2,6},{3,7},{4,0},{5,1},{6,2},{7,3},{8,12},{9,13},{10,... | collective-permute-start | bytes 1572872 | tf_op jit(solution)/shard_map/ppermute | solution.py:134
  2.7 6.4 %collective-permute-start.3 = (bf16[48,4096]{1,0:T(8,128)(2,1)S(1)}, bf16[48,4096]{1,0:T(8,128)(2,1)S(1)}, u32[]{:S(2)}, u32[]{:S(2)}) collective-permute-start(bf16[48,4096]{1,0:T(8,128)(2,1)S(1)} %slice_bitcast_fusion), channel_id=1, source_target_pairs={{0,3},{1,2},{2,1},{3,0},{4,7},{5,6},{6,5},{7,4},{8,11},{9,10},{10,... | collective-permute-start | bytes 1179656 | tf_op jit(solution)/shard_map/ppermute | solution.py:134
  9.1 1.5 %collective-permute-start = (bf16[48,4096]{1,0:T(8,128)(2,1)S(1)}, bf16[48,4096]{1,0:T(8,128)(2,1)S(1)}, u32[]{:S(2)}, u32[]{:S(2)}) collective-permute-start(bf16[48,4096]{1,0:T(8,128)(2,1)S(1)} %slice_bitcast_fusion), channel_id=1, source_target_pairs={{0,1},{1,0},{2,3},{3,2},{4,5},{5,4},{6,7},{7,6},{8,9},{9,8},{10,11... | collective-permute-start | bytes 1179656 | tf_op jit(solution)/shard_map/ppermute | solution.py:134
  10.6 2.2 %collective-permute-start.6 = (bf16[64,4096]{1,0:T(8,128)(2,1)}, bf16[64,4096]{1,0:T(8,128)(2,1)S(1)}, u32[]{:S(2)}, u32[]{:S(2)}) collective-permute-start(bf16[64,4096]{1,0:T(8,128)(2,1)} %refs_0_.2), channel_id=1, source_target_pairs={{0,12},{1,13},{2,14},{3,15},{4,8},{5,9},{6,10},{7,11},{8,4},{9,5},... | collective-permute-start | bytes 1572872 | tf_op jit(solution)/shard_map/ppermute | solution.py:134
  15.1 2.2 %copy-done = bf16[14,9,128,128]{3,2,1,0:T(8,128)(2,1)S(1)} copy-done((bf16[14,9,128,128]{3,2,1,0:T(8,128)(2,1)S(1)}, bf16[14,9,128,128]{3,2,1,0:T(8,128)(2,1)}, u32[]{:S(2)}) %copy-start) | copy-done | bytes 4128792
  17.2 2.2 %copy-done.2 = bf16[14,9,128,128]{3,2,1,0:T(8,128)(2,1)S(1)} copy-done((bf16[14,9,128,128]{3,2,1,0:T(8,128)(2,1)S(1)}, bf16[14,9,128,128]{3,2,1,0:T(8,128)(2,1)}, u32[]{:S(2)}) %copy-start.2) | copy-done | bytes 4128792
  19.5 1.1 %collective-permute-start.4 = (bf16[64,4096]{1,0:T(8,128)(2,1)S(1)}, bf16[64,4096]{1,0:T(8,128)(2,1)S(1)}, u32[]{:S(2)}, u32[]{:S(2)}) collective-permute-start(bf16[64,4096]{1,0:T(8,128)(2,1)S(1)} %collective-permute-done.1.refs_0_), channel_id=1, source_target_pairs={{0,12},{1,13},{2,14},{3,15},{4,8},{5,9},{6,10},{7,11},{8,4},{9,5},... | collective-permute-start | bytes 1572872 | tf_op jit(solution)/shard_map/ppermute | solution.py:134
  21.6 1.3 %copy-done.3 = bf16[14,9,128,128]{3,2,1,0:T(8,128)(2,1)S(1)} copy-done((bf16[14,9,128,128]{3,2,1,0:T(8,128)(2,1)S(1)}, bf16[14,9,128,128]{3,2,1,0:T(8,128)(2,1)}, u32[]{:S(2)}) %copy-start.3) | copy-done | bytes 4128792
  22.8 3.5 %shard_map.65.refs_7_ = bf16[1024,1792]{1,0:T(8,128)(2,1)} custom-call(s32[268]{0:T(512)S(1)} %shard_map.64.table_ref, bf16[64,4096]{1,0:T(8,128)(2,1)S(1)} %copy-done.4, bf16[14,9,128,128]{3,2,1,0:T(8,128)(2,1)S(1)} %copy-done.1, bf16[14,9,128,128]{3,2,1,0:T(8,128)(2,1)S(1)} %copy-done.3), custom_call_target="tpu_custom_call" | custom-call | flops 5219999744 | bytes 229376 | tf_op jit(solution)/shard_map/pallas_call | solution.py:111
  26.4 4.1 %collective-permute-start.2 = (bf16[48,4096]{1,0:T(8,128)(2,1)S(1)}, bf16[48,4096]{1,0:T(8,128)(2,1)S(1)}, u32[]{:S(2)}, u32[]{:S(2)}) collective-permute-start(bf16[48,4096]{1,0:T(8,128)(2,1)S(1)} %collective-permute-done.refs_3_), channel_id=1, source_target_pairs={{0,3},{1,2},{2,1},{3,0},{4,7},{5,6},{6,5},{7,4},{8,11},{9,10},{10,... | collective-permute-start | bytes 1179656 | tf_op jit(solution)/shard_map/ppermute | solution.py:134
  30.6 1.9 %collective-permute-start.8 = (bf16[64,4096]{1,0:T(8,128)(2,1)S(1)}, bf16[64,4096]{1,0:T(8,128)(2,1)S(1)}, u32[]{:S(2)}, u32[]{:S(2)}) collective-permute-start(bf16[64,4096]{1,0:T(8,128)(2,1)S(1)} %pad_maximum_fusion.3), channel_id=1, source_target_pairs={{0,1},{1,0},{2,3},{3,2},{4,5},{5,4},{6,7},{7,6},{8,9},{9,8},{10,11... | collective-permute-start | bytes 1572872 | tf_op jit(solution)/shard_map/ppermute | solution.py:134
  33.3 7.6 %shard_map.66.refs_5_ = bf16[1024,1792]{1,0:T(8,128)(2,1)} custom-call(s32[268]{0:T(512)S(1)} %shard_map.64.table_ref, bf16[64,4096]{1,0:T(8,128)(2,1)S(1)} %collective-permute-done.1.refs_0_, bf16[64,4096]{1,0:T(8,128)(2,1)S(1)} %collective-permute-done.6.refs_1_, ...), custom_call_target="tpu_custom_call", output_to_operand_aliasing={{}: (8, {})} | custom-call | flops 11939999744 | bytes 1032192 | tf_op jit(solution)/shard_map/pallas_call | solution.py:111
  40.9 3.6 %collective-permute-done.5.refs_1_ = bf16[96,4096]{1,0:T(8,128)(2,1)S(1)} collective-permute-done((bf16[96,4096]{1,0:T(8,128)(2,1)S(1)}, bf16[96,4096]{1,0:T(8,128)(2,1)S(1)}, u32[]{:S(2)}, u32[]{:S(2)}) %collective-permute-start.5) | collective-permute-done | bytes 786464 | tf_op jit(solution)/shard_map/ppermute | solution.py:134
  44.6 2.3 %collective-permute-start.11 = (bf16[192,4096]{1,0:T(8,128)(2,1)S(1)}, bf16[192,4096]{1,0:T(8,128)(2,1)S(1)}, u32[]{:S(2)}, u32[]{:S(2)}) collective-permute-start(bf16[192,4096]{1,0:T(8,128)(2,1)S(1)} %pad_maximum_fusion), channel_id=1, source_target_pairs={{0,12},{1,13},{2,14},{3,15},{4,8},{5,9},{6,10},{7,11},{8,4},{9,5},... | collective-permute-start | bytes 4718600 | tf_op jit(solution)/shard_map/ppermute | solution.py:134
  47.0 4.2 %collective-permute-done.2.refs_0_ = bf16[48,4096]{1,0:T(8,128)(2,1)S(1)} collective-permute-done((bf16[48,4096]{1,0:T(8,128)(2,1)S(1)}, bf16[48,4096]{1,0:T(8,128)(2,1)S(1)}, u32[]{:S(2)}, u32[]{:S(2)}) %collective-permute-start.2) | collective-permute-done | bytes 393248 | tf_op jit(solution)/shard_map/ppermute | solution.py:134
  51.2 1.9 %collective-permute-start.12 = (bf16[64,4096]{1,0:T(8,128)(2,1)S(1)}, bf16[64,4096]{1,0:T(8,128)(2,1)S(1)}, u32[]{:S(2)}, u32[]{:S(2)}) collective-permute-start(bf16[64,4096]{1,0:T(8,128)(2,1)S(1)} %pad_maximum_fusion.3), channel_id=1, source_target_pairs={{0,3},{1,2},{2,1},{3,0},{4,7},{5,6},{6,5},{7,4},{8,11},{9,10},{10,... | collective-permute-start | bytes 1572872 | tf_op jit(solution)/shard_map/ppermute | solution.py:134
  53.8 6.1 %shard_map.67.refs_5_ = bf16[1024,1792]{1,0:T(8,128)(2,1)} custom-call(s32[268]{0:T(512)S(1)} %shard_map.64.table_ref, bf16[48,4096]{1,0:T(8,128)(2,1)S(1)} %collective-permute-done.2.refs_0_, bf16[96,4096]{1,0:T(8,128)(2,1)S(1)} %collective-permute-done.5.refs_1_, ...), custom_call_target="tpu_custom_call", output_to_operand_aliasing={{}: (6, {})} | custom-call | flops 9539999744 | bytes 745472 | tf_op jit(solution)/shard_map/pallas_call | solution.py:111
  59.9 5.3 %collective-permute-done.7.refs_0_ = bf16[48,4096]{1,0:T(8,128)(2,1)S(1)} collective-permute-done((bf16[48,4096]{1,0:T(8,128)(2,1)S(1)}, bf16[48,4096]{1,0:T(8,128)(2,1)S(1)}, u32[]{:S(2)}, u32[]{:S(2)}) %collective-permute-start.7) | collective-permute-done | bytes 393248 | tf_op jit(solution)/shard_map/ppermute | solution.py:134
  65.1 2.2 %collective-permute-start.10 = (bf16[64,4096]{1,0:T(8,128)(2,1)S(1)}, bf16[64,4096]{1,0:T(8,128)(2,1)S(1)}, u32[]{:S(2)}, u32[]{:S(2)}) collective-permute-start(bf16[64,4096]{1,0:T(8,128)(2,1)S(1)} %collective-permute-done.8.refs_2_), channel_id=1, source_target_pairs={{0,3},{1,2},{2,1},{3,0},{4,7},{5,6},{6,5},{7,4},{8,11},{9,10},{10,... | collective-permute-start | bytes 1572872 | tf_op jit(solution)/shard_map/ppermute | solution.py:134
  67.4 1.1 %collective-permute-start.9 = (bf16[96,4096]{1,0:T(8,128)(2,1)S(1)}, bf16[96,4096]{1,0:T(8,128)(2,1)S(1)}, u32[]{:S(2)}, u32[]{:S(2)}) collective-permute-start(bf16[96,4096]{1,0:T(8,128)(2,1)S(1)} %pad_maximum_fusion.2), channel_id=1, source_target_pairs={{0,12},{1,13},{2,14},{3,15},{4,8},{5,9},{6,10},{7,11},{8,4},{9,5},... | collective-permute-start | bytes 2359304 | tf_op jit(solution)/shard_map/ppermute | solution.py:134
  68.6 2.0 %collective-permute-done.11.refs_1_ = bf16[192,4096]{1,0:T(8,128)(2,1)S(1)} collective-permute-done((bf16[192,4096]{1,0:T(8,128)(2,1)S(1)}, bf16[192,4096]{1,0:T(8,128)(2,1)S(1)}, u32[]{:S(2)}, u32[]{:S(2)}) %collective-permute-start.11) | collective-permute-done | bytes 1572896 | tf_op jit(solution)/shard_map/ppermute | solution.py:134
  70.6 8.1 %shard_map.68.refs_4_ = bf16[1024,1792]{1,0:T(8,128)(2,1)} custom-call(s32[268]{0:T(512)S(1)} %shard_map.64.table_ref, bf16[48,4096]{1,0:T(8,128)(2,1)S(1)} %collective-permute-done.7.refs_0_, bf16[192,4096]{1,0:T(8,128)(2,1)S(1)} %collective-permute-done.11.refs_1_, ...), custom_call_target="tpu_custom_call", output_to_operand_aliasing={{}: (6, {})} | custom-call | flops 12419999744 | bytes 1089536 | tf_op jit(solution)/shard_map/pallas_call | solution.py:111
  78.7 2.1 %collective-permute-done.9.refs_0_ = bf16[96,4096]{1,0:T(8,128)(2,1)S(1)} collective-permute-done((bf16[96,4096]{1,0:T(8,128)(2,1)S(1)}, bf16[96,4096]{1,0:T(8,128)(2,1)S(1)}, u32[]{:S(2)}, u32[]{:S(2)}) %collective-permute-start.9) | collective-permute-done | bytes 786464 | tf_op jit(solution)/shard_map/ppermute | solution.py:134
  80.7 5.0 %shard_map.69 = bf16[1024,1792]{1,0:T(8,128)(2,1)} custom-call(s32[268]{0:T(512)S(1)} %shard_map.64.table_ref, bf16[96,4096]{1,0:T(8,128)(2,1)S(1)} %collective-permute-done.9.refs_0_, bf16[64,4096]{1,0:T(8,128)(2,1)S(1)} %collective-permute-done.10.refs_1_, bf16[14,9,128,128]{3,2,1,0:T(8,128)(2,1)S(1)} %copy-done.1, ...), custom_call_target="tpu_custom_call", output_to_operand_aliasing={{}: (5, {})} | custom-call | flops 8099999744 | bytes 573440 | tf_op jit(solution)/shard_map/pallas_call | solution.py:111
  (31 shorter events, 6.3 us)
Async XLA Ops:
  0.0 19.4 %collective-permute-start.1 = (bf16[64,4096]{1,0:T(8,128)(2,1)}, bf16[64,4096]{1,0:T(8,128)(2,1)S(1)}, u32[]{:S(2)}, u32[]{:S(2)}) collective-permute-start(bf16[64,4096]{1,0:T(8,128)(2,1)} %refs_0_.2), channel_id=1, source_target_pairs={{0,4},{1,5},{2,6},{3,7},{4,0},{5,1},{6,2},{7,3},{8,12},{9,13},{10,... | collective-permute-start | bytes 1572872 | tf_op jit(solution)/shard_map/ppermute | solution.py:134
  1.6 17.8 %copy-start.4 = (bf16[64,4096]{1,0:T(8,128)(2,1)S(1)}, bf16[64,4096]{1,0:T(8,128)(2,1)}, u32[]{:S(2)}) copy-start(bf16[64,4096]{1,0:T(8,128)(2,1)} %refs_0_.2) | copy-start | bytes 1572868
  2.7 23.7 %collective-permute-start.3 = (bf16[48,4096]{1,0:T(8,128)(2,1)S(1)}, bf16[48,4096]{1,0:T(8,128)(2,1)S(1)}, u32[]{:S(2)}, u32[]{:S(2)}) collective-permute-start(bf16[48,4096]{1,0:T(8,128)(2,1)S(1)} %slice_bitcast_fusion), channel_id=1, source_target_pairs={{0,3},{1,2},{2,1},{3,0},{4,7},{5,6},{6,5},{7,4},{8,11},{9,10},{10,... | collective-permute-start | bytes 1179656 | tf_op jit(solution)/shard_map/ppermute | solution.py:134
  9.1 17.3 %collective-permute-start = (bf16[48,4096]{1,0:T(8,128)(2,1)S(1)}, bf16[48,4096]{1,0:T(8,128)(2,1)S(1)}, u32[]{:S(2)}, u32[]{:S(2)}) collective-permute-start(bf16[48,4096]{1,0:T(8,128)(2,1)S(1)} %slice_bitcast_fusion), channel_id=1, source_target_pairs={{0,1},{1,0},{2,3},{3,2},{4,5},{5,4},{6,7},{7,6},{8,9},{9,8},{10,11... | collective-permute-start | bytes 1179656 | tf_op jit(solution)/shard_map/ppermute | solution.py:134
  10.6 10.6 %collective-permute-start.6 = (bf16[64,4096]{1,0:T(8,128)(2,1)}, bf16[64,4096]{1,0:T(8,128)(2,1)S(1)}, u32[]{:S(2)}, u32[]{:S(2)}) collective-permute-start(bf16[64,4096]{1,0:T(8,128)(2,1)} %refs_0_.2), channel_id=1, source_target_pairs={{0,12},{1,13},{2,14},{3,15},{4,8},{5,9},{6,10},{7,11},{8,4},{9,5},... | collective-permute-start | bytes 1572872 | tf_op jit(solution)/shard_map/ppermute | solution.py:134
  15.1 2.2 %copy-start = (bf16[14,9,128,128]{3,2,1,0:T(8,128)(2,1)S(1)}, bf16[14,9,128,128]{3,2,1,0:T(8,128)(2,1)}, u32[]{:S(2)}) copy-start(bf16[14,9,128,128]{3,2,1,0:T(8,128)(2,1)} %refs_2_.3) | copy-start | bytes 12386308
  17.2 2.2 %copy-start.2 = (bf16[14,9,128,128]{3,2,1,0:T(8,128)(2,1)S(1)}, bf16[14,9,128,128]{3,2,1,0:T(8,128)(2,1)}, u32[]{:S(2)}) copy-start(bf16[14,9,128,128]{3,2,1,0:T(8,128)(2,1)} %refs_3_.5) | copy-start | bytes 12386308
  19.4 2.2 %copy-start.1 = (bf16[14,9,128,128]{3,2,1,0:T(8,128)(2,1)S(1)}, bf16[14,9,128,128]{3,2,1,0:T(8,128)(2,1)}, u32[]{:S(2)}) copy-start(bf16[14,9,128,128]{3,2,1,0:T(8,128)(2,1)} %refs_2_.3) | copy-start | bytes 12386308
  19.4 3.4 %copy-start.3 = (bf16[14,9,128,128]{3,2,1,0:T(8,128)(2,1)S(1)}, bf16[14,9,128,128]{3,2,1,0:T(8,128)(2,1)}, u32[]{:S(2)}) copy-start(bf16[14,9,128,128]{3,2,1,0:T(8,128)(2,1)} %refs_3_.5) | copy-start | bytes 12386308
  19.5 11.1 %collective-permute-start.4 = (bf16[64,4096]{1,0:T(8,128)(2,1)S(1)}, bf16[64,4096]{1,0:T(8,128)(2,1)S(1)}, u32[]{:S(2)}, u32[]{:S(2)}) collective-permute-start(bf16[64,4096]{1,0:T(8,128)(2,1)S(1)} %collective-permute-done.1.refs_0_), channel_id=1, source_target_pairs={{0,12},{1,13},{2,14},{3,15},{4,8},{5,9},{6,10},{7,11},{8,4},{9,5},... | collective-permute-start | bytes 1572872 | tf_op jit(solution)/shard_map/ppermute | solution.py:134
  26.4 24.8 %collective-permute-start.2 = (bf16[48,4096]{1,0:T(8,128)(2,1)S(1)}, bf16[48,4096]{1,0:T(8,128)(2,1)S(1)}, u32[]{:S(2)}, u32[]{:S(2)}) collective-permute-start(bf16[48,4096]{1,0:T(8,128)(2,1)S(1)} %collective-permute-done.refs_3_), channel_id=1, source_target_pairs={{0,3},{1,2},{2,1},{3,0},{4,7},{5,6},{6,5},{7,4},{8,11},{9,10},{10,... | collective-permute-start | bytes 1179656 | tf_op jit(solution)/shard_map/ppermute | solution.py:134
  30.6 23.2 %collective-permute-start.8 = (bf16[64,4096]{1,0:T(8,128)(2,1)S(1)}, bf16[64,4096]{1,0:T(8,128)(2,1)S(1)}, u32[]{:S(2)}, u32[]{:S(2)}) collective-permute-start(bf16[64,4096]{1,0:T(8,128)(2,1)S(1)} %pad_maximum_fusion.3), channel_id=1, source_target_pairs={{0,1},{1,0},{2,3},{3,2},{4,5},{5,4},{6,7},{7,6},{8,9},{9,8},{10,11... | collective-permute-start | bytes 1572872 | tf_op jit(solution)/shard_map/ppermute | solution.py:134
  32.5 12.0 %collective-permute-start.5 = (bf16[96,4096]{1,0:T(8,128)(2,1)S(1)}, bf16[96,4096]{1,0:T(8,128)(2,1)S(1)}, u32[]{:S(2)}, u32[]{:S(2)}) collective-permute-start(bf16[96,4096]{1,0:T(8,128)(2,1)S(1)} %pad_maximum_fusion.1), channel_id=1, source_target_pairs={{0,4},{1,5},{2,6},{3,7},{4,0},{5,1},{6,2},{7,3},{8,12},{9,13},{10,... | collective-permute-start | bytes 2359304 | tf_op jit(solution)/shard_map/ppermute | solution.py:134
  44.6 25.9 %collective-permute-start.11 = (bf16[192,4096]{1,0:T(8,128)(2,1)S(1)}, bf16[192,4096]{1,0:T(8,128)(2,1)S(1)}, u32[]{:S(2)}, u32[]{:S(2)}) collective-permute-start(bf16[192,4096]{1,0:T(8,128)(2,1)S(1)} %pad_maximum_fusion), channel_id=1, source_target_pairs={{0,12},{1,13},{2,14},{3,15},{4,8},{5,9},{6,10},{7,11},{8,4},{9,5},... | collective-permute-start | bytes 4718600 | tf_op jit(solution)/shard_map/ppermute | solution.py:134
  51.2 17.4 %collective-permute-start.12 = (bf16[64,4096]{1,0:T(8,128)(2,1)S(1)}, bf16[64,4096]{1,0:T(8,128)(2,1)S(1)}, u32[]{:S(2)}, u32[]{:S(2)}) collective-permute-start(bf16[64,4096]{1,0:T(8,128)(2,1)S(1)} %pad_maximum_fusion.3), channel_id=1, source_target_pairs={{0,3},{1,2},{2,1},{3,0},{4,7},{5,6},{6,5},{7,4},{8,11},{9,10},{10,... | collective-permute-start | bytes 1572872 | tf_op jit(solution)/shard_map/ppermute | solution.py:134
  53.1 12.1 %collective-permute-start.7 = (bf16[48,4096]{1,0:T(8,128)(2,1)S(1)}, bf16[48,4096]{1,0:T(8,128)(2,1)S(1)}, u32[]{:S(2)}, u32[]{:S(2)}) collective-permute-start(bf16[48,4096]{1,0:T(8,128)(2,1)S(1)} %collective-permute-done.2.refs_0_), channel_id=1, source_target_pairs={{0,4},{1,5},{2,6},{3,7},{4,0},{5,1},{6,2},{7,3},{8,12},{9,13},{10,... | collective-permute-start | bytes 1179656 | tf_op jit(solution)/shard_map/ppermute | solution.py:134
  65.1 13.5 %collective-permute-start.10 = (bf16[64,4096]{1,0:T(8,128)(2,1)S(1)}, bf16[64,4096]{1,0:T(8,128)(2,1)S(1)}, u32[]{:S(2)}, u32[]{:S(2)}) collective-permute-start(bf16[64,4096]{1,0:T(8,128)(2,1)S(1)} %collective-permute-done.8.refs_2_), channel_id=1, source_target_pairs={{0,3},{1,2},{2,1},{3,0},{4,7},{5,6},{6,5},{7,4},{8,11},{9,10},{10,... | collective-permute-start | bytes 1572872 | tf_op jit(solution)/shard_map/ppermute | solution.py:134
  67.4 13.3 %collective-permute-start.9 = (bf16[96,4096]{1,0:T(8,128)(2,1)S(1)}, bf16[96,4096]{1,0:T(8,128)(2,1)S(1)}, u32[]{:S(2)}, u32[]{:S(2)}) collective-permute-start(bf16[96,4096]{1,0:T(8,128)(2,1)S(1)} %pad_maximum_fusion.2), channel_id=1, source_target_pairs={{0,12},{1,13},{2,14},{3,15},{4,8},{5,9},{6,10},{7,11},{8,4},{9,5},... | collective-permute-start | bytes 2359304 | tf_op jit(solution)/shard_map/ppermute | solution.py:134

commit v6 on v5

--- a/solution.py
+++ b/solution.py
@@ -164,7 +164,7 @@
         p2 = swap(after(joined(pair, p1), result), "y", 1)
         q1 = swap(after(z3, p1, result), "y", 0)
         b2 = swap(after(column, z3, result), "z", 1)
-        b3 = swap(after(b1, q1), "z", 1)
+        b3 = swap(after(b1, z3, result), "z", 1)
         q2 = swap(after(joined(z3, q1), b1), "y", 1)
         for pieces in ([z3, p1, b1], [q1, p2, b2], [q2, b3]):
             result = run(pieces, result)

time: 86.1 us -> 86.1 us (level)
  transfers between devices with their start and end apart: 13 -> 13, of which waited for: 6 -> 7; matrix products, arithmetic and copies ran while one was open for 4% -> 4% of each run, Pallas kernels for 29% -> 29%
where the time goes in v6:
time: 86.1 us; the launch traced here: 85.9 us
  Pallas kernels  30.2 us (35%)
  starting transfers between devices  27.2 us (32%)
  waiting for transfers between devices  18.3 us (21%)
  local copies, waits for them, and re-layouts  8.75 us (10%)
  other arithmetic  1.05 us (1%)
    pallas_call x5, Pallas kernels, project(): pl.pallas_call(functools.partial(project_kernel, layout, starts, len(prev...  30.2 us
    ppermute x13, starting transfers between devices, swap(): rows = lax.ppermute(piece.rows, AXES, pairs)  27.2 us
    ppermute x13, waiting for transfers between devices, swap(): rows = lax.ppermute(piece.rows, AXES, pairs)  18.3 us
    unnamed x10, local copies, waits for them, and re-layouts  6.02 us
  transfers between devices with their start and end apart: 13, of which 7 were waited for; matrix products, arithmetic and copies ran while one was open for 4% of the time, Pallas kernels for 29%

profile of v6, /device:TPU:4, one launch (start us, length us, event | category | flops | bytes accessed | tf_op | source)
XLA Modules:
  0.0 85.9 jit_solution(9473355714587067257)
XLA Ops:
  0.0 1.6 %collective-permute-start.1 = (bf16[64,4096]{1,0:T(8,128)(2,1)}, bf16[64,4096]{1,0:T(8,128)(2,1)S(1)}, u32[]{:S(2)}, u32[]{:S(2)}) collective-permute-start(bf16[64,4096]{1,0:T(8,128)(2,1)} %refs_0_.2), channel_id=1, source_target_pairs={{0,4},{1,5},{2,6},{3,7},{4,0},{5,1},{6,2},{7,3},{8,12},{9,13},{10,... | collective-permute-start | bytes 1572872 | tf_op jit(solution)/shard_map/ppermute | solution.py:134
  1.6 1.1 %slice_bitcast_fusion = bf16[48,4096]{1,0:T(8,128)(2,1)S(1)} fusion(bf16[1,64,4096]{2,1,0:T(8,128)(2,1)} %bitcast.16), kind=kLoop, calls=%fused_computation.4 | loop fusion | bytes 786432 | tf_op jit(solution)/shard_map/reshape | solution.py:36
  2.7 6.4 %collective-permute-start.3 = (bf16[48,4096]{1,0:T(8,128)(2,1)S(1)}, bf16[48,4096]{1,0:T(8,128)(2,1)S(1)}, u32[]{:S(2)}, u32[]{:S(2)}) collective-permute-start(bf16[48,4096]{1,0:T(8,128)(2,1)S(1)} %slice_bitcast_fusion), channel_id=1, source_target_pairs={{0,3},{1,2},{2,1},{3,0},{4,7},{5,6},{6,5},{7,4},{8,11},{9,10},{10,... | collective-permute-start | bytes 1179656 | tf_op jit(solution)/shard_map/ppermute | solution.py:134
  9.1 1.5 %collective-permute-start = (bf16[48,4096]{1,0:T(8,128)(2,1)S(1)}, bf16[48,4096]{1,0:T(8,128)(2,1)S(1)}, u32[]{:S(2)}, u32[]{:S(2)}) collective-permute-start(bf16[48,4096]{1,0:T(8,128)(2,1)S(1)} %slice_bitcast_fusion), channel_id=1, source_target_pairs={{0,1},{1,0},{2,3},{3,2},{4,5},{5,4},{6,7},{7,6},{8,9},{9,8},{10,11... | collective-permute-start | bytes 1179656 | tf_op jit(solution)/shard_map/ppermute | solution.py:134
  10.6 2.2 %collective-permute-start.6 = (bf16[64,4096]{1,0:T(8,128)(2,1)}, bf16[64,4096]{1,0:T(8,128)(2,1)S(1)}, u32[]{:S(2)}, u32[]{:S(2)}) collective-permute-start(bf16[64,4096]{1,0:T(8,128)(2,1)} %refs_0_.2), channel_id=1, source_target_pairs={{0,12},{1,13},{2,14},{3,15},{4,8},{5,9},{6,10},{7,11},{8,4},{9,5},... | collective-permute-start | bytes 1572872 | tf_op jit(solution)/shard_map/ppermute | solution.py:134
  15.1 2.2 %copy-done = bf16[14,9,128,128]{3,2,1,0:T(8,128)(2,1)S(1)} copy-done((bf16[14,9,128,128]{3,2,1,0:T(8,128)(2,1)S(1)}, bf16[14,9,128,128]{3,2,1,0:T(8,128)(2,1)}, u32[]{:S(2)}) %copy-start) | copy-done | bytes 4128792
  17.2 2.2 %copy-done.2 = bf16[14,9,128,128]{3,2,1,0:T(8,128)(2,1)S(1)} copy-done((bf16[14,9,128,128]{3,2,1,0:T(8,128)(2,1)S(1)}, bf16[14,9,128,128]{3,2,1,0:T(8,128)(2,1)}, u32[]{:S(2)}) %copy-start.2) | copy-done | bytes 4128792
  19.5 1.1 %collective-permute-start.4 = (bf16[64,4096]{1,0:T(8,128)(2,1)S(1)}, bf16[64,4096]{1,0:T(8,128)(2,1)S(1)}, u32[]{:S(2)}, u32[]{:S(2)}) collective-permute-start(bf16[64,4096]{1,0:T(8,128)(2,1)S(1)} %collective-permute-done.1.refs_0_), channel_id=1, source_target_pairs={{0,12},{1,13},{2,14},{3,15},{4,8},{5,9},{6,10},{7,11},{8,4},{9,5},... | collective-permute-start | bytes 1572872 | tf_op jit(solution)/shard_map/ppermute | solution.py:134
  21.6 1.3 %copy-done.3 = bf16[14,9,128,128]{3,2,1,0:T(8,128)(2,1)S(1)} copy-done((bf16[14,9,128,128]{3,2,1,0:T(8,128)(2,1)S(1)}, bf16[14,9,128,128]{3,2,1,0:T(8,128)(2,1)}, u32[]{:S(2)}) %copy-start.3) | copy-done | bytes 4128792
  22.8 3.5 %shard_map.65.refs_7_ = bf16[1024,1792]{1,0:T(8,128)(2,1)} custom-call(s32[268]{0:T(512)S(1)} %shard_map.64.table_ref, bf16[64,4096]{1,0:T(8,128)(2,1)S(1)} %copy-done.4, bf16[14,9,128,128]{3,2,1,0:T(8,128)(2,1)S(1)} %copy-done.1, bf16[14,9,128,128]{3,2,1,0:T(8,128)(2,1)S(1)} %copy-done.3), custom_call_target="tpu_custom_call" | custom-call | flops 5219999744 | bytes 229376 | tf_op jit(solution)/shard_map/pallas_call | solution.py:111
  26.4 4.1 %collective-permute-start.2 = (bf16[48,4096]{1,0:T(8,128)(2,1)S(1)}, bf16[48,4096]{1,0:T(8,128)(2,1)S(1)}, u32[]{:S(2)}, u32[]{:S(2)}) collective-permute-start(bf16[48,4096]{1,0:T(8,128)(2,1)S(1)} %collective-permute-done.refs_3_), channel_id=1, source_target_pairs={{0,3},{1,2},{2,1},{3,0},{4,7},{5,6},{6,5},{7,4},{8,11},{9,10},{10,... | collective-permute-start | bytes 1179656 | tf_op jit(solution)/shard_map/ppermute | solution.py:134
  30.6 1.9 %collective-permute-start.8 = (bf16[64,4096]{1,0:T(8,128)(2,1)S(1)}, bf16[64,4096]{1,0:T(8,128)(2,1)S(1)}, u32[]{:S(2)}, u32[]{:S(2)}) collective-permute-start(bf16[64,4096]{1,0:T(8,128)(2,1)S(1)} %pad_maximum_fusion.3), channel_id=1, source_target_pairs={{0,1},{1,0},{2,3},{3,2},{4,5},{5,4},{6,7},{7,6},{8,9},{9,8},{10,11... | collective-permute-start | bytes 1572872 | tf_op jit(solution)/shard_map/ppermute | solution.py:134
  33.3 7.5 %shard_map.66.refs_5_ = bf16[1024,1792]{1,0:T(8,128)(2,1)} custom-call(s32[268]{0:T(512)S(1)} %shard_map.64.table_ref, bf16[64,4096]{1,0:T(8,128)(2,1)S(1)} %collective-permute-done.1.refs_0_, bf16[64,4096]{1,0:T(8,128)(2,1)S(1)} %collective-permute-done.6.refs_1_, ...), custom_call_target="tpu_custom_call", output_to_operand_aliasing={{}: (8, {})} | custom-call | flops 11939999744 | bytes 1032192 | tf_op jit(solution)/shard_map/pallas_call | solution.py:111
  40.9 3.6 %collective-permute-done.5.refs_1_ = bf16[96,4096]{1,0:T(8,128)(2,1)S(1)} collective-permute-done((bf16[96,4096]{1,0:T(8,128)(2,1)S(1)}, bf16[96,4096]{1,0:T(8,128)(2,1)S(1)}, u32[]{:S(2)}, u32[]{:S(2)}) %collective-permute-start.5) | collective-permute-done | bytes 786464 | tf_op jit(solution)/shard_map/ppermute | solution.py:134
  44.6 2.3 %collective-permute-start.11 = (bf16[192,4096]{1,0:T(8,128)(2,1)S(1)}, bf16[192,4096]{1,0:T(8,128)(2,1)S(1)}, u32[]{:S(2)}, u32[]{:S(2)}) collective-permute-start(bf16[192,4096]{1,0:T(8,128)(2,1)S(1)} %pad_maximum_fusion), channel_id=1, source_target_pairs={{0,12},{1,13},{2,14},{3,15},{4,8},{5,9},{6,10},{7,11},{8,4},{9,5},... | collective-permute-start | bytes 4718600 | tf_op jit(solution)/shard_map/ppermute | solution.py:134
  47.0 4.2 %collective-permute-done.2.refs_0_ = bf16[48,4096]{1,0:T(8,128)(2,1)S(1)} collective-permute-done((bf16[48,4096]{1,0:T(8,128)(2,1)S(1)}, bf16[48,4096]{1,0:T(8,128)(2,1)S(1)}, u32[]{:S(2)}, u32[]{:S(2)}) %collective-permute-start.2) | collective-permute-done | bytes 393248 | tf_op jit(solution)/shard_map/ppermute | solution.py:134
  51.1 1.9 %collective-permute-start.12 = (bf16[64,4096]{1,0:T(8,128)(2,1)S(1)}, bf16[64,4096]{1,0:T(8,128)(2,1)S(1)}, u32[]{:S(2)}, u32[]{:S(2)}) collective-permute-start(bf16[64,4096]{1,0:T(8,128)(2,1)S(1)} %pad_maximum_fusion.3), channel_id=1, source_target_pairs={{0,3},{1,2},{2,1},{3,0},{4,7},{5,6},{6,5},{7,4},{8,11},{9,10},{10,... | collective-permute-start | bytes 1572872 | tf_op jit(solution)/shard_map/ppermute | solution.py:134
  53.1 2.2 %collective-permute-start.10 = (bf16[64,4096]{1,0:T(8,128)(2,1)S(1)}, bf16[64,4096]{1,0:T(8,128)(2,1)S(1)}, u32[]{:S(2)}, u32[]{:S(2)}) collective-permute-start(bf16[64,4096]{1,0:T(8,128)(2,1)S(1)} %collective-permute-done.8.refs_2_), channel_id=1, source_target_pairs={{0,3},{1,2},{2,1},{3,0},{4,7},{5,6},{6,5},{7,4},{8,11},{9,10},{10,... | collective-permute-start | bytes 1572872 | tf_op jit(solution)/shard_map/ppermute | solution.py:134
  55.3 6.1 %shard_map.67.refs_5_ = bf16[1024,1792]{1,0:T(8,128)(2,1)} custom-call(s32[268]{0:T(512)S(1)} %shard_map.64.table_ref, bf16[48,4096]{1,0:T(8,128)(2,1)S(1)} %collective-permute-done.2.refs_0_, bf16[96,4096]{1,0:T(8,128)(2,1)S(1)} %collective-permute-done.5.refs_1_, ...), custom_call_target="tpu_custom_call", output_to_operand_aliasing={{}: (6, {})} | custom-call | flops 9539999744 | bytes 745472 | tf_op jit(solution)/shard_map/pallas_call | solution.py:111
  61.4 5.9 %collective-permute-done.7.refs_0_ = bf16[48,4096]{1,0:T(8,128)(2,1)S(1)} collective-permute-done((bf16[48,4096]{1,0:T(8,128)(2,1)S(1)}, bf16[48,4096]{1,0:T(8,128)(2,1)S(1)}, u32[]{:S(2)}, u32[]{:S(2)}) %collective-permute-start.7) | collective-permute-done | bytes 393248 | tf_op jit(solution)/shard_map/ppermute | solution.py:134
  67.4 1.2 %collective-permute-start.9 = (bf16[96,4096]{1,0:T(8,128)(2,1)S(1)}, bf16[96,4096]{1,0:T(8,128)(2,1)S(1)}, u32[]{:S(2)}, u32[]{:S(2)}) collective-permute-start(bf16[96,4096]{1,0:T(8,128)(2,1)S(1)} %pad_maximum_fusion.2), channel_id=1, source_target_pairs={{0,12},{1,13},{2,14},{3,15},{4,8},{5,9},{6,10},{7,11},{8,4},{9,5},... | collective-permute-start | bytes 2359304 | tf_op jit(solution)/shard_map/ppermute | solution.py:134
  70.6 8.0 %shard_map.68.refs_4_ = bf16[1024,1792]{1,0:T(8,128)(2,1)} custom-call(s32[268]{0:T(512)S(1)} %shard_map.64.table_ref, bf16[48,4096]{1,0:T(8,128)(2,1)S(1)} %collective-permute-done.7.refs_0_, bf16[192,4096]{1,0:T(8,128)(2,1)S(1)} %collective-permute-done.11.refs_1_, ...), custom_call_target="tpu_custom_call", output_to_operand_aliasing={{}: (6, {})} | custom-call | flops 12419999744 | bytes 1089536 | tf_op jit(solution)/shard_map/pallas_call | solution.py:111
  78.6 2.1 %collective-permute-done.9.refs_0_ = bf16[96,4096]{1,0:T(8,128)(2,1)S(1)} collective-permute-done((bf16[96,4096]{1,0:T(8,128)(2,1)S(1)}, bf16[96,4096]{1,0:T(8,128)(2,1)S(1)}, u32[]{:S(2)}, u32[]{:S(2)}) %collective-permute-start.9) | collective-permute-done | bytes 786464 | tf_op jit(solution)/shard_map/ppermute | solution.py:134
  80.7 5.0 %shard_map.69 = bf16[1024,1792]{1,0:T(8,128)(2,1)} custom-call(s32[268]{0:T(512)S(1)} %shard_map.64.table_ref, bf16[96,4096]{1,0:T(8,128)(2,1)S(1)} %collective-permute-done.9.refs_0_, bf16[64,4096]{1,0:T(8,128)(2,1)S(1)} %collective-permute-done.10.refs_1_, bf16[14,9,128,128]{3,2,1,0:T(8,128)(2,1)S(1)} %copy-done.1, ...), custom_call_target="tpu_custom_call", output_to_operand_aliasing={{}: (5, {})} | custom-call | flops 8099999744 | bytes 573440 | tf_op jit(solution)/shard_map/pallas_call | solution.py:111
  (31 shorter events, 6.4 us)
Async XLA Ops:
  0.0 19.4 %collective-permute-start.1 = (bf16[64,4096]{1,0:T(8,128)(2,1)}, bf16[64,4096]{1,0:T(8,128)(2,1)S(1)}, u32[]{:S(2)}, u32[]{:S(2)}) collective-permute-start(bf16[64,4096]{1,0:T(8,128)(2,1)} %refs_0_.2), channel_id=1, source_target_pairs={{0,4},{1,5},{2,6},{3,7},{4,0},{5,1},{6,2},{7,3},{8,12},{9,13},{10,... | collective-permute-start | bytes 1572872 | tf_op jit(solution)/shard_map/ppermute | solution.py:134
  1.6 17.8 %copy-start.4 = (bf16[64,4096]{1,0:T(8,128)(2,1)S(1)}, bf16[64,4096]{1,0:T(8,128)(2,1)}, u32[]{:S(2)}) copy-start(bf16[64,4096]{1,0:T(8,128)(2,1)} %refs_0_.2) | copy-start | bytes 1572868
  2.7 23.7 %collective-permute-start.3 = (bf16[48,4096]{1,0:T(8,128)(2,1)S(1)}, bf16[48,4096]{1,0:T(8,128)(2,1)S(1)}, u32[]{:S(2)}, u32[]{:S(2)}) collective-permute-start(bf16[48,4096]{1,0:T(8,128)(2,1)S(1)} %slice_bitcast_fusion), channel_id=1, source_target_pairs={{0,3},{1,2},{2,1},{3,0},{4,7},{5,6},{6,5},{7,4},{8,11},{9,10},{10,... | collective-permute-start | bytes 1179656 | tf_op jit(solution)/shard_map/ppermute | solution.py:134
  9.1 17.3 %collective-permute-start = (bf16[48,4096]{1,0:T(8,128)(2,1)S(1)}, bf16[48,4096]{1,0:T(8,128)(2,1)S(1)}, u32[]{:S(2)}, u32[]{:S(2)}) collective-permute-start(bf16[48,4096]{1,0:T(8,128)(2,1)S(1)} %slice_bitcast_fusion), channel_id=1, source_target_pairs={{0,1},{1,0},{2,3},{3,2},{4,5},{5,4},{6,7},{7,6},{8,9},{9,8},{10,11... | collective-permute-start | bytes 1179656 | tf_op jit(solution)/shard_map/ppermute | solution.py:134
  10.6 10.6 %collective-permute-start.6 = (bf16[64,4096]{1,0:T(8,128)(2,1)}, bf16[64,4096]{1,0:T(8,128)(2,1)S(1)}, u32[]{:S(2)}, u32[]{:S(2)}) collective-permute-start(bf16[64,4096]{1,0:T(8,128)(2,1)} %refs_0_.2), channel_id=1, source_target_pairs={{0,12},{1,13},{2,14},{3,15},{4,8},{5,9},{6,10},{7,11},{8,4},{9,5},... | collective-permute-start | bytes 1572872 | tf_op jit(solution)/shard_map/ppermute | solution.py:134
  15.1 2.2 %copy-start = (bf16[14,9,128,128]{3,2,1,0:T(8,128)(2,1)S(1)}, bf16[14,9,128,128]{3,2,1,0:T(8,128)(2,1)}, u32[]{:S(2)}) copy-start(bf16[14,9,128,128]{3,2,1,0:T(8,128)(2,1)} %refs_2_.3) | copy-start | bytes 12386308
  17.2 2.2 %copy-start.2 = (bf16[14,9,128,128]{3,2,1,0:T(8,128)(2,1)S(1)}, bf16[14,9,128,128]{3,2,1,0:T(8,128)(2,1)}, u32[]{:S(2)}) copy-start(bf16[14,9,128,128]{3,2,1,0:T(8,128)(2,1)} %refs_3_.5) | copy-start | bytes 12386308
  19.4 2.2 %copy-start.1 = (bf16[14,9,128,128]{3,2,1,0:T(8,128)(2,1)S(1)}, bf16[14,9,128,128]{3,2,1,0:T(8,128)(2,1)}, u32[]{:S(2)}) copy-start(bf16[14,9,128,128]{3,2,1,0:T(8,128)(2,1)} %refs_2_.3) | copy-start | bytes 12386308
  19.4 3.4 %copy-start.3 = (bf16[14,9,128,128]{3,2,1,0:T(8,128)(2,1)S(1)}, bf16[14,9,128,128]{3,2,1,0:T(8,128)(2,1)}, u32[]{:S(2)}) copy-start(bf16[14,9,128,128]{3,2,1,0:T(8,128)(2,1)} %refs_3_.5) | copy-start | bytes 12386308
  19.5 11.1 %collective-permute-start.4 = (bf16[64,4096]{1,0:T(8,128)(2,1)S(1)}, bf16[64,4096]{1,0:T(8,128)(2,1)S(1)}, u32[]{:S(2)}, u32[]{:S(2)}) collective-permute-start(bf16[64,4096]{1,0:T(8,128)(2,1)S(1)} %collective-permute-done.1.refs_0_), channel_id=1, source_target_pairs={{0,12},{1,13},{2,14},{3,15},{4,8},{5,9},{6,10},{7,11},{8,4},{9,5},... | collective-permute-start | bytes 1572872 | tf_op jit(solution)/shard_map/ppermute | solution.py:134
  26.4 24.8 %collective-permute-start.2 = (bf16[48,4096]{1,0:T(8,128)(2,1)S(1)}, bf16[48,4096]{1,0:T(8,128)(2,1)S(1)}, u32[]{:S(2)}, u32[]{:S(2)}) collective-permute-start(bf16[48,4096]{1,0:T(8,128)(2,1)S(1)} %collective-permute-done.refs_3_), channel_id=1, source_target_pairs={{0,3},{1,2},{2,1},{3,0},{4,7},{5,6},{6,5},{7,4},{8,11},{9,10},{10,... | collective-permute-start | bytes 1179656 | tf_op jit(solution)/shard_map/ppermute | solution.py:134
  30.6 22.5 %collective-permute-start.8 = (bf16[64,4096]{1,0:T(8,128)(2,1)S(1)}, bf16[64,4096]{1,0:T(8,128)(2,1)S(1)}, u32[]{:S(2)}, u32[]{:S(2)}) collective-permute-start(bf16[64,4096]{1,0:T(8,128)(2,1)S(1)} %pad_maximum_fusion.3), channel_id=1, source_target_pairs={{0,1},{1,0},{2,3},{3,2},{4,5},{5,4},{6,7},{7,6},{8,9},{9,8},{10,11... | collective-permute-start | bytes 1572872 | tf_op jit(solution)/shard_map/ppermute | solution.py:134
  32.5 12.0 %collective-permute-start.5 = (bf16[96,4096]{1,0:T(8,128)(2,1)S(1)}, bf16[96,4096]{1,0:T(8,128)(2,1)S(1)}, u32[]{:S(2)}, u32[]{:S(2)}) collective-permute-start(bf16[96,4096]{1,0:T(8,128)(2,1)S(1)} %pad_maximum_fusion.1), channel_id=1, source_target_pairs={{0,4},{1,5},{2,6},{3,7},{4,0},{5,1},{6,2},{7,3},{8,12},{9,13},{10,... | collective-permute-start | bytes 2359304 | tf_op jit(solution)/shard_map/ppermute | solution.py:134
  44.6 25.9 %collective-permute-start.11 = (bf16[192,4096]{1,0:T(8,128)(2,1)S(1)}, bf16[192,4096]{1,0:T(8,128)(2,1)S(1)}, u32[]{:S(2)}, u32[]{:S(2)}) collective-permute-start(bf16[192,4096]{1,0:T(8,128)(2,1)S(1)} %pad_maximum_fusion), channel_id=1, source_target_pairs={{0,12},{1,13},{2,14},{3,15},{4,8},{5,9},{6,10},{7,11},{8,4},{9,5},... | collective-permute-start | bytes 4718600 | tf_op jit(solution)/shard_map/ppermute | solution.py:134
  51.1 18.5 %collective-permute-start.12 = (bf16[64,4096]{1,0:T(8,128)(2,1)S(1)}, bf16[64,4096]{1,0:T(8,128)(2,1)S(1)}, u32[]{:S(2)}, u32[]{:S(2)}) collective-permute-start(bf16[64,4096]{1,0:T(8,128)(2,1)S(1)} %pad_maximum_fusion.3), channel_id=1, source_target_pairs={{0,3},{1,2},{2,1},{3,0},{4,7},{5,6},{6,5},{7,4},{8,11},{9,10},{10,... | collective-permute-start | bytes 1572872 | tf_op jit(solution)/shard_map/ppermute | solution.py:134
  53.1 25.5 %collective-permute-start.10 = (bf16[64,4096]{1,0:T(8,128)(2,1)S(1)}, bf16[64,4096]{1,0:T(8,128)(2,1)S(1)}, u32[]{:S(2)}, u32[]{:S(2)}) collective-permute-start(bf16[64,4096]{1,0:T(8,128)(2,1)S(1)} %collective-permute-done.8.refs_2_), channel_id=1, source_target_pairs={{0,3},{1,2},{2,1},{3,0},{4,7},{5,6},{6,5},{7,4},{8,11},{9,10},{10,... | collective-permute-start | bytes 1572872 | tf_op jit(solution)/shard_map/ppermute | solution.py:134
  55.3 12.1 %collective-permute-start.7 = (bf16[48,4096]{1,0:T(8,128)(2,1)S(1)}, bf16[48,4096]{1,0:T(8,128)(2,1)S(1)}, u32[]{:S(2)}, u32[]{:S(2)}) collective-permute-start(bf16[48,4096]{1,0:T(8,128)(2,1)S(1)} %collective-permute-done.2.refs_0_), channel_id=1, source_target_pairs={{0,4},{1,5},{2,6},{3,7},{4,0},{5,1},{6,2},{7,3},{8,12},{9,13},{10,... | collective-permute-start | bytes 1179656 | tf_op jit(solution)/shard_map/ppermute | solution.py:134
  67.4 13.3 %collective-permute-start.9 = (bf16[96,4096]{1,0:T(8,128)(2,1)S(1)}, bf16[96,4096]{1,0:T(8,128)(2,1)S(1)}, u32[]{:S(2)}, u32[]{:S(2)}) collective-permute-start(bf16[96,4096]{1,0:T(8,128)(2,1)S(1)} %pad_maximum_fusion.2), channel_id=1, source_target_pairs={{0,12},{1,13},{2,14},{3,15},{4,8},{5,9},{6,10},{7,11},{8,4},{9,5},... | collective-permute-start | bytes 2359304 | tf_op jit(solution)/shard_map/ppermute | solution.py:134

commit v7 on v6

--- a/solution.py
+++ b/solution.py
@@ -154,19 +154,21 @@
         y2 = swap(after(own, mine), "y", 1)
         y3 = swap(after(y1, table), "y", 1)
         result = run([after(own, y1)], None)
-        z1, z2 = after(z1, y1, result), after(z2, y1, result)
+        z1, z2 = after(z1, y3, result), after(z2, y3, result)
         z3 = swap(z1, "z", 1)
         pair = joined(z1, z2)
         p1 = swap(after(pair, y3), "y", 0)
         column = joined(*[p.part(0, TURNED) for p in (own, y1, y2, y3)])
         b1 = swap(column, "z", 0)
         result = run([y1, after(y2, column), y3, z1, z2], result)
-        p2 = swap(after(joined(pair, p1), result), "y", 1)
+        p2 = swap(after(pair, result), "y", 1)
+        p3 = swap(after(p1, result), "y", 1)
+        result = run([after(p1, result)], result)
         q1 = swap(after(z3, p1, result), "y", 0)
         b2 = swap(after(column, z3, result), "z", 1)
         b3 = swap(after(b1, z3, result), "z", 1)
         q2 = swap(after(joined(z3, q1), b1), "y", 1)
-        for pieces in ([z3, p1, b1], [q1, p2, b2], [q2, b3]):
+        for pieces in ([z3, after(p2, q1), b1], [p3, q1, b2], [q2, b3]):
             result = run(pieces, result)
         return result
 

time: 86.1 us -> 86.7 us (level); the launches traced: 85.9 us -> 85.2 us
  starting transfers between devices: 27.2 us -> 24.4 us
  Pallas kernels: 30.2 us -> 32.2 us
    ppermute x13 -> x14, starting transfers between devices: 27.2 us -> 24.4 us  [swap(): rows = lax.ppermute(piece.rows, AXES, pairs)]
    pallas_call x5 -> x6, Pallas kernels: 30.2 us -> 32.2 us  [project(): pl.pallas_call(functools.partial(project_kernel, layout, starts, len(prev...]
    ppermute x13 -> x14, waiting for transfers between devices: 18.3 us -> 18.6 us  [swap(): rows = lax.ppermute(piece.rows, AXES, pairs)]
    unnamed x10 -> x11, local copies, waits for them, and re-layouts: 6.02 us -> 6.03 us
  transfers between devices with their start and end apart: 13 -> 14, of which waited for: 7 -> 6; matrix products, arithmetic and copies ran while one was open for 4% -> 4% of each run, Pallas kernels for 29% -> 32%
where the time goes in v7:
time: 86.7 us; the launch traced here: 85.2 us
  Pallas kernels  32.2 us (37%)
  starting transfers between devices  24.4 us (28%)
  waiting for transfers between devices  18.6 us (21%)
  local copies, waits for them, and re-layouts  8.78 us (10%)
    pallas_call x6, Pallas kernels, project(): pl.pallas_call(functools.partial(project_kernel, layout, starts, len(prev...  32.2 us
    ppermute x14, starting transfers between devices, swap(): rows = lax.ppermute(piece.rows, AXES, pairs)  24.4 us
    ppermute x14, waiting for transfers between devices, swap(): rows = lax.ppermute(piece.rows, AXES, pairs)  18.6 us
    unnamed x11, local copies, waits for them, and re-layouts  6.03 us
  transfers between devices with their start and end apart: 14, of which 6 were waited for; matrix products, arithmetic and copies ran while one was open for 4% of the time, Pallas kernels for 32%

profile of v7, /device:TPU:4, one launch (start us, length us, event | category | flops | bytes accessed | tf_op | source)
XLA Modules:
  0.0 85.2 jit_solution(8815186436614622957)
XLA Ops:
  0.0 1.6 %collective-permute-start.1 = (bf16[64,4096]{1,0:T(8,128)(2,1)}, bf16[64,4096]{1,0:T(8,128)(2,1)S(1)}, u32[]{:S(2)}, u32[]{:S(2)}) collective-permute-start(bf16[64,4096]{1,0:T(8,128)(2,1)} %refs_0_.2), channel_id=1, source_target_pairs={{0,4},{1,5},{2,6},{3,7},{4,0},{5,1},{6,2},{7,3},{8,12},{9,13},{10,... | collective-permute-start | bytes 1572872 | tf_op jit(solution)/shard_map/ppermute | solution.py:134
  2.7 6.4 %collective-permute-start.4 = (bf16[48,4096]{1,0:T(8,128)(2,1)S(1)}, bf16[48,4096]{1,0:T(8,128)(2,1)S(1)}, u32[]{:S(2)}, u32[]{:S(2)}) collective-permute-start(bf16[48,4096]{1,0:T(8,128)(2,1)S(1)} %slice_bitcast_fusion), channel_id=1, source_target_pairs={{0,3},{1,2},{2,1},{3,0},{4,7},{5,6},{6,5},{7,4},{8,11},{9,10},{10,... | collective-permute-start | bytes 1179656 | tf_op jit(solution)/shard_map/ppermute | solution.py:134
  9.1 1.5 %collective-permute-start = (bf16[48,4096]{1,0:T(8,128)(2,1)S(1)}, bf16[48,4096]{1,0:T(8,128)(2,1)S(1)}, u32[]{:S(2)}, u32[]{:S(2)}) collective-permute-start(bf16[48,4096]{1,0:T(8,128)(2,1)S(1)} %slice_bitcast_fusion), channel_id=1, source_target_pairs={{0,1},{1,0},{2,3},{3,2},{4,5},{5,4},{6,7},{7,6},{8,9},{9,8},{10,11... | collective-permute-start | bytes 1179656 | tf_op jit(solution)/shard_map/ppermute | solution.py:134
  10.6 2.2 %collective-permute-start.6 = (bf16[64,4096]{1,0:T(8,128)(2,1)}, bf16[64,4096]{1,0:T(8,128)(2,1)S(1)}, u32[]{:S(2)}, u32[]{:S(2)}) collective-permute-start(bf16[64,4096]{1,0:T(8,128)(2,1)} %refs_0_.2), channel_id=1, source_target_pairs={{0,12},{1,13},{2,14},{3,15},{4,8},{5,9},{6,10},{7,11},{8,4},{9,5},... | collective-permute-start | bytes 1572872 | tf_op jit(solution)/shard_map/ppermute | solution.py:134
  15.1 2.2 %copy-done = bf16[14,9,128,128]{3,2,1,0:T(8,128)(2,1)S(1)} copy-done((bf16[14,9,128,128]{3,2,1,0:T(8,128)(2,1)S(1)}, bf16[14,9,128,128]{3,2,1,0:T(8,128)(2,1)}, u32[]{:S(2)}) %copy-start) | copy-done | bytes 4128792
  17.2 2.2 %copy-done.2 = bf16[14,9,128,128]{3,2,1,0:T(8,128)(2,1)S(1)} copy-done((bf16[14,9,128,128]{3,2,1,0:T(8,128)(2,1)S(1)}, bf16[14,9,128,128]{3,2,1,0:T(8,128)(2,1)}, u32[]{:S(2)}) %copy-start.2) | copy-done | bytes 4128792
  19.5 1.1 %collective-permute-start.2 = (bf16[64,4096]{1,0:T(8,128)(2,1)S(1)}, bf16[64,4096]{1,0:T(8,128)(2,1)S(1)}, u32[]{:S(2)}, u32[]{:S(2)}) collective-permute-start(bf16[64,4096]{1,0:T(8,128)(2,1)S(1)} %collective-permute-done.1.refs_0_), channel_id=1, source_target_pairs={{0,12},{1,13},{2,14},{3,15},{4,8},{5,9},{6,10},{7,11},{8,4},{9,5},... | collective-permute-start | bytes 1572872 | tf_op jit(solution)/shard_map/ppermute | solution.py:134
  21.6 1.3 %copy-done.3 = bf16[14,9,128,128]{3,2,1,0:T(8,128)(2,1)S(1)} copy-done((bf16[14,9,128,128]{3,2,1,0:T(8,128)(2,1)S(1)}, bf16[14,9,128,128]{3,2,1,0:T(8,128)(2,1)}, u32[]{:S(2)}) %copy-start.3) | copy-done | bytes 4128792
  22.8 3.5 %shard_map.65.refs_7_ = bf16[1024,1792]{1,0:T(8,128)(2,1)} custom-call(s32[268]{0:T(512)S(1)} %shard_map.64.table_ref, bf16[64,4096]{1,0:T(8,128)(2,1)S(1)} %copy-done.4, bf16[14,9,128,128]{3,2,1,0:T(8,128)(2,1)S(1)} %copy-done.1, bf16[14,9,128,128]{3,2,1,0:T(8,128)(2,1)S(1)} %copy-done.3), custom_call_target="tpu_custom_call" | custom-call | flops 5219999744 | bytes 229376 | tf_op jit(solution)/shard_map/pallas_call | solution.py:111
  26.4 3.6 %collective-permute-done.2.refs_2_ = bf16[64,4096]{1,0:T(8,128)(2,1)S(1)} collective-permute-done((bf16[64,4096]{1,0:T(8,128)(2,1)S(1)}, bf16[64,4096]{1,0:T(8,128)(2,1)S(1)}, u32[]{:S(2)}, u32[]{:S(2)}) %collective-permute-start.2) | collective-permute-done | bytes 524320 | tf_op jit(solution)/shard_map/ppermute | solution.py:134
  30.6 1.5 %collective-permute-start.8 = (bf16[64,4096]{1,0:T(8,128)(2,1)S(1)}, bf16[64,4096]{1,0:T(8,128)(2,1)S(1)}, u32[]{:S(2)}, u32[]{:S(2)}) collective-permute-start(bf16[64,4096]{1,0:T(8,128)(2,1)S(1)} %pad_maximum_fusion.1), channel_id=1, source_target_pairs={{0,1},{1,0},{2,3},{3,2},{4,5},{5,4},{6,7},{7,6},{8,9},{9,8},{10,11... | collective-permute-start | bytes 1572872 | tf_op jit(solution)/shard_map/ppermute | solution.py:134
  32.4 7.5 %shard_map.66.refs_3_ = bf16[1024,1792]{1,0:T(8,128)(2,1)} custom-call(s32[268]{0:T(512)S(1)} %shard_map.64.table_ref, bf16[64,4096]{1,0:T(8,128)(2,1)S(1)} %collective-permute-done.1.refs_0_, bf16[64,4096]{1,0:T(8,128)(2,1)S(1)} %collective-permute-done.6.refs_1_, ...), custom_call_target="tpu_custom_call", output_to_operand_aliasing={{}: (8, {})} | custom-call | flops 11939999744 | bytes 1032192 | tf_op jit(solution)/shard_map/pallas_call | solution.py:111
  39.9 2.9 %collective-permute-start.13 = (bf16[96,4096]{1,0:T(8,128)(2,1)S(1)}, bf16[96,4096]{1,0:T(8,128)(2,1)S(1)}, u32[]{:S(2)}, u32[]{:S(2)}) collective-permute-start(bf16[96,4096]{1,0:T(8,128)(2,1)S(1)} %constant_dynamic-update-slice_fusion), channel_id=1, source_target_pairs={{0,12},{1,13},{2,14},{3,15},{4,8},{5,9},{6,10},{7,11},{8,4},{9,5},... | collective-permute-start | bytes 2359304 | tf_op jit(solution)/shard_map/ppermute | solution.py:134
  42.8 1.8 %collective-permute-done.5.refs_0_ = bf16[96,4096]{1,0:T(8,128)(2,1)S(1)} collective-permute-done((bf16[96,4096]{1,0:T(8,128)(2,1)S(1)}, bf16[96,4096]{1,0:T(8,128)(2,1)S(1)}, u32[]{:S(2)}, u32[]{:S(2)}) %collective-permute-start.5) | collective-permute-done | bytes 786464 | tf_op jit(solution)/shard_map/ppermute | solution.py:134
  44.6 3.9 %shard_map.67.refs_5_ = bf16[1024,1792]{1,0:T(8,128)(2,1)} custom-call(s32[268]{0:T(512)S(1)} %shard_map.64.table_ref, bf16[96,4096]{1,0:T(8,128)(2,1)S(1)} %collective-permute-done.5.refs_0_, bf16[14,9,128,128]{3,2,1,0:T(8,128)(2,1)S(1)} %copy-done.1, bf16[14,9,128,128]{3,2,1,0:T(8,128)(2,1)S(1)} %copy-done.3, ...), custom_call_target="tpu_custom_call", output_to_operand_aliasing={{}: (4, {})} | custom-call | flops 6179999744 | bytes 344064 | tf_op jit(solution)/shard_map/pallas_call | solution.py:111
  48.5 3.6 %collective-permute-done.3.refs_0_ = bf16[48,4096]{1,0:T(8,128)(2,1)S(1)} collective-permute-done((bf16[48,4096]{1,0:T(8,128)(2,1)S(1)}, bf16[48,4096]{1,0:T(8,128)(2,1)S(1)}, u32[]{:S(2)}, u32[]{:S(2)}) %collective-permute-start.3) | collective-permute-done | bytes 393248 | tf_op jit(solution)/shard_map/ppermute | solution.py:134
  53.3 2.8 %collective-permute-start.12 = (bf16[64,4096]{1,0:T(8,128)(2,1)S(1)}, bf16[64,4096]{1,0:T(8,128)(2,1)S(1)}, u32[]{:S(2)}, u32[]{:S(2)}) collective-permute-start(bf16[64,4096]{1,0:T(8,128)(2,1)S(1)} %pad_maximum_fusion.1), channel_id=1, source_target_pairs={{0,3},{1,2},{2,1},{3,0},{4,7},{5,6},{6,5},{7,4},{8,11},{9,10},{10,... | collective-permute-start | bytes 1572872 | tf_op jit(solution)/shard_map/ppermute | solution.py:134
  56.1 1.3 %collective-permute-start.10 = (bf16[64,4096]{1,0:T(8,128)(2,1)S(1)}, bf16[64,4096]{1,0:T(8,128)(2,1)S(1)}, u32[]{:S(2)}, u32[]{:S(2)}) collective-permute-start(bf16[64,4096]{1,0:T(8,128)(2,1)S(1)} %collective-permute-done.8.refs_2_), channel_id=1, source_target_pairs={{0,3},{1,2},{2,1},{3,0},{4,7},{5,6},{6,5},{7,4},{8,11},{9,10},{10,... | collective-permute-start | bytes 1572872 | tf_op jit(solution)/shard_map/ppermute | solution.py:134
  57.4 6.8 %collective-permute-done.7.refs_1_ = bf16[48,4096]{1,0:T(8,128)(2,1)S(1)} collective-permute-done((bf16[48,4096]{1,0:T(8,128)(2,1)S(1)}, bf16[48,4096]{1,0:T(8,128)(2,1)S(1)}, u32[]{:S(2)}, u32[]{:S(2)}) %collective-permute-start.7) | collective-permute-done | bytes 393248 | tf_op jit(solution)/shard_map/ppermute | solution.py:134
  64.2 1.2 %collective-permute-start.9 = (bf16[96,4096]{1,0:T(8,128)(2,1)S(1)}, bf16[96,4096]{1,0:T(8,128)(2,1)S(1)}, u32[]{:S(2)}, u32[]{:S(2)}) collective-permute-start(bf16[96,4096]{1,0:T(8,128)(2,1)S(1)} %pad_maximum_fusion), channel_id=1, source_target_pairs={{0,12},{1,13},{2,14},{3,15},{4,8},{5,9},{6,10},{7,11},{8,4},{9,5},... | collective-permute-start | bytes 2359304 | tf_op jit(solution)/shard_map/ppermute | solution.py:134
  65.5 6.1 %shard_map.68.refs_5_ = bf16[1024,1792]{1,0:T(8,128)(2,1)} custom-call(s32[268]{0:T(512)S(1)} %shard_map.64.table_ref, bf16[48,4096]{1,0:T(8,128)(2,1)S(1)} %collective-permute-done.3.refs_0_, bf16[96,4096]{1,0:T(8,128)(2,1)S(1)} %collective-permute-done.13.refs_1_, ...), custom_call_target="tpu_custom_call", output_to_operand_aliasing={{}: (6, {})} | custom-call | flops 9539999744 | bytes 745472 | tf_op jit(solution)/shard_map/pallas_call | solution.py:111
  71.6 6.2 %shard_map.69.refs_4_ = bf16[1024,1792]{1,0:T(8,128)(2,1)} custom-call(s32[268]{0:T(512)S(1)} %shard_map.64.table_ref, bf16[96,4096]{1,0:T(8,128)(2,1)S(1)} %collective-permute-done.11.refs_0_, bf16[48,4096]{1,0:T(8,128)(2,1)S(1)} %collective-permute-done.7.refs_1_, ...), custom_call_target="tpu_custom_call", output_to_operand_aliasing={{}: (6, {})} | custom-call | flops 9539999744 | bytes 745472 | tf_op jit(solution)/shard_map/pallas_call | solution.py:111
  77.8 2.2 %collective-permute-done.10.refs_1_ = bf16[64,4096]{1,0:T(8,128)(2,1)S(1)} collective-permute-done((bf16[64,4096]{1,0:T(8,128)(2,1)S(1)}, bf16[64,4096]{1,0:T(8,128)(2,1)S(1)}, u32[]{:S(2)}, u32[]{:S(2)}) %collective-permute-start.10) | collective-permute-done | bytes 524320 | tf_op jit(solution)/shard_map/ppermute | solution.py:134
  80.0 5.0 %shard_map.70 = bf16[1024,1792]{1,0:T(8,128)(2,1)} custom-call(s32[268]{0:T(512)S(1)} %shard_map.64.table_ref, bf16[96,4096]{1,0:T(8,128)(2,1)S(1)} %collective-permute-done.9.refs_0_, bf16[64,4096]{1,0:T(8,128)(2,1)S(1)} %collective-permute-done.10.refs_1_, bf16[14,9,128,128]{3,2,1,0:T(8,128)(2,1)S(1)} %copy-done.1, ...), custom_call_target="tpu_custom_call", output_to_operand_aliasing={{}: (5, {})} | custom-call | flops 8099999744 | bytes 573440 | tf_op jit(solution)/shard_map/pallas_call | solution.py:111
  (34 shorter events, 6.5 us)
Async XLA Ops:
  0.0 19.4 %collective-permute-start.1 = (bf16[64,4096]{1,0:T(8,128)(2,1)}, bf16[64,4096]{1,0:T(8,128)(2,1)S(1)}, u32[]{:S(2)}, u32[]{:S(2)}) collective-permute-start(bf16[64,4096]{1,0:T(8,128)(2,1)} %refs_0_.2), channel_id=1, source_target_pairs={{0,4},{1,5},{2,6},{3,7},{4,0},{5,1},{6,2},{7,3},{8,12},{9,13},{10,... | collective-permute-start | bytes 1572872 | tf_op jit(solution)/shard_map/ppermute | solution.py:134
  1.6 17.8 %copy-start.4 = (bf16[64,4096]{1,0:T(8,128)(2,1)S(1)}, bf16[64,4096]{1,0:T(8,128)(2,1)}, u32[]{:S(2)}) copy-start(bf16[64,4096]{1,0:T(8,128)(2,1)} %refs_0_.2) | copy-start | bytes 1572868
  2.7 27.8 %collective-permute-start.4 = (bf16[48,4096]{1,0:T(8,128)(2,1)S(1)}, bf16[48,4096]{1,0:T(8,128)(2,1)S(1)}, u32[]{:S(2)}, u32[]{:S(2)}) collective-permute-start(bf16[48,4096]{1,0:T(8,128)(2,1)S(1)} %slice_bitcast_fusion), channel_id=1, source_target_pairs={{0,3},{1,2},{2,1},{3,0},{4,7},{5,6},{6,5},{7,4},{8,11},{9,10},{10,... | collective-permute-start | bytes 1179656 | tf_op jit(solution)/shard_map/ppermute | solution.py:134
  9.1 17.3 %collective-permute-start = (bf16[48,4096]{1,0:T(8,128)(2,1)S(1)}, bf16[48,4096]{1,0:T(8,128)(2,1)S(1)}, u32[]{:S(2)}, u32[]{:S(2)}) collective-permute-start(bf16[48,4096]{1,0:T(8,128)(2,1)S(1)} %slice_bitcast_fusion), channel_id=1, source_target_pairs={{0,1},{1,0},{2,3},{3,2},{4,5},{5,4},{6,7},{7,6},{8,9},{9,8},{10,11... | collective-permute-start | bytes 1179656 | tf_op jit(solution)/shard_map/ppermute | solution.py:134
  10.6 10.6 %collective-permute-start.6 = (bf16[64,4096]{1,0:T(8,128)(2,1)}, bf16[64,4096]{1,0:T(8,128)(2,1)S(1)}, u32[]{:S(2)}, u32[]{:S(2)}) collective-permute-start(bf16[64,4096]{1,0:T(8,128)(2,1)} %refs_0_.2), channel_id=1, source_target_pairs={{0,12},{1,13},{2,14},{3,15},{4,8},{5,9},{6,10},{7,11},{8,4},{9,5},... | collective-permute-start | bytes 1572872 | tf_op jit(solution)/shard_map/ppermute | solution.py:134
  15.1 2.2 %copy-start = (bf16[14,9,128,128]{3,2,1,0:T(8,128)(2,1)S(1)}, bf16[14,9,128,128]{3,2,1,0:T(8,128)(2,1)}, u32[]{:S(2)}) copy-start(bf16[14,9,128,128]{3,2,1,0:T(8,128)(2,1)} %refs_2_.5) | copy-start | bytes 12386308
  17.2 2.2 %copy-start.2 = (bf16[14,9,128,128]{3,2,1,0:T(8,128)(2,1)S(1)}, bf16[14,9,128,128]{3,2,1,0:T(8,128)(2,1)}, u32[]{:S(2)}) copy-start(bf16[14,9,128,128]{3,2,1,0:T(8,128)(2,1)} %refs_3_.5) | copy-start | bytes 12386308
  19.4 2.2 %copy-start.1 = (bf16[14,9,128,128]{3,2,1,0:T(8,128)(2,1)S(1)}, bf16[14,9,128,128]{3,2,1,0:T(8,128)(2,1)}, u32[]{:S(2)}) copy-start(bf16[14,9,128,128]{3,2,1,0:T(8,128)(2,1)} %refs_2_.5) | copy-start | bytes 12386308
  19.4 3.4 %copy-start.3 = (bf16[14,9,128,128]{3,2,1,0:T(8,128)(2,1)S(1)}, bf16[14,9,128,128]{3,2,1,0:T(8,128)(2,1)}, u32[]{:S(2)}) copy-start(bf16[14,9,128,128]{3,2,1,0:T(8,128)(2,1)} %refs_3_.5) | copy-start | bytes 12386308
  19.5 10.5 %collective-permute-start.2 = (bf16[64,4096]{1,0:T(8,128)(2,1)S(1)}, bf16[64,4096]{1,0:T(8,128)(2,1)S(1)}, u32[]{:S(2)}, u32[]{:S(2)}) collective-permute-start(bf16[64,4096]{1,0:T(8,128)(2,1)S(1)} %collective-permute-done.1.refs_0_), channel_id=1, source_target_pairs={{0,12},{1,13},{2,14},{3,15},{4,8},{5,9},{6,10},{7,11},{8,4},{9,5},... | collective-permute-start | bytes 1572872 | tf_op jit(solution)/shard_map/ppermute | solution.py:134
  29.9 22.2 %collective-permute-start.3 = (bf16[48,4096]{1,0:T(8,128)(2,1)S(1)}, bf16[48,4096]{1,0:T(8,128)(2,1)S(1)}, u32[]{:S(2)}, u32[]{:S(2)}) collective-permute-start(bf16[48,4096]{1,0:T(8,128)(2,1)S(1)} %collective-permute-done.refs_3_), channel_id=1, source_target_pairs={{0,3},{1,2},{2,1},{3,0},{4,7},{5,6},{6,5},{7,4},{8,11},{9,10},{10,... | collective-permute-start | bytes 1179656 | tf_op jit(solution)/shard_map/ppermute | solution.py:134
  30.6 22.7 %collective-permute-start.8 = (bf16[64,4096]{1,0:T(8,128)(2,1)S(1)}, bf16[64,4096]{1,0:T(8,128)(2,1)S(1)}, u32[]{:S(2)}, u32[]{:S(2)}) collective-permute-start(bf16[64,4096]{1,0:T(8,128)(2,1)S(1)} %pad_maximum_fusion.1), channel_id=1, source_target_pairs={{0,1},{1,0},{2,3},{3,2},{4,5},{5,4},{6,7},{7,6},{8,9},{9,8},{10,11... | collective-permute-start | bytes 1572872 | tf_op jit(solution)/shard_map/ppermute | solution.py:134
  32.1 12.5 %collective-permute-start.5 = (bf16[96,4096]{1,0:T(8,128)(2,1)S(1)}, bf16[96,4096]{1,0:T(8,128)(2,1)S(1)}, u32[]{:S(2)}, u32[]{:S(2)}) collective-permute-start(bf16[96,4096]{1,0:T(8,128)(2,1)S(1)} %constant_dynamic-update-slice_fusion), channel_id=1, source_target_pairs={{0,4},{1,5},{2,6},{3,7},{4,0},{5,1},{6,2},{7,3},{8,12},{9,13},{10,... | collective-permute-start | bytes 2359304 | tf_op jit(solution)/shard_map/ppermute | solution.py:134
  39.9 17.5 %collective-permute-start.13 = (bf16[96,4096]{1,0:T(8,128)(2,1)S(1)}, bf16[96,4096]{1,0:T(8,128)(2,1)S(1)}, u32[]{:S(2)}, u32[]{:S(2)}) collective-permute-start(bf16[96,4096]{1,0:T(8,128)(2,1)S(1)} %constant_dynamic-update-slice_fusion), channel_id=1, source_target_pairs={{0,12},{1,13},{2,14},{3,15},{4,8},{5,9},{6,10},{7,11},{8,4},{9,5},... | collective-permute-start | bytes 2359304 | tf_op jit(solution)/shard_map/ppermute | solution.py:134
  52.1 12.1 %collective-permute-start.7 = (bf16[48,4096]{1,0:T(8,128)(2,1)S(1)}, bf16[48,4096]{1,0:T(8,128)(2,1)S(1)}, u32[]{:S(2)}, u32[]{:S(2)}) collective-permute-start(bf16[48,4096]{1,0:T(8,128)(2,1)S(1)} %collective-permute-done.3.refs_0_), channel_id=1, source_target_pairs={{0,4},{1,5},{2,6},{3,7},{4,0},{5,1},{6,2},{7,3},{8,12},{9,13},{10,... | collective-permute-start | bytes 1179656 | tf_op jit(solution)/shard_map/ppermute | solution.py:134
  52.1 19.5 %collective-permute-start.11 = (bf16[96,4096]{1,0:T(8,128)(2,1)S(1)}, bf16[96,4096]{1,0:T(8,128)(2,1)S(1)}, u32[]{:S(2)}, u32[]{:S(2)}) collective-permute-start(bf16[96,4096]{1,0:T(8,128)(2,1)S(1)} %collective-permute-done.5.refs_0_), channel_id=1, source_target_pairs={{0,12},{1,13},{2,14},{3,15},{4,8},{5,9},{6,10},{7,11},{8,4},{9,5},... | collective-permute-start | bytes 2359304 | tf_op jit(solution)/shard_map/ppermute | solution.py:134
  53.3 18.3 %collective-permute-start.12 = (bf16[64,4096]{1,0:T(8,128)(2,1)S(1)}, bf16[64,4096]{1,0:T(8,128)(2,1)S(1)}, u32[]{:S(2)}, u32[]{:S(2)}) collective-permute-start(bf16[64,4096]{1,0:T(8,128)(2,1)S(1)} %pad_maximum_fusion.1), channel_id=1, source_target_pairs={{0,3},{1,2},{2,1},{3,0},{4,7},{5,6},{6,5},{7,4},{8,11},{9,10},{10,... | collective-permute-start | bytes 1572872 | tf_op jit(solution)/shard_map/ppermute | solution.py:134
  56.1 23.9 %collective-permute-start.10 = (bf16[64,4096]{1,0:T(8,128)(2,1)S(1)}, bf16[64,4096]{1,0:T(8,128)(2,1)S(1)}, u32[]{:S(2)}, u32[]{:S(2)}) collective-permute-start(bf16[64,4096]{1,0:T(8,128)(2,1)S(1)} %collective-permute-done.8.refs_2_), channel_id=1, source_target_pairs={{0,3},{1,2},{2,1},{3,0},{4,7},{5,6},{6,5},{7,4},{8,11},{9,10},{10,... | collective-permute-start | bytes 1572872 | tf_op jit(solution)/shard_map/ppermute | solution.py:134
  64.2 15.7 %collective-permute-start.9 = (bf16[96,4096]{1,0:T(8,128)(2,1)S(1)}, bf16[96,4096]{1,0:T(8,128)(2,1)S(1)}, u32[]{:S(2)}, u32[]{:S(2)}) collective-permute-start(bf16[96,4096]{1,0:T(8,128)(2,1)S(1)} %pad_maximum_fusion), channel_id=1, source_target_pairs={{0,12},{1,13},{2,14},{3,15},{4,8},{5,9},{6,10},{7,11},{8,4},{9,5},... | collective-permute-start | bytes 2359304 | tf_op jit(solution)/shard_map/ppermute | solution.py:134

commit v8 on v6

--- a/solution.py
+++ b/solution.py
@@ -13,7 +13,7 @@
 AXES = ("dp", "tensor")
 TURNED = 16
 UNROLL = 7
-COST = 30_000_000
+COST = 24_000_000
 
 
 STEPS = {("y", 0): 1, ("y", 1): 2, ("z", 0): 4, ("z", 1): 8}
@@ -165,8 +165,9 @@
         q1 = swap(after(z3, p1, result), "y", 0)
         b2 = swap(after(column, z3, result), "z", 1)
         b3 = swap(after(b1, z3, result), "z", 1)
-        q2 = swap(after(joined(z3, q1), b1), "y", 1)
-        for pieces in ([z3, p1, b1], [q1, p2, b2], [q2, b3]):
+        result = run([z3, p1, b1], result)
+        q2 = swap(after(joined(z3, q1), result), "y", 1)
+        for pieces in ([q1, p2, b2], [q2, b3]):
             result = run(pieces, result)
         return result
 

time: 86.1 us -> 93.9 us (1.091)
  the two profiles are of different devices: /device:TPU:4 before, /device:TPU:80 now
where the time goes in v8:
time: 93.9 us; the launch traced here: 93.7 us
  Pallas kernels  30.2 us (32%)
  waiting for transfers between devices  30 us (32%)
  starting transfers between devices  24.3 us (26%)
  local copies, waits for them, and re-layouts  7.77 us (8%)
  other arithmetic  1.06 us (1%)
    pallas_call x5, Pallas kernels, project(): pl.pallas_call(functools.partial(project_kernel, layout, starts, len(prev...  30.2 us
    ppermute x13, waiting for transfers between devices, swap(): rows = lax.ppermute(piece.rows, AXES, pairs)  30 us
    ppermute x13, starting transfers between devices, swap(): rows = lax.ppermute(piece.rows, AXES, pairs)  24.3 us
    unnamed x10, local copies, waits for them, and re-layouts  5.05 us
  transfers between devices with their start and end apart: 13, of which 7 were waited for; matrix products, arithmetic and copies ran while one was open for 4% of the time, Pallas kernels for 27%

profile of v8, /device:TPU:80, one launch (start us, length us, event | category | flops | bytes accessed | tf_op | source)
XLA Modules:
  0.0 93.7 jit_solution(14229537060945024828)
XLA Ops:
  0.0 1.3 %collective-permute-start.1 = (bf16[64,4096]{1,0:T(8,128)(2,1)}, bf16[64,4096]{1,0:T(8,128)(2,1)S(1)}, u32[]{:S(2)}, u32[]{:S(2)}) collective-permute-start(bf16[64,4096]{1,0:T(8,128)(2,1)} %refs_0_.2), channel_id=1, source_target_pairs={{0,4},{1,5},{2,6},{3,7},{4,0},{5,1},{6,2},{7,3},{8,12},{9,13},{10,... | collective-permute-start | bytes 1572872 | tf_op jit(solution)/shard_map/ppermute | solution.py:134
  1.3 1.1 %slice_bitcast_fusion = bf16[48,4096]{1,0:T(8,128)(2,1)S(1)} fusion(bf16[1,64,4096]{2,1,0:T(8,128)(2,1)} %bitcast.16), kind=kLoop, calls=%fused_computation.4 | loop fusion | bytes 786432 | tf_op jit(solution)/shard_map/reshape | solution.py:36
  2.5 5.9 %collective-permute-start.3 = (bf16[48,4096]{1,0:T(8,128)(2,1)S(1)}, bf16[48,4096]{1,0:T(8,128)(2,1)S(1)}, u32[]{:S(2)}, u32[]{:S(2)}) collective-permute-start(bf16[48,4096]{1,0:T(8,128)(2,1)S(1)} %slice_bitcast_fusion), channel_id=1, source_target_pairs={{0,3},{1,2},{2,1},{3,0},{4,7},{5,6},{6,5},{7,4},{8,11},{9,10},{10,... | collective-permute-start | bytes 1179656 | tf_op jit(solution)/shard_map/ppermute | solution.py:134
  8.5 0.8 reshape.38
  9.2 0.8 reshape.39
  10.8 2.2 %copy-done = bf16[14,9,128,128]{3,2,1,0:T(8,128)(2,1)S(1)} copy-done((bf16[14,9,128,128]{3,2,1,0:T(8,128)(2,1)S(1)}, bf16[14,9,128,128]{3,2,1,0:T(8,128)(2,1)}, u32[]{:S(2)}) %copy-start) | copy-done | bytes 4128792
  13.0 2.2 %copy-done.2 = bf16[14,9,128,128]{3,2,1,0:T(8,128)(2,1)S(1)} copy-done((bf16[14,9,128,128]{3,2,1,0:T(8,128)(2,1)S(1)}, bf16[14,9,128,128]{3,2,1,0:T(8,128)(2,1)}, u32[]{:S(2)}) %copy-start.2) | copy-done | bytes 4128792
  15.2 2.1 %collective-permute-start.4 = (bf16[64,4096]{1,0:T(8,128)(2,1)S(1)}, bf16[64,4096]{1,0:T(8,128)(2,1)S(1)}, u32[]{:S(2)}, u32[]{:S(2)}) collective-permute-start(bf16[64,4096]{1,0:T(8,128)(2,1)S(1)} %collective-permute-done.1.refs_0_), channel_id=1, source_target_pairs={{0,12},{1,13},{2,14},{3,15},{4,8},{5,9},{6,10},{7,11},{8,4},{9,5},... | collective-permute-start | bytes 1572872 | tf_op jit(solution)/shard_map/ppermute | solution.py:134
  18.6 3.5 %shard_map.65.refs_7_ = bf16[1024,1792]{1,0:T(8,128)(2,1)} custom-call(s32[268]{0:T(512)S(1)} %shard_map.64.table_ref, bf16[64,4096]{1,0:T(8,128)(2,1)S(1)} %copy-done.4, bf16[14,9,128,128]{3,2,1,0:T(8,128)(2,1)S(1)} %copy-done.1, bf16[14,9,128,128]{3,2,1,0:T(8,128)(2,1)S(1)} %copy-done.3), custom_call_target="tpu_custom_call" | custom-call | flops 4176000000 | bytes 229376 | tf_op jit(solution)/shard_map/pallas_call | solution.py:111
  22.1 1.3 %collective-permute-done.3.refs_4_ = bf16[48,4096]{1,0:T(8,128)(2,1)S(1)} collective-permute-done((bf16[48,4096]{1,0:T(8,128)(2,1)S(1)}, bf16[48,4096]{1,0:T(8,128)(2,1)S(1)}, u32[]{:S(2)}, u32[]{:S(2)}) %collective-permute-start.3) | collective-permute-done | bytes 393248 | tf_op jit(solution)/shard_map/ppermute | solution.py:134
  23.4 2.7 %collective-permute-start.2 = (bf16[48,4096]{1,0:T(8,128)(2,1)S(1)}, bf16[48,4096]{1,0:T(8,128)(2,1)S(1)}, u32[]{:S(2)}, u32[]{:S(2)}) collective-permute-start(bf16[48,4096]{1,0:T(8,128)(2,1)S(1)} %collective-permute-done.refs_3_), channel_id=1, source_target_pairs={{0,3},{1,2},{2,1},{3,0},{4,7},{5,6},{6,5},{7,4},{8,11},{9,10},{10,... | collective-permute-start | bytes 1179656 | tf_op jit(solution)/shard_map/ppermute | solution.py:134
  26.2 2.3 %collective-permute-start.5 = (bf16[96,4096]{1,0:T(8,128)(2,1)S(1)}, bf16[96,4096]{1,0:T(8,128)(2,1)S(1)}, u32[]{:S(2)}, u32[]{:S(2)}) collective-permute-start(bf16[96,4096]{1,0:T(8,128)(2,1)S(1)} %pad_maximum_fusion.1), channel_id=1, source_target_pairs={{0,4},{1,5},{2,6},{3,7},{4,0},{5,1},{6,2},{7,3},{8,12},{9,13},{10,... | collective-permute-start | bytes 2359304 | tf_op jit(solution)/shard_map/ppermute | solution.py:134
  28.6 1.6 %collective-permute-start.8 = (bf16[64,4096]{1,0:T(8,128)(2,1)S(1)}, bf16[64,4096]{1,0:T(8,128)(2,1)S(1)}, u32[]{:S(2)}, u32[]{:S(2)}) collective-permute-start(bf16[64,4096]{1,0:T(8,128)(2,1)S(1)} %pad_maximum_fusion.3), channel_id=1, source_target_pairs={{0,1},{1,0},{2,3},{3,2},{4,5},{5,4},{6,7},{7,6},{8,9},{9,8},{10,11... | collective-permute-start | bytes 1572872 | tf_op jit(solution)/shard_map/ppermute | solution.py:134
  30.2 7.5 %shard_map.66.refs_5_ = bf16[1024,1792]{1,0:T(8,128)(2,1)} custom-call(s32[268]{0:T(512)S(1)} %shard_map.64.table_ref, bf16[64,4096]{1,0:T(8,128)(2,1)S(1)} %collective-permute-done.1.refs_0_, bf16[64,4096]{1,0:T(8,128)(2,1)S(1)} %collective-permute-done.6.refs_1_, ...), custom_call_target="tpu_custom_call", output_to_operand_aliasing={{}: (8, {})} | custom-call | flops 9552000000 | bytes 1032192 | tf_op jit(solution)/shard_map/pallas_call | solution.py:111
  37.7 0.8 collective-permute-done.5.refs_1_
  38.7 3.5 %collective-permute-start.11 = (bf16[192,4096]{1,0:T(8,128)(2,1)S(1)}, bf16[192,4096]{1,0:T(8,128)(2,1)S(1)}, u32[]{:S(2)}, u32[]{:S(2)}) collective-permute-start(bf16[192,4096]{1,0:T(8,128)(2,1)S(1)} %pad_maximum_fusion), channel_id=1, source_target_pairs={{0,12},{1,13},{2,14},{3,15},{4,8},{5,9},{6,10},{7,11},{8,4},{9,5},... | collective-permute-start | bytes 4718600 | tf_op jit(solution)/shard_map/ppermute | solution.py:134
  42.2 4.9 %collective-permute-done.2.refs_0_ = bf16[48,4096]{1,0:T(8,128)(2,1)S(1)} collective-permute-done((bf16[48,4096]{1,0:T(8,128)(2,1)S(1)}, bf16[48,4096]{1,0:T(8,128)(2,1)S(1)}, u32[]{:S(2)}, u32[]{:S(2)}) %collective-permute-start.2) | collective-permute-done | bytes 393248 | tf_op jit(solution)/shard_map/ppermute | solution.py:134
  47.1 4.6 %collective-permute-start.12 = (bf16[64,4096]{1,0:T(8,128)(2,1)S(1)}, bf16[64,4096]{1,0:T(8,128)(2,1)S(1)}, u32[]{:S(2)}, u32[]{:S(2)}) collective-permute-start(bf16[64,4096]{1,0:T(8,128)(2,1)S(1)} %pad_maximum_fusion.3), channel_id=1, source_target_pairs={{0,3},{1,2},{2,1},{3,0},{4,7},{5,6},{6,5},{7,4},{8,11},{9,10},{10,... | collective-permute-start | bytes 1572872 | tf_op jit(solution)/shard_map/ppermute | solution.py:134
  51.7 12.6 %collective-permute-done.8.refs_2_ = bf16[64,4096]{1,0:T(8,128)(2,1)S(1)} collective-permute-done((bf16[64,4096]{1,0:T(8,128)(2,1)S(1)}, bf16[64,4096]{1,0:T(8,128)(2,1)S(1)}, u32[]{:S(2)}, u32[]{:S(2)}) %collective-permute-start.8) | collective-permute-done | bytes 524320 | tf_op jit(solution)/shard_map/ppermute | solution.py:134
  64.3 6.1 %shard_map.67.refs_5_ = bf16[1024,1792]{1,0:T(8,128)(2,1)} custom-call(s32[268]{0:T(512)S(1)} %shard_map.64.table_ref, bf16[48,4096]{1,0:T(8,128)(2,1)S(1)} %collective-permute-done.2.refs_0_, bf16[96,4096]{1,0:T(8,128)(2,1)S(1)} %collective-permute-done.5.refs_1_, ...), custom_call_target="tpu_custom_call", output_to_operand_aliasing={{}: (6, {})} | custom-call | flops 7632000000 | bytes 745472 | tf_op jit(solution)/shard_map/pallas_call | solution.py:111
  70.4 6.0 %collective-permute-done.7.refs_0_ = bf16[48,4096]{1,0:T(8,128)(2,1)S(1)} collective-permute-done((bf16[48,4096]{1,0:T(8,128)(2,1)S(1)}, bf16[48,4096]{1,0:T(8,128)(2,1)S(1)}, u32[]{:S(2)}, u32[]{:S(2)}) %collective-permute-start.7) | collective-permute-done | bytes 393248 | tf_op jit(solution)/shard_map/ppermute | solution.py:134
  76.6 8.1 %shard_map.68.refs_4_ = bf16[1024,1792]{1,0:T(8,128)(2,1)} custom-call(s32[268]{0:T(512)S(1)} %shard_map.64.table_ref, bf16[48,4096]{1,0:T(8,128)(2,1)S(1)} %collective-permute-done.7.refs_0_, bf16[192,4096]{1,0:T(8,128)(2,1)S(1)} %collective-permute-done.11.refs_1_, ...), custom_call_target="tpu_custom_call", output_to_operand_aliasing={{}: (6, {})} | custom-call | flops 9936000000 | bytes 1089536 | tf_op jit(solution)/shard_map/pallas_call | solution.py:111
  84.7 3.9 %collective-permute-done.9.refs_0_ = bf16[96,4096]{1,0:T(8,128)(2,1)S(1)} collective-permute-done((bf16[96,4096]{1,0:T(8,128)(2,1)S(1)}, bf16[96,4096]{1,0:T(8,128)(2,1)S(1)}, u32[]{:S(2)}, u32[]{:S(2)}) %collective-permute-start.9) | collective-permute-done | bytes 786464 | tf_op jit(solution)/shard_map/ppermute | solution.py:134
  88.5 5.0 %shard_map.69 = bf16[1024,1792]{1,0:T(8,128)(2,1)} custom-call(s32[268]{0:T(512)S(1)} %shard_map.64.table_ref, bf16[96,4096]{1,0:T(8,128)(2,1)S(1)} %collective-permute-done.9.refs_0_, bf16[64,4096]{1,0:T(8,128)(2,1)S(1)} %collective-permute-done.10.refs_1_, bf16[14,9,128,128]{3,2,1,0:T(8,128)(2,1)S(1)} %copy-done.1, ...), custom_call_target="tpu_custom_call", output_to_operand_aliasing={{}: (5, {})} | custom-call | flops 6480000000 | bytes 573440 | tf_op jit(solution)/shard_map/pallas_call | solution.py:111
  (31 shorter events, 2.6 us)
Async XLA Ops:
  0.0 15.2 %collective-permute-start.1 = (bf16[64,4096]{1,0:T(8,128)(2,1)}, bf16[64,4096]{1,0:T(8,128)(2,1)S(1)}, u32[]{:S(2)}, u32[]{:S(2)}) collective-permute-start(bf16[64,4096]{1,0:T(8,128)(2,1)} %refs_0_.2), channel_id=1, source_target_pairs={{0,4},{1,5},{2,6},{3,7},{4,0},{5,1},{6,2},{7,3},{8,12},{9,13},{10,... | collective-permute-start | bytes 1572872 | tf_op jit(solution)/shard_map/ppermute | solution.py:134
  1.3 13.9 %copy-start.4 = (bf16[64,4096]{1,0:T(8,128)(2,1)S(1)}, bf16[64,4096]{1,0:T(8,128)(2,1)}, u32[]{:S(2)}) copy-start(bf16[64,4096]{1,0:T(8,128)(2,1)} %refs_0_.2) | copy-start | bytes 1572868
  2.4 19.7 %collective-permute-start = (bf16[48,4096]{1,0:T(8,128)(2,1)S(1)}, bf16[48,4096]{1,0:T(8,128)(2,1)S(1)}, u32[]{:S(2)}, u32[]{:S(2)}) collective-permute-start(bf16[48,4096]{1,0:T(8,128)(2,1)S(1)} %slice_bitcast_fusion), channel_id=1, source_target_pairs={{0,1},{1,0},{2,3},{3,2},{4,5},{5,4},{6,7},{7,6},{8,9},{9,8},{10,11... | collective-permute-start | bytes 1179656 | tf_op jit(solution)/shard_map/ppermute | solution.py:134
  2.5 20.9 %collective-permute-start.3 = (bf16[48,4096]{1,0:T(8,128)(2,1)S(1)}, bf16[48,4096]{1,0:T(8,128)(2,1)S(1)}, u32[]{:S(2)}, u32[]{:S(2)}) collective-permute-start(bf16[48,4096]{1,0:T(8,128)(2,1)S(1)} %slice_bitcast_fusion), channel_id=1, source_target_pairs={{0,3},{1,2},{2,1},{3,0},{4,7},{5,6},{6,5},{7,4},{8,11},{9,10},{10,... | collective-permute-start | bytes 1179656 | tf_op jit(solution)/shard_map/ppermute | solution.py:134
  8.5 9.4 %collective-permute-start.6 = (bf16[64,4096]{1,0:T(8,128)(2,1)}, bf16[64,4096]{1,0:T(8,128)(2,1)S(1)}, u32[]{:S(2)}, u32[]{:S(2)}) collective-permute-start(bf16[64,4096]{1,0:T(8,128)(2,1)} %refs_0_.2), channel_id=1, source_target_pairs={{0,12},{1,13},{2,14},{3,15},{4,8},{5,9},{6,10},{7,11},{8,4},{9,5},... | collective-permute-start | bytes 1572872 | tf_op jit(solution)/shard_map/ppermute | solution.py:134
  10.8 2.2 %copy-start = (bf16[14,9,128,128]{3,2,1,0:T(8,128)(2,1)S(1)}, bf16[14,9,128,128]{3,2,1,0:T(8,128)(2,1)}, u32[]{:S(2)}) copy-start(bf16[14,9,128,128]{3,2,1,0:T(8,128)(2,1)} %refs_2_.3) | copy-start | bytes 12386308
  13.0 2.2 %copy-start.2 = (bf16[14,9,128,128]{3,2,1,0:T(8,128)(2,1)S(1)}, bf16[14,9,128,128]{3,2,1,0:T(8,128)(2,1)}, u32[]{:S(2)}) copy-start(bf16[14,9,128,128]{3,2,1,0:T(8,128)(2,1)} %refs_3_.5) | copy-start | bytes 12386308
  15.1 2.7 %copy-start.1 = (bf16[14,9,128,128]{3,2,1,0:T(8,128)(2,1)S(1)}, bf16[14,9,128,128]{3,2,1,0:T(8,128)(2,1)}, u32[]{:S(2)}) copy-start(bf16[14,9,128,128]{3,2,1,0:T(8,128)(2,1)} %refs_2_.3) | copy-start | bytes 12386308
  15.1 3.4 %copy-start.3 = (bf16[14,9,128,128]{3,2,1,0:T(8,128)(2,1)S(1)}, bf16[14,9,128,128]{3,2,1,0:T(8,128)(2,1)}, u32[]{:S(2)}) copy-start(bf16[14,9,128,128]{3,2,1,0:T(8,128)(2,1)} %refs_3_.5) | copy-start | bytes 12386308
  15.2 11.0 %collective-permute-start.4 = (bf16[64,4096]{1,0:T(8,128)(2,1)S(1)}, bf16[64,4096]{1,0:T(8,128)(2,1)S(1)}, u32[]{:S(2)}, u32[]{:S(2)}) collective-permute-start(bf16[64,4096]{1,0:T(8,128)(2,1)S(1)} %collective-permute-done.1.refs_0_), channel_id=1, source_target_pairs={{0,12},{1,13},{2,14},{3,15},{4,8},{5,9},{6,10},{7,11},{8,4},{9,5},... | collective-permute-start | bytes 1572872 | tf_op jit(solution)/shard_map/ppermute | solution.py:134
  23.4 23.7 %collective-permute-start.2 = (bf16[48,4096]{1,0:T(8,128)(2,1)S(1)}, bf16[48,4096]{1,0:T(8,128)(2,1)S(1)}, u32[]{:S(2)}, u32[]{:S(2)}) collective-permute-start(bf16[48,4096]{1,0:T(8,128)(2,1)S(1)} %collective-permute-done.refs_3_), channel_id=1, source_target_pairs={{0,3},{1,2},{2,1},{3,0},{4,7},{5,6},{6,5},{7,4},{8,11},{9,10},{10,... | collective-permute-start | bytes 1179656 | tf_op jit(solution)/shard_map/ppermute | solution.py:134
  26.2 12.3 %collective-permute-start.5 = (bf16[96,4096]{1,0:T(8,128)(2,1)S(1)}, bf16[96,4096]{1,0:T(8,128)(2,1)S(1)}, u32[]{:S(2)}, u32[]{:S(2)}) collective-permute-start(bf16[96,4096]{1,0:T(8,128)(2,1)S(1)} %pad_maximum_fusion.1), channel_id=1, source_target_pairs={{0,4},{1,5},{2,6},{3,7},{4,0},{5,1},{6,2},{7,3},{8,12},{9,13},{10,... | collective-permute-start | bytes 2359304 | tf_op jit(solution)/shard_map/ppermute | solution.py:134
  28.6 35.7 %collective-permute-start.8 = (bf16[64,4096]{1,0:T(8,128)(2,1)S(1)}, bf16[64,4096]{1,0:T(8,128)(2,1)S(1)}, u32[]{:S(2)}, u32[]{:S(2)}) collective-permute-start(bf16[64,4096]{1,0:T(8,128)(2,1)S(1)} %pad_maximum_fusion.3), channel_id=1, source_target_pairs={{0,1},{1,0},{2,3},{3,2},{4,5},{5,4},{6,7},{7,6},{8,9},{9,8},{10,11... | collective-permute-start | bytes 1572872 | tf_op jit(solution)/shard_map/ppermute | solution.py:134
  38.7 37.9 %collective-permute-start.11 = (bf16[192,4096]{1,0:T(8,128)(2,1)S(1)}, bf16[192,4096]{1,0:T(8,128)(2,1)S(1)}, u32[]{:S(2)}, u32[]{:S(2)}) collective-permute-start(bf16[192,4096]{1,0:T(8,128)(2,1)S(1)} %pad_maximum_fusion), channel_id=1, source_target_pairs={{0,12},{1,13},{2,14},{3,15},{4,8},{5,9},{6,10},{7,11},{8,4},{9,5},... | collective-permute-start | bytes 4718600 | tf_op jit(solution)/shard_map/ppermute | solution.py:134
  47.1 29.5 %collective-permute-start.12 = (bf16[64,4096]{1,0:T(8,128)(2,1)S(1)}, bf16[64,4096]{1,0:T(8,128)(2,1)S(1)}, u32[]{:S(2)}, u32[]{:S(2)}) collective-permute-start(bf16[64,4096]{1,0:T(8,128)(2,1)S(1)} %pad_maximum_fusion.3), channel_id=1, source_target_pairs={{0,3},{1,2},{2,1},{3,0},{4,7},{5,6},{6,5},{7,4},{8,11},{9,10},{10,... | collective-permute-start | bytes 1572872 | tf_op jit(solution)/shard_map/ppermute | solution.py:134
  64.3 20.3 %collective-permute-start.10 = (bf16[64,4096]{1,0:T(8,128)(2,1)S(1)}, bf16[64,4096]{1,0:T(8,128)(2,1)S(1)}, u32[]{:S(2)}, u32[]{:S(2)}) collective-permute-start(bf16[64,4096]{1,0:T(8,128)(2,1)S(1)} %collective-permute-done.8.refs_2_), channel_id=1, source_target_pairs={{0,3},{1,2},{2,1},{3,0},{4,7},{5,6},{6,5},{7,4},{8,11},{9,10},{10,... | collective-permute-start | bytes 1572872 | tf_op jit(solution)/shard_map/ppermute | solution.py:134
  64.3 12.1 %collective-permute-start.7 = (bf16[48,4096]{1,0:T(8,128)(2,1)S(1)}, bf16[48,4096]{1,0:T(8,128)(2,1)S(1)}, u32[]{:S(2)}, u32[]{:S(2)}) collective-permute-start(bf16[48,4096]{1,0:T(8,128)(2,1)S(1)} %collective-permute-done.2.refs_0_), channel_id=1, source_target_pairs={{0,4},{1,5},{2,6},{3,7},{4,0},{5,1},{6,2},{7,3},{8,12},{9,13},{10,... | collective-permute-start | bytes 1179656 | tf_op jit(solution)/shard_map/ppermute | solution.py:134
  76.4 12.1 %collective-permute-start.9 = (bf16[96,4096]{1,0:T(8,128)(2,1)S(1)}, bf16[96,4096]{1,0:T(8,128)(2,1)S(1)}, u32[]{:S(2)}, u32[]{:S(2)}) collective-permute-start(bf16[96,4096]{1,0:T(8,128)(2,1)S(1)} %pad_maximum_fusion.2), channel_id=1, source_target_pairs={{0,12},{1,13},{2,14},{3,15},{4,8},{5,9},{6,10},{7,11},{8,4},{9,5},... | collective-permute-start | bytes 2359304 | tf_op jit(solution)/shard_map/ppermute | solution.py:134

commit v9 on v8

--- a/solution.py
+++ b/solution.py
@@ -164,7 +164,7 @@
         p2 = swap(after(joined(pair, p1), result), "y", 1)
         q1 = swap(after(z3, p1, result), "y", 0)
         b2 = swap(after(column, z3, result), "z", 1)
-        b3 = swap(after(b1, z3, result), "z", 1)
+        b3 = swap(after(b1, q1), "z", 1)
         result = run([z3, p1, b1], result)
         q2 = swap(after(joined(z3, q1), result), "y", 1)
         for pieces in ([q1, p2, b2], [q2, b3]):

time: 93.9 us -> 88.1 us (0.938)
  the two profiles are of different devices: /device:TPU:80 before, /device:TPU:8 now
where the time goes in v9:
time: 88.1 us; the launch traced here: 87.8 us
  Pallas kernels  30.2 us (34%)
  starting transfers between devices  27.1 us (31%)
  waiting for transfers between devices  19.3 us (22%)
  local copies, waits for them, and re-layouts  9.8 us (11%)
  other arithmetic  1.07 us (1%)
    pallas_call x5, Pallas kernels, project(): pl.pallas_call(functools.partial(project_kernel, layout, starts, len(prev...  30.2 us
    ppermute x13, starting transfers between devices, swap(): rows = lax.ppermute(piece.rows, AXES, pairs)  27.1 us
    ppermute x13, waiting for transfers between devices, swap(): rows = lax.ppermute(piece.rows, AXES, pairs)  19.3 us
    unnamed x10, local copies, waits for them, and re-layouts  7.07 us
  transfers between devices with their start and end apart: 13, of which 5 were waited for; matrix products, arithmetic and copies ran while one was open for 4% of the time, Pallas kernels for 29%

profile of v9, /device:TPU:8, one launch (start us, length us, event | category | flops | bytes accessed | tf_op | source)
XLA Modules:
  0.0 87.8 jit_solution(6124269147960100751)
XLA Ops:
  0.0 2.2 %collective-permute-start.1 = (bf16[64,4096]{1,0:T(8,128)(2,1)}, bf16[64,4096]{1,0:T(8,128)(2,1)S(1)}, u32[]{:S(2)}, u32[]{:S(2)}) collective-permute-start(bf16[64,4096]{1,0:T(8,128)(2,1)} %refs_0_.2), channel_id=1, source_target_pairs={{0,4},{1,5},{2,6},{3,7},{4,0},{5,1},{6,2},{7,3},{8,12},{9,13},{10,... | collective-permute-start | bytes 1572872 | tf_op jit(solution)/shard_map/ppermute | solution.py:134
  2.2 1.1 %slice_bitcast_fusion = bf16[48,4096]{1,0:T(8,128)(2,1)S(1)} fusion(bf16[1,64,4096]{2,1,0:T(8,128)(2,1)} %bitcast.16), kind=kLoop, calls=%fused_computation.4 | loop fusion | bytes 786432 | tf_op jit(solution)/shard_map/reshape | solution.py:36
  3.3 1.6 %collective-permute-start = (bf16[48,4096]{1,0:T(8,128)(2,1)S(1)}, bf16[48,4096]{1,0:T(8,128)(2,1)S(1)}, u32[]{:S(2)}, u32[]{:S(2)}) collective-permute-start(bf16[48,4096]{1,0:T(8,128)(2,1)S(1)} %slice_bitcast_fusion), channel_id=1, source_target_pairs={{0,1},{1,0},{2,3},{3,2},{4,5},{5,4},{6,7},{7,6},{8,9},{9,8},{10,11... | collective-permute-start | bytes 1179656 | tf_op jit(solution)/shard_map/ppermute | solution.py:134
  4.9 4.5 %collective-permute-start.3 = (bf16[48,4096]{1,0:T(8,128)(2,1)S(1)}, bf16[48,4096]{1,0:T(8,128)(2,1)S(1)}, u32[]{:S(2)}, u32[]{:S(2)}) collective-permute-start(bf16[48,4096]{1,0:T(8,128)(2,1)S(1)} %slice_bitcast_fusion), channel_id=1, source_target_pairs={{0,3},{1,2},{2,1},{3,0},{4,7},{5,6},{6,5},{7,4},{8,11},{9,10},{10,... | collective-permute-start | bytes 1179656 | tf_op jit(solution)/shard_map/ppermute | solution.py:134
  9.4 2.4 %collective-permute-start.6 = (bf16[64,4096]{1,0:T(8,128)(2,1)}, bf16[64,4096]{1,0:T(8,128)(2,1)S(1)}, u32[]{:S(2)}, u32[]{:S(2)}) collective-permute-start(bf16[64,4096]{1,0:T(8,128)(2,1)} %refs_0_.2), channel_id=1, source_target_pairs={{0,12},{1,13},{2,14},{3,15},{4,8},{5,9},{6,10},{7,11},{8,4},{9,5},... | collective-permute-start | bytes 1572872 | tf_op jit(solution)/shard_map/ppermute | solution.py:134
  12.6 0.8 reshape.39
  14.2 2.2 %copy-done = bf16[14,9,128,128]{3,2,1,0:T(8,128)(2,1)S(1)} copy-done((bf16[14,9,128,128]{3,2,1,0:T(8,128)(2,1)S(1)}, bf16[14,9,128,128]{3,2,1,0:T(8,128)(2,1)}, u32[]{:S(2)}) %copy-start) | copy-done | bytes 4128792
  16.3 2.2 %copy-done.2 = bf16[14,9,128,128]{3,2,1,0:T(8,128)(2,1)S(1)} copy-done((bf16[14,9,128,128]{3,2,1,0:T(8,128)(2,1)S(1)}, bf16[14,9,128,128]{3,2,1,0:T(8,128)(2,1)}, u32[]{:S(2)}) %copy-start.2) | copy-done | bytes 4128792
  19.2 1.5 %copy-done.1 = bf16[14,9,128,128]{3,2,1,0:T(8,128)(2,1)S(1)} copy-done((bf16[14,9,128,128]{3,2,1,0:T(8,128)(2,1)S(1)}, bf16[14,9,128,128]{3,2,1,0:T(8,128)(2,1)}, u32[]{:S(2)}) %copy-start.1) | copy-done | bytes 4128792
  20.7 1.3 %copy-done.3 = bf16[14,9,128,128]{3,2,1,0:T(8,128)(2,1)S(1)} copy-done((bf16[14,9,128,128]{3,2,1,0:T(8,128)(2,1)S(1)}, bf16[14,9,128,128]{3,2,1,0:T(8,128)(2,1)}, u32[]{:S(2)}) %copy-start.3) | copy-done | bytes 4128792
  21.9 3.5 %shard_map.65.refs_7_ = bf16[1024,1792]{1,0:T(8,128)(2,1)} custom-call(s32[268]{0:T(512)S(1)} %shard_map.64.table_ref, bf16[64,4096]{1,0:T(8,128)(2,1)S(1)} %copy-done.4, bf16[14,9,128,128]{3,2,1,0:T(8,128)(2,1)S(1)} %copy-done.1, bf16[14,9,128,128]{3,2,1,0:T(8,128)(2,1)S(1)} %copy-done.3), custom_call_target="tpu_custom_call" | custom-call | flops 4176000000 | bytes 229376 | tf_op jit(solution)/shard_map/pallas_call | solution.py:111
  25.5 3.7 %collective-permute-start.2 = (bf16[48,4096]{1,0:T(8,128)(2,1)S(1)}, bf16[48,4096]{1,0:T(8,128)(2,1)S(1)}, u32[]{:S(2)}, u32[]{:S(2)}) collective-permute-start(bf16[48,4096]{1,0:T(8,128)(2,1)S(1)} %collective-permute-done.refs_3_), channel_id=1, source_target_pairs={{0,3},{1,2},{2,1},{3,0},{4,7},{5,6},{6,5},{7,4},{8,11},{9,10},{10,... | collective-permute-start | bytes 1179656 | tf_op jit(solution)/shard_map/ppermute | solution.py:134
  29.2 3.0 %collective-permute-start.5 = (bf16[96,4096]{1,0:T(8,128)(2,1)S(1)}, bf16[96,4096]{1,0:T(8,128)(2,1)S(1)}, u32[]{:S(2)}, u32[]{:S(2)}) collective-permute-start(bf16[96,4096]{1,0:T(8,128)(2,1)S(1)} %pad_maximum_fusion.1), channel_id=1, source_target_pairs={{0,4},{1,5},{2,6},{3,7},{4,0},{5,1},{6,2},{7,3},{8,12},{9,13},{10,... | collective-permute-start | bytes 2359304 | tf_op jit(solution)/shard_map/ppermute | solution.py:134
  32.3 1.4 %collective-permute-start.8 = (bf16[64,4096]{1,0:T(8,128)(2,1)S(1)}, bf16[64,4096]{1,0:T(8,128)(2,1)S(1)}, u32[]{:S(2)}, u32[]{:S(2)}) collective-permute-start(bf16[64,4096]{1,0:T(8,128)(2,1)S(1)} %pad_maximum_fusion.3), channel_id=1, source_target_pairs={{0,1},{1,0},{2,3},{3,2},{4,5},{5,4},{6,7},{7,6},{8,9},{9,8},{10,11... | collective-permute-start | bytes 1572872 | tf_op jit(solution)/shard_map/ppermute | solution.py:134
  33.8 7.5 %shard_map.66.refs_5_ = bf16[1024,1792]{1,0:T(8,128)(2,1)} custom-call(s32[268]{0:T(512)S(1)} %shard_map.64.table_ref, bf16[64,4096]{1,0:T(8,128)(2,1)S(1)} %collective-permute-done.1.refs_0_, bf16[64,4096]{1,0:T(8,128)(2,1)S(1)} %collective-permute-done.6.refs_1_, ...), custom_call_target="tpu_custom_call", output_to_operand_aliasing={{}: (8, {})} | custom-call | flops 9552000000 | bytes 1032192 | tf_op jit(solution)/shard_map/pallas_call | solution.py:111
  41.3 0.9 %collective-permute-done.5.refs_1_ = bf16[96,4096]{1,0:T(8,128)(2,1)S(1)} collective-permute-done((bf16[96,4096]{1,0:T(8,128)(2,1)S(1)}, bf16[96,4096]{1,0:T(8,128)(2,1)S(1)}, u32[]{:S(2)}, u32[]{:S(2)}) %collective-permute-start.5) | collective-permute-done | bytes 786464 | tf_op jit(solution)/shard_map/ppermute | solution.py:134
  43.0 6.1 %collective-permute-done.2.refs_0_ = bf16[48,4096]{1,0:T(8,128)(2,1)S(1)} collective-permute-done((bf16[48,4096]{1,0:T(8,128)(2,1)S(1)}, bf16[48,4096]{1,0:T(8,128)(2,1)S(1)}, u32[]{:S(2)}, u32[]{:S(2)}) %collective-permute-start.2) | collective-permute-done | bytes 393248 | tf_op jit(solution)/shard_map/ppermute | solution.py:134
  49.2 4.7 %collective-permute-start.7 = (bf16[48,4096]{1,0:T(8,128)(2,1)S(1)}, bf16[48,4096]{1,0:T(8,128)(2,1)S(1)}, u32[]{:S(2)}, u32[]{:S(2)}) collective-permute-start(bf16[48,4096]{1,0:T(8,128)(2,1)S(1)} %collective-permute-done.2.refs_0_), channel_id=1, source_target_pairs={{0,4},{1,5},{2,6},{3,7},{4,0},{5,1},{6,2},{7,3},{8,12},{9,13},{10,... | collective-permute-start | bytes 1179656 | tf_op jit(solution)/shard_map/ppermute | solution.py:134
  53.9 6.1 %shard_map.67.refs_5_ = bf16[1024,1792]{1,0:T(8,128)(2,1)} custom-call(s32[268]{0:T(512)S(1)} %shard_map.64.table_ref, bf16[48,4096]{1,0:T(8,128)(2,1)S(1)} %collective-permute-done.2.refs_0_, bf16[96,4096]{1,0:T(8,128)(2,1)S(1)} %collective-permute-done.5.refs_1_, ...), custom_call_target="tpu_custom_call", output_to_operand_aliasing={{}: (6, {})} | custom-call | flops 7632000000 | bytes 745472 | tf_op jit(solution)/shard_map/pallas_call | solution.py:111
  60.0 3.9 %collective-permute-done.7.refs_0_ = bf16[48,4096]{1,0:T(8,128)(2,1)S(1)} collective-permute-done((bf16[48,4096]{1,0:T(8,128)(2,1)S(1)}, bf16[48,4096]{1,0:T(8,128)(2,1)S(1)}, u32[]{:S(2)}, u32[]{:S(2)}) %collective-permute-start.7) | collective-permute-done | bytes 393248 | tf_op jit(solution)/shard_map/ppermute | solution.py:134
  64.0 2.6 %collective-permute-start.9 = (bf16[96,4096]{1,0:T(8,128)(2,1)S(1)}, bf16[96,4096]{1,0:T(8,128)(2,1)S(1)}, u32[]{:S(2)}, u32[]{:S(2)}) collective-permute-start(bf16[96,4096]{1,0:T(8,128)(2,1)S(1)} %pad_maximum_fusion.2), channel_id=1, source_target_pairs={{0,12},{1,13},{2,14},{3,15},{4,8},{5,9},{6,10},{7,11},{8,4},{9,5},... | collective-permute-start | bytes 2359304 | tf_op jit(solution)/shard_map/ppermute | solution.py:134
  66.8 8.1 %shard_map.68.refs_4_ = bf16[1024,1792]{1,0:T(8,128)(2,1)} custom-call(s32[268]{0:T(512)S(1)} %shard_map.64.table_ref, bf16[48,4096]{1,0:T(8,128)(2,1)S(1)} %collective-permute-done.7.refs_0_, bf16[192,4096]{1,0:T(8,128)(2,1)S(1)} %collective-permute-done.11.refs_1_, ...), custom_call_target="tpu_custom_call", output_to_operand_aliasing={{}: (6, {})} | custom-call | flops 9936000000 | bytes 1089536 | tf_op jit(solution)/shard_map/pallas_call | solution.py:111
  74.9 7.8 %collective-permute-done.10.refs_1_ = bf16[64,4096]{1,0:T(8,128)(2,1)S(1)} collective-permute-done((bf16[64,4096]{1,0:T(8,128)(2,1)S(1)}, bf16[64,4096]{1,0:T(8,128)(2,1)S(1)}, u32[]{:S(2)}, u32[]{:S(2)}) %collective-permute-start.10) | collective-permute-done | bytes 524320 | tf_op jit(solution)/shard_map/ppermute | solution.py:134
  82.7 5.0 %shard_map.69 = bf16[1024,1792]{1,0:T(8,128)(2,1)} custom-call(s32[268]{0:T(512)S(1)} %shard_map.64.table_ref, bf16[96,4096]{1,0:T(8,128)(2,1)S(1)} %collective-permute-done.9.refs_0_, bf16[64,4096]{1,0:T(8,128)(2,1)S(1)} %collective-permute-done.10.refs_1_, bf16[14,9,128,128]{3,2,1,0:T(8,128)(2,1)S(1)} %copy-done.1, ...), custom_call_target="tpu_custom_call", output_to_operand_aliasing={{}: (5, {})} | custom-call | flops 6480000000 | bytes 573440 | tf_op jit(solution)/shard_map/pallas_call | solution.py:111
  (31 shorter events, 3.5 us)
Async XLA Ops:
  0.0 18.5 %collective-permute-start.1 = (bf16[64,4096]{1,0:T(8,128)(2,1)}, bf16[64,4096]{1,0:T(8,128)(2,1)S(1)}, u32[]{:S(2)}, u32[]{:S(2)}) collective-permute-start(bf16[64,4096]{1,0:T(8,128)(2,1)} %refs_0_.2), channel_id=1, source_target_pairs={{0,4},{1,5},{2,6},{3,7},{4,0},{5,1},{6,2},{7,3},{8,12},{9,13},{10,... | collective-permute-start | bytes 1572872 | tf_op jit(solution)/shard_map/ppermute | solution.py:134
  2.2 16.3 %copy-start.4 = (bf16[64,4096]{1,0:T(8,128)(2,1)S(1)}, bf16[64,4096]{1,0:T(8,128)(2,1)}, u32[]{:S(2)}) copy-start(bf16[64,4096]{1,0:T(8,128)(2,1)} %refs_0_.2) | copy-start | bytes 1572868
  3.3 22.2 %collective-permute-start = (bf16[48,4096]{1,0:T(8,128)(2,1)S(1)}, bf16[48,4096]{1,0:T(8,128)(2,1)S(1)}, u32[]{:S(2)}, u32[]{:S(2)}) collective-permute-start(bf16[48,4096]{1,0:T(8,128)(2,1)S(1)} %slice_bitcast_fusion), channel_id=1, source_target_pairs={{0,1},{1,0},{2,3},{3,2},{4,5},{5,4},{6,7},{7,6},{8,9},{9,8},{10,11... | collective-permute-start | bytes 1179656 | tf_op jit(solution)/shard_map/ppermute | solution.py:134
  4.9 20.5 %collective-permute-start.3 = (bf16[48,4096]{1,0:T(8,128)(2,1)S(1)}, bf16[48,4096]{1,0:T(8,128)(2,1)S(1)}, u32[]{:S(2)}, u32[]{:S(2)}) collective-permute-start(bf16[48,4096]{1,0:T(8,128)(2,1)S(1)} %slice_bitcast_fusion), channel_id=1, source_target_pairs={{0,3},{1,2},{2,1},{3,0},{4,7},{5,6},{6,5},{7,4},{8,11},{9,10},{10,... | collective-permute-start | bytes 1179656 | tf_op jit(solution)/shard_map/ppermute | solution.py:134
  9.4 9.8 %collective-permute-start.6 = (bf16[64,4096]{1,0:T(8,128)(2,1)}, bf16[64,4096]{1,0:T(8,128)(2,1)S(1)}, u32[]{:S(2)}, u32[]{:S(2)}) collective-permute-start(bf16[64,4096]{1,0:T(8,128)(2,1)} %refs_0_.2), channel_id=1, source_target_pairs={{0,12},{1,13},{2,14},{3,15},{4,8},{5,9},{6,10},{7,11},{8,4},{9,5},... | collective-permute-start | bytes 1572872 | tf_op jit(solution)/shard_map/ppermute | solution.py:134
  14.2 2.2 %copy-start = (bf16[14,9,128,128]{3,2,1,0:T(8,128)(2,1)S(1)}, bf16[14,9,128,128]{3,2,1,0:T(8,128)(2,1)}, u32[]{:S(2)}) copy-start(bf16[14,9,128,128]{3,2,1,0:T(8,128)(2,1)} %refs_2_.3) | copy-start | bytes 12386308
  16.3 2.2 %copy-start.2 = (bf16[14,9,128,128]{3,2,1,0:T(8,128)(2,1)S(1)}, bf16[14,9,128,128]{3,2,1,0:T(8,128)(2,1)}, u32[]{:S(2)}) copy-start(bf16[14,9,128,128]{3,2,1,0:T(8,128)(2,1)} %refs_3_.5) | copy-start | bytes 12386308
  18.5 2.2 %copy-start.1 = (bf16[14,9,128,128]{3,2,1,0:T(8,128)(2,1)S(1)}, bf16[14,9,128,128]{3,2,1,0:T(8,128)(2,1)}, u32[]{:S(2)}) copy-start(bf16[14,9,128,128]{3,2,1,0:T(8,128)(2,1)} %refs_2_.3) | copy-start | bytes 12386308
  18.5 3.4 %copy-start.3 = (bf16[14,9,128,128]{3,2,1,0:T(8,128)(2,1)S(1)}, bf16[14,9,128,128]{3,2,1,0:T(8,128)(2,1)}, u32[]{:S(2)}) copy-start(bf16[14,9,128,128]{3,2,1,0:T(8,128)(2,1)} %refs_3_.5) | copy-start | bytes 12386308
  18.6 10.7 %collective-permute-start.4 = (bf16[64,4096]{1,0:T(8,128)(2,1)S(1)}, bf16[64,4096]{1,0:T(8,128)(2,1)S(1)}, u32[]{:S(2)}, u32[]{:S(2)}) collective-permute-start(bf16[64,4096]{1,0:T(8,128)(2,1)S(1)} %collective-permute-done.1.refs_0_), channel_id=1, source_target_pairs={{0,12},{1,13},{2,14},{3,15},{4,8},{5,9},{6,10},{7,11},{8,4},{9,5},... | collective-permute-start | bytes 1572872 | tf_op jit(solution)/shard_map/ppermute | solution.py:134
  25.5 23.7 %collective-permute-start.2 = (bf16[48,4096]{1,0:T(8,128)(2,1)S(1)}, bf16[48,4096]{1,0:T(8,128)(2,1)S(1)}, u32[]{:S(2)}, u32[]{:S(2)}) collective-permute-start(bf16[48,4096]{1,0:T(8,128)(2,1)S(1)} %collective-permute-done.refs_3_), channel_id=1, source_target_pairs={{0,3},{1,2},{2,1},{3,0},{4,7},{5,6},{6,5},{7,4},{8,11},{9,10},{10,... | collective-permute-start | bytes 1179656 | tf_op jit(solution)/shard_map/ppermute | solution.py:134
  29.2 13.0 %collective-permute-start.5 = (bf16[96,4096]{1,0:T(8,128)(2,1)S(1)}, bf16[96,4096]{1,0:T(8,128)(2,1)S(1)}, u32[]{:S(2)}, u32[]{:S(2)}) collective-permute-start(bf16[96,4096]{1,0:T(8,128)(2,1)S(1)} %pad_maximum_fusion.1), channel_id=1, source_target_pairs={{0,4},{1,5},{2,6},{3,7},{4,0},{5,1},{6,2},{7,3},{8,12},{9,13},{10,... | collective-permute-start | bytes 2359304 | tf_op jit(solution)/shard_map/ppermute | solution.py:134
  32.3 21.5 %collective-permute-start.8 = (bf16[64,4096]{1,0:T(8,128)(2,1)S(1)}, bf16[64,4096]{1,0:T(8,128)(2,1)S(1)}, u32[]{:S(2)}, u32[]{:S(2)}) collective-permute-start(bf16[64,4096]{1,0:T(8,128)(2,1)S(1)} %pad_maximum_fusion.3), channel_id=1, source_target_pairs={{0,1},{1,0},{2,3},{3,2},{4,5},{5,4},{6,7},{7,6},{8,9},{9,8},{10,11... | collective-permute-start | bytes 1572872 | tf_op jit(solution)/shard_map/ppermute | solution.py:134
  42.4 24.4 %collective-permute-start.11 = (bf16[192,4096]{1,0:T(8,128)(2,1)S(1)}, bf16[192,4096]{1,0:T(8,128)(2,1)S(1)}, u32[]{:S(2)}, u32[]{:S(2)}) collective-permute-start(bf16[192,4096]{1,0:T(8,128)(2,1)S(1)} %pad_maximum_fusion), channel_id=1, source_target_pairs={{0,12},{1,13},{2,14},{3,15},{4,8},{5,9},{6,10},{7,11},{8,4},{9,5},... | collective-permute-start | bytes 4718600 | tf_op jit(solution)/shard_map/ppermute | solution.py:134
  49.2 17.6 %collective-permute-start.12 = (bf16[64,4096]{1,0:T(8,128)(2,1)S(1)}, bf16[64,4096]{1,0:T(8,128)(2,1)S(1)}, u32[]{:S(2)}, u32[]{:S(2)}) collective-permute-start(bf16[64,4096]{1,0:T(8,128)(2,1)S(1)} %pad_maximum_fusion.3), channel_id=1, source_target_pairs={{0,3},{1,2},{2,1},{3,0},{4,7},{5,6},{6,5},{7,4},{8,11},{9,10},{10,... | collective-permute-start | bytes 1572872 | tf_op jit(solution)/shard_map/ppermute | solution.py:134
  49.2 14.7 %collective-permute-start.7 = (bf16[48,4096]{1,0:T(8,128)(2,1)S(1)}, bf16[48,4096]{1,0:T(8,128)(2,1)S(1)}, u32[]{:S(2)}, u32[]{:S(2)}) collective-permute-start(bf16[48,4096]{1,0:T(8,128)(2,1)S(1)} %collective-permute-done.2.refs_0_), channel_id=1, source_target_pairs={{0,4},{1,5},{2,6},{3,7},{4,0},{5,1},{6,2},{7,3},{8,12},{9,13},{10,... | collective-permute-start | bytes 1179656 | tf_op jit(solution)/shard_map/ppermute | solution.py:134
  64.0 18.7 %collective-permute-start.9 = (bf16[96,4096]{1,0:T(8,128)(2,1)S(1)}, bf16[96,4096]{1,0:T(8,128)(2,1)S(1)}, u32[]{:S(2)}, u32[]{:S(2)}) collective-permute-start(bf16[96,4096]{1,0:T(8,128)(2,1)S(1)} %pad_maximum_fusion.2), channel_id=1, source_target_pairs={{0,12},{1,13},{2,14},{3,15},{4,8},{5,9},{6,10},{7,11},{8,4},{9,5},... | collective-permute-start | bytes 2359304 | tf_op jit(solution)/shard_map/ppermute | solution.py:134
  66.5 16.1 %collective-permute-start.10 = (bf16[64,4096]{1,0:T(8,128)(2,1)S(1)}, bf16[64,4096]{1,0:T(8,128)(2,1)S(1)}, u32[]{:S(2)}, u32[]{:S(2)}) collective-permute-start(bf16[64,4096]{1,0:T(8,128)(2,1)S(1)} %collective-permute-done.8.refs_2_), channel_id=1, source_target_pairs={{0,3},{1,2},{2,1},{3,0},{4,7},{5,6},{6,5},{7,4},{8,11},{9,10},{10,... | collective-permute-start | bytes 1572872 | tf_op jit(solution)/shard_map/ppermute | solution.py:134

commit v10 on v9

--- a/solution.py
+++ b/solution.py
@@ -166,7 +166,7 @@
         b2 = swap(after(column, z3, result), "z", 1)
         b3 = swap(after(b1, q1), "z", 1)
         result = run([z3, p1, b1], result)
-        q2 = swap(after(joined(z3, q1), result), "y", 1)
+        q2 = swap(after(joined(z3, q1), p2, result), "y", 1)
         for pieces in ([q1, p2, b2], [q2, b3]):
             result = run(pieces, result)
         return result

time: 88.1 us -> 88.5 us (level)
  the two profiles are of different devices: /device:TPU:8 before, /device:TPU:4 now
where the time goes in v10:
time: 88.5 us; the launch traced here: 88.2 us
  Pallas kernels  30.2 us (34%)
  starting transfers between devices  24.6 us (28%)
  waiting for transfers between devices  23.4 us (26%)
  local copies, waits for them, and re-layouts  8.73 us (10%)
  other arithmetic  1.06 us (1%)
    pallas_call x5, Pallas kernels, project(): pl.pallas_call(functools.partial(project_kernel, layout, starts, len(prev...  30.2 us
    ppermute x13, starting transfers between devices, swap(): rows = lax.ppermute(piece.rows, AXES, pairs)  24.6 us
    ppermute x13, waiting for transfers between devices, swap(): rows = lax.ppermute(piece.rows, AXES, pairs)  23.4 us
    unnamed x10, local copies, waits for them, and re-layouts  6 us
  transfers between devices with their start and end apart: 13, of which 7 were waited for; matrix products, arithmetic and copies ran while one was open for 4% of the time, Pallas kernels for 29%

profile of v10, /device:TPU:4, one launch (start us, length us, event | category | flops | bytes accessed | tf_op | source)
XLA Modules:
  0.0 88.2 jit_solution(5414918323605310326)
XLA Ops:
  0.0 1.6 %collective-permute-start.1 = (bf16[64,4096]{1,0:T(8,128)(2,1)}, bf16[64,4096]{1,0:T(8,128)(2,1)S(1)}, u32[]{:S(2)}, u32[]{:S(2)}) collective-permute-start(bf16[64,4096]{1,0:T(8,128)(2,1)} %refs_0_.2), channel_id=1, source_target_pairs={{0,4},{1,5},{2,6},{3,7},{4,0},{5,1},{6,2},{7,3},{8,12},{9,13},{10,... | collective-permute-start | bytes 1572872 | tf_op jit(solution)/shard_map/ppermute | solution.py:134
  1.6 1.1 %slice_bitcast_fusion = bf16[48,4096]{1,0:T(8,128)(2,1)S(1)} fusion(bf16[1,64,4096]{2,1,0:T(8,128)(2,1)} %bitcast.16), kind=kLoop, calls=%fused_computation.4 | loop fusion | bytes 786432 | tf_op jit(solution)/shard_map/reshape | solution.py:36
  2.7 3.4 %collective-permute-start = (bf16[48,4096]{1,0:T(8,128)(2,1)S(1)}, bf16[48,4096]{1,0:T(8,128)(2,1)S(1)}, u32[]{:S(2)}, u32[]{:S(2)}) collective-permute-start(bf16[48,4096]{1,0:T(8,128)(2,1)S(1)} %slice_bitcast_fusion), channel_id=1, source_target_pairs={{0,1},{1,0},{2,3},{3,2},{4,5},{5,4},{6,7},{7,6},{8,9},{9,8},{10,11... | collective-permute-start | bytes 1179656 | tf_op jit(solution)/shard_map/ppermute | solution.py:134
  6.1 4.5 %collective-permute-start.3 = (bf16[48,4096]{1,0:T(8,128)(2,1)S(1)}, bf16[48,4096]{1,0:T(8,128)(2,1)S(1)}, u32[]{:S(2)}, u32[]{:S(2)}) collective-permute-start(bf16[48,4096]{1,0:T(8,128)(2,1)S(1)} %slice_bitcast_fusion), channel_id=1, source_target_pairs={{0,3},{1,2},{2,1},{3,0},{4,7},{5,6},{6,5},{7,4},{8,11},{9,10},{10,... | collective-permute-start | bytes 1179656 | tf_op jit(solution)/shard_map/ppermute | solution.py:134
  10.6 2.2 %collective-permute-start.6 = (bf16[64,4096]{1,0:T(8,128)(2,1)}, bf16[64,4096]{1,0:T(8,128)(2,1)S(1)}, u32[]{:S(2)}, u32[]{:S(2)}) collective-permute-start(bf16[64,4096]{1,0:T(8,128)(2,1)} %refs_0_.2), channel_id=1, source_target_pairs={{0,12},{1,13},{2,14},{3,15},{4,8},{5,9},{6,10},{7,11},{8,4},{9,5},... | collective-permute-start | bytes 1572872 | tf_op jit(solution)/shard_map/ppermute | solution.py:134
  12.7 0.8 reshape.39
  13.5 0.8 reshape.38
  15.1 2.2 %copy-done = bf16[14,9,128,128]{3,2,1,0:T(8,128)(2,1)S(1)} copy-done((bf16[14,9,128,128]{3,2,1,0:T(8,128)(2,1)S(1)}, bf16[14,9,128,128]{3,2,1,0:T(8,128)(2,1)}, u32[]{:S(2)}) %copy-start) | copy-done | bytes 4128792
  17.2 2.2 %copy-done.2 = bf16[14,9,128,128]{3,2,1,0:T(8,128)(2,1)S(1)} copy-done((bf16[14,9,128,128]{3,2,1,0:T(8,128)(2,1)S(1)}, bf16[14,9,128,128]{3,2,1,0:T(8,128)(2,1)}, u32[]{:S(2)}) %copy-start.2) | copy-done | bytes 4128792
  19.5 1.1 %collective-permute-start.4 = (bf16[64,4096]{1,0:T(8,128)(2,1)S(1)}, bf16[64,4096]{1,0:T(8,128)(2,1)S(1)}, u32[]{:S(2)}, u32[]{:S(2)}) collective-permute-start(bf16[64,4096]{1,0:T(8,128)(2,1)S(1)} %collective-permute-done.1.refs_0_), channel_id=1, source_target_pairs={{0,12},{1,13},{2,14},{3,15},{4,8},{5,9},{6,10},{7,11},{8,4},{9,5},... | collective-permute-start | bytes 1572872 | tf_op jit(solution)/shard_map/ppermute | solution.py:134
  21.6 1.3 %copy-done.3 = bf16[14,9,128,128]{3,2,1,0:T(8,128)(2,1)S(1)} copy-done((bf16[14,9,128,128]{3,2,1,0:T(8,128)(2,1)S(1)}, bf16[14,9,128,128]{3,2,1,0:T(8,128)(2,1)}, u32[]{:S(2)}) %copy-start.3) | copy-done | bytes 4128792
  22.8 3.5 %shard_map.65.refs_7_ = bf16[1024,1792]{1,0:T(8,128)(2,1)} custom-call(s32[268]{0:T(512)S(1)} %shard_map.64.table_ref, bf16[64,4096]{1,0:T(8,128)(2,1)S(1)} %copy-done.4, bf16[14,9,128,128]{3,2,1,0:T(8,128)(2,1)S(1)} %copy-done.1, bf16[14,9,128,128]{3,2,1,0:T(8,128)(2,1)S(1)} %copy-done.3), custom_call_target="tpu_custom_call" | custom-call | flops 4176000000 | bytes 229376 | tf_op jit(solution)/shard_map/pallas_call | solution.py:111
  26.4 4.0 %collective-permute-start.2 = (bf16[48,4096]{1,0:T(8,128)(2,1)S(1)}, bf16[48,4096]{1,0:T(8,128)(2,1)S(1)}, u32[]{:S(2)}, u32[]{:S(2)}) collective-permute-start(bf16[48,4096]{1,0:T(8,128)(2,1)S(1)} %collective-permute-done.refs_3_), channel_id=1, source_target_pairs={{0,3},{1,2},{2,1},{3,0},{4,7},{5,6},{6,5},{7,4},{8,11},{9,10},{10,... | collective-permute-start | bytes 1179656 | tf_op jit(solution)/shard_map/ppermute | solution.py:134
  30.5 1.5 %collective-permute-start.9 = (bf16[64,4096]{1,0:T(8,128)(2,1)S(1)}, bf16[64,4096]{1,0:T(8,128)(2,1)S(1)}, u32[]{:S(2)}, u32[]{:S(2)}) collective-permute-start(bf16[64,4096]{1,0:T(8,128)(2,1)S(1)} %pad_maximum_fusion.3), channel_id=1, source_target_pairs={{0,1},{1,0},{2,3},{3,2},{4,5},{5,4},{6,7},{7,6},{8,9},{9,8},{10,11... | collective-permute-start | bytes 1572872 | tf_op jit(solution)/shard_map/ppermute | solution.py:134
  32.4 7.6 %shard_map.66.refs_5_ = bf16[1024,1792]{1,0:T(8,128)(2,1)} custom-call(s32[268]{0:T(512)S(1)} %shard_map.64.table_ref, bf16[64,4096]{1,0:T(8,128)(2,1)S(1)} %collective-permute-done.1.refs_0_, bf16[64,4096]{1,0:T(8,128)(2,1)S(1)} %collective-permute-done.6.refs_1_, ...), custom_call_target="tpu_custom_call", output_to_operand_aliasing={{}: (8, {})} | custom-call | flops 9552000000 | bytes 1032192 | tf_op jit(solution)/shard_map/pallas_call | solution.py:111
  39.9 4.0 %collective-permute-done.5.refs_1_ = bf16[96,4096]{1,0:T(8,128)(2,1)S(1)} collective-permute-done((bf16[96,4096]{1,0:T(8,128)(2,1)S(1)}, bf16[96,4096]{1,0:T(8,128)(2,1)S(1)}, u32[]{:S(2)}, u32[]{:S(2)}) %collective-permute-start.5) | collective-permute-done | bytes 786464 | tf_op jit(solution)/shard_map/ppermute | solution.py:134
  44.8 3.6 %collective-permute-done.2.refs_0_ = bf16[48,4096]{1,0:T(8,128)(2,1)S(1)} collective-permute-done((bf16[48,4096]{1,0:T(8,128)(2,1)S(1)}, bf16[48,4096]{1,0:T(8,128)(2,1)S(1)}, u32[]{:S(2)}, u32[]{:S(2)}) %collective-permute-start.2) | collective-permute-done | bytes 393248 | tf_op jit(solution)/shard_map/ppermute | solution.py:134
  48.5 4.7 %collective-permute-start.12 = (bf16[64,4096]{1,0:T(8,128)(2,1)S(1)}, bf16[64,4096]{1,0:T(8,128)(2,1)S(1)}, u32[]{:S(2)}, u32[]{:S(2)}) collective-permute-start(bf16[64,4096]{1,0:T(8,128)(2,1)S(1)} %pad_maximum_fusion.3), channel_id=1, source_target_pairs={{0,3},{1,2},{2,1},{3,0},{4,7},{5,6},{6,5},{7,4},{8,11},{9,10},{10,... | collective-permute-start | bytes 1572872 | tf_op jit(solution)/shard_map/ppermute | solution.py:134
  53.4 6.1 %shard_map.67.refs_5_ = bf16[1024,1792]{1,0:T(8,128)(2,1)} custom-call(s32[268]{0:T(512)S(1)} %shard_map.64.table_ref, bf16[48,4096]{1,0:T(8,128)(2,1)S(1)} %collective-permute-done.2.refs_0_, bf16[96,4096]{1,0:T(8,128)(2,1)S(1)} %collective-permute-done.5.refs_1_, ...), custom_call_target="tpu_custom_call", output_to_operand_aliasing={{}: (6, {})} | custom-call | flops 7632000000 | bytes 745472 | tf_op jit(solution)/shard_map/pallas_call | solution.py:111
  59.5 5.7 %collective-permute-done.7.refs_0_ = bf16[48,4096]{1,0:T(8,128)(2,1)S(1)} collective-permute-done((bf16[48,4096]{1,0:T(8,128)(2,1)S(1)}, bf16[48,4096]{1,0:T(8,128)(2,1)S(1)}, u32[]{:S(2)}, u32[]{:S(2)}) %collective-permute-start.7) | collective-permute-done | bytes 393248 | tf_op jit(solution)/shard_map/ppermute | solution.py:134
  65.3 4.5 %collective-permute-done.8.refs_1_ = bf16[192,4096]{1,0:T(8,128)(2,1)S(1)} collective-permute-done((bf16[192,4096]{1,0:T(8,128)(2,1)S(1)}, bf16[192,4096]{1,0:T(8,128)(2,1)S(1)}, u32[]{:S(2)}, u32[]{:S(2)}) %collective-permute-start.8) | collective-permute-done | bytes 1572896 | tf_op jit(solution)/shard_map/ppermute | solution.py:134
  70.1 8.0 %shard_map.68.refs_4_ = bf16[1024,1792]{1,0:T(8,128)(2,1)} custom-call(s32[268]{0:T(512)S(1)} %shard_map.64.table_ref, bf16[48,4096]{1,0:T(8,128)(2,1)S(1)} %collective-permute-done.7.refs_0_, bf16[192,4096]{1,0:T(8,128)(2,1)S(1)} %collective-permute-done.8.refs_1_, ...), custom_call_target="tpu_custom_call", output_to_operand_aliasing={{}: (6, {})} | custom-call | flops 9936000000 | bytes 1089536 | tf_op jit(solution)/shard_map/pallas_call | solution.py:111
  78.8 4.2 %collective-permute-done.10.refs_0_ = bf16[96,4096]{1,0:T(8,128)(2,1)S(1)} collective-permute-done((bf16[96,4096]{1,0:T(8,128)(2,1)S(1)}, bf16[96,4096]{1,0:T(8,128)(2,1)S(1)}, u32[]{:S(2)}, u32[]{:S(2)}) %collective-permute-start.10) | collective-permute-done | bytes 786464 | tf_op jit(solution)/shard_map/ppermute | solution.py:134
  83.1 5.0 %shard_map.69 = bf16[1024,1792]{1,0:T(8,128)(2,1)} custom-call(s32[268]{0:T(512)S(1)} %shard_map.64.table_ref, bf16[96,4096]{1,0:T(8,128)(2,1)S(1)} %collective-permute-done.10.refs_0_, bf16[64,4096]{1,0:T(8,128)(2,1)S(1)} %collective-permute-done.11.refs_1_, bf16[14,9,128,128]{3,2,1,0:T(8,128)(2,1)S(1)} %copy-done.1, ...), custom_call_target="tpu_custom_call", output_to_operand_aliasing={{}: (5, {})} | custom-call | flops 6480000000 | bytes 573440 | tf_op jit(solution)/shard_map/pallas_call | solution.py:111
  (31 shorter events, 4.4 us)
Async XLA Ops:
  0.0 19.4 %collective-permute-start.1 = (bf16[64,4096]{1,0:T(8,128)(2,1)}, bf16[64,4096]{1,0:T(8,128)(2,1)S(1)}, u32[]{:S(2)}, u32[]{:S(2)}) collective-permute-start(bf16[64,4096]{1,0:T(8,128)(2,1)} %refs_0_.2), channel_id=1, source_target_pairs={{0,4},{1,5},{2,6},{3,7},{4,0},{5,1},{6,2},{7,3},{8,12},{9,13},{10,... | collective-permute-start | bytes 1572872 | tf_op jit(solution)/shard_map/ppermute | solution.py:134
  1.6 17.8 %copy-start.4 = (bf16[64,4096]{1,0:T(8,128)(2,1)S(1)}, bf16[64,4096]{1,0:T(8,128)(2,1)}, u32[]{:S(2)}) copy-start(bf16[64,4096]{1,0:T(8,128)(2,1)} %refs_0_.2) | copy-start | bytes 1572868
  2.7 23.7 %collective-permute-start = (bf16[48,4096]{1,0:T(8,128)(2,1)S(1)}, bf16[48,4096]{1,0:T(8,128)(2,1)S(1)}, u32[]{:S(2)}, u32[]{:S(2)}) collective-permute-start(bf16[48,4096]{1,0:T(8,128)(2,1)S(1)} %slice_bitcast_fusion), channel_id=1, source_target_pairs={{0,1},{1,0},{2,3},{3,2},{4,5},{5,4},{6,7},{7,6},{8,9},{9,8},{10,11... | collective-permute-start | bytes 1179656 | tf_op jit(solution)/shard_map/ppermute | solution.py:134
  6.1 24.3 %collective-permute-start.3 = (bf16[48,4096]{1,0:T(8,128)(2,1)S(1)}, bf16[48,4096]{1,0:T(8,128)(2,1)S(1)}, u32[]{:S(2)}, u32[]{:S(2)}) collective-permute-start(bf16[48,4096]{1,0:T(8,128)(2,1)S(1)} %slice_bitcast_fusion), channel_id=1, source_target_pairs={{0,3},{1,2},{2,1},{3,0},{4,7},{5,6},{6,5},{7,4},{8,11},{9,10},{10,... | collective-permute-start | bytes 1179656 | tf_op jit(solution)/shard_map/ppermute | solution.py:134
  10.6 10.6 %collective-permute-start.6 = (bf16[64,4096]{1,0:T(8,128)(2,1)}, bf16[64,4096]{1,0:T(8,128)(2,1)S(1)}, u32[]{:S(2)}, u32[]{:S(2)}) collective-permute-start(bf16[64,4096]{1,0:T(8,128)(2,1)} %refs_0_.2), channel_id=1, source_target_pairs={{0,12},{1,13},{2,14},{3,15},{4,8},{5,9},{6,10},{7,11},{8,4},{9,5},... | collective-permute-start | bytes 1572872 | tf_op jit(solution)/shard_map/ppermute | solution.py:134
  15.1 2.2 %copy-start = (bf16[14,9,128,128]{3,2,1,0:T(8,128)(2,1)S(1)}, bf16[14,9,128,128]{3,2,1,0:T(8,128)(2,1)}, u32[]{:S(2)}) copy-start(bf16[14,9,128,128]{3,2,1,0:T(8,128)(2,1)} %refs_2_.3) | copy-start | bytes 12386308
  17.2 2.2 %copy-start.2 = (bf16[14,9,128,128]{3,2,1,0:T(8,128)(2,1)S(1)}, bf16[14,9,128,128]{3,2,1,0:T(8,128)(2,1)}, u32[]{:S(2)}) copy-start(bf16[14,9,128,128]{3,2,1,0:T(8,128)(2,1)} %refs_3_.5) | copy-start | bytes 12386308
  19.4 2.2 %copy-start.1 = (bf16[14,9,128,128]{3,2,1,0:T(8,128)(2,1)S(1)}, bf16[14,9,128,128]{3,2,1,0:T(8,128)(2,1)}, u32[]{:S(2)}) copy-start(bf16[14,9,128,128]{3,2,1,0:T(8,128)(2,1)} %refs_2_.3) | copy-start | bytes 12386308
  19.4 3.4 %copy-start.3 = (bf16[14,9,128,128]{3,2,1,0:T(8,128)(2,1)S(1)}, bf16[14,9,128,128]{3,2,1,0:T(8,128)(2,1)}, u32[]{:S(2)}) copy-start(bf16[14,9,128,128]{3,2,1,0:T(8,128)(2,1)} %refs_3_.5) | copy-start | bytes 12386308
  19.5 10.9 %collective-permute-start.4 = (bf16[64,4096]{1,0:T(8,128)(2,1)S(1)}, bf16[64,4096]{1,0:T(8,128)(2,1)S(1)}, u32[]{:S(2)}, u32[]{:S(2)}) collective-permute-start(bf16[64,4096]{1,0:T(8,128)(2,1)S(1)} %collective-permute-done.1.refs_0_), channel_id=1, source_target_pairs={{0,12},{1,13},{2,14},{3,15},{4,8},{5,9},{6,10},{7,11},{8,4},{9,5},... | collective-permute-start | bytes 1572872 | tf_op jit(solution)/shard_map/ppermute | solution.py:134
  26.4 22.1 %collective-permute-start.2 = (bf16[48,4096]{1,0:T(8,128)(2,1)S(1)}, bf16[48,4096]{1,0:T(8,128)(2,1)S(1)}, u32[]{:S(2)}, u32[]{:S(2)}) collective-permute-start(bf16[48,4096]{1,0:T(8,128)(2,1)S(1)} %collective-permute-done.refs_3_), channel_id=1, source_target_pairs={{0,3},{1,2},{2,1},{3,0},{4,7},{5,6},{6,5},{7,4},{8,11},{9,10},{10,... | collective-permute-start | bytes 1179656 | tf_op jit(solution)/shard_map/ppermute | solution.py:134
  30.5 23.0 %collective-permute-start.9 = (bf16[64,4096]{1,0:T(8,128)(2,1)S(1)}, bf16[64,4096]{1,0:T(8,128)(2,1)S(1)}, u32[]{:S(2)}, u32[]{:S(2)}) collective-permute-start(bf16[64,4096]{1,0:T(8,128)(2,1)S(1)} %pad_maximum_fusion.3), channel_id=1, source_target_pairs={{0,1},{1,0},{2,3},{3,2},{4,5},{5,4},{6,7},{7,6},{8,9},{9,8},{10,11... | collective-permute-start | bytes 1572872 | tf_op jit(solution)/shard_map/ppermute | solution.py:134
  32.0 12.0 %collective-permute-start.5 = (bf16[96,4096]{1,0:T(8,128)(2,1)S(1)}, bf16[96,4096]{1,0:T(8,128)(2,1)S(1)}, u32[]{:S(2)}, u32[]{:S(2)}) collective-permute-start(bf16[96,4096]{1,0:T(8,128)(2,1)S(1)} %pad_maximum_fusion.1), channel_id=1, source_target_pairs={{0,4},{1,5},{2,6},{3,7},{4,0},{5,1},{6,2},{7,3},{8,12},{9,13},{10,... | collective-permute-start | bytes 2359304 | tf_op jit(solution)/shard_map/ppermute | solution.py:134
  44.1 25.8 %collective-permute-start.8 = (bf16[192,4096]{1,0:T(8,128)(2,1)S(1)}, bf16[192,4096]{1,0:T(8,128)(2,1)S(1)}, u32[]{:S(2)}, u32[]{:S(2)}) collective-permute-start(bf16[192,4096]{1,0:T(8,128)(2,1)S(1)} %pad_maximum_fusion), channel_id=1, source_target_pairs={{0,12},{1,13},{2,14},{3,15},{4,8},{5,9},{6,10},{7,11},{8,4},{9,5},... | collective-permute-start | bytes 4718600 | tf_op jit(solution)/shard_map/ppermute | solution.py:134
  48.5 21.7 %collective-permute-start.12 = (bf16[64,4096]{1,0:T(8,128)(2,1)S(1)}, bf16[64,4096]{1,0:T(8,128)(2,1)S(1)}, u32[]{:S(2)}, u32[]{:S(2)}) collective-permute-start(bf16[64,4096]{1,0:T(8,128)(2,1)S(1)} %pad_maximum_fusion.3), channel_id=1, source_target_pairs={{0,3},{1,2},{2,1},{3,0},{4,7},{5,6},{6,5},{7,4},{8,11},{9,10},{10,... | collective-permute-start | bytes 1572872 | tf_op jit(solution)/shard_map/ppermute | solution.py:134
  53.2 12.1 %collective-permute-start.7 = (bf16[48,4096]{1,0:T(8,128)(2,1)S(1)}, bf16[48,4096]{1,0:T(8,128)(2,1)S(1)}, u32[]{:S(2)}, u32[]{:S(2)}) collective-permute-start(bf16[48,4096]{1,0:T(8,128)(2,1)S(1)} %collective-permute-done.2.refs_0_), channel_id=1, source_target_pairs={{0,4},{1,5},{2,6},{3,7},{4,0},{5,1},{6,2},{7,3},{8,12},{9,13},{10,... | collective-permute-start | bytes 1179656 | tf_op jit(solution)/shard_map/ppermute | solution.py:134
  65.3 13.6 %collective-permute-start.11 = (bf16[64,4096]{1,0:T(8,128)(2,1)S(1)}, bf16[64,4096]{1,0:T(8,128)(2,1)S(1)}, u32[]{:S(2)}, u32[]{:S(2)}) collective-permute-start(bf16[64,4096]{1,0:T(8,128)(2,1)S(1)} %collective-permute-done.9.refs_2_), channel_id=1, source_target_pairs={{0,3},{1,2},{2,1},{3,0},{4,7},{5,6},{6,5},{7,4},{8,11},{9,10},{10,... | collective-permute-start | bytes 1572872 | tf_op jit(solution)/shard_map/ppermute | solution.py:134
  69.9 13.2 %collective-permute-start.10 = (bf16[96,4096]{1,0:T(8,128)(2,1)S(1)}, bf16[96,4096]{1,0:T(8,128)(2,1)S(1)}, u32[]{:S(2)}, u32[]{:S(2)}) collective-permute-start(bf16[96,4096]{1,0:T(8,128)(2,1)S(1)} %pad_maximum_fusion.2), channel_id=1, source_target_pairs={{0,12},{1,13},{2,14},{3,15},{4,8},{5,9},{6,10},{7,11},{8,4},{9,5},... | collective-permute-start | bytes 2359304 | tf_op jit(solution)/shard_map/ppermute | solution.py:134
